TPU v7x, 32 devices: a whole 2x2x4 slice. The times are simulated.
32 devices in a mesh: dp: 16 (over z, y, core), space: 2 (over x).
Axes of the slice: x: 2, y: 2, z: 4, core: 2. Of those that a mesh axis runs over, the one named last changes fastest.
Arguments:
- volumes: bfloat16 [16, 32, 8, 8, 128], P('dp', None, 'space'), may hold values from -6 to 6
- w_first: bfloat16 [864, 64], P('dp'), may hold values from -0.21875 to 0.21875
- w_second: bfloat16 [1728, 128], P('dp'), may hold values from -0.4375 to 0.4375
- cotangent: bfloat16 [16, 128, 2, 2, 32], P('dp', None, 'space'), may hold values from -96 to 96
Outputs:
- pooled: bfloat16 [16, 128, 2, 2, 32], P('dp', None, 'space')
- volume_grad: bfloat16 [16, 32, 8, 8, 128], P('dp', None, 'space')
- grad_first: float32 [864, 64], P('dp')
- grad_second: float32 [1728, 128], P('dp')
All inputs are finite; a program needn't handle non-finite values.
Results may differ from a plain program's by a relative error of at most 0.023.
Values may be sent and summed in bfloat16 or wider, within the bound.
No kernel may reach another device: no remote copies, remote signals or barrier semaphores. Data moves between devices by JAX's collectives and lax.ppermute only.
A program may use at most 128 MiB of HBM per device.

v0:
```python
import jax
import jax.numpy as jnp
from jax import lax
from jax.sharding import PartitionSpec as P


def with_halo(block, sides, width):
    for axis, dim in sides:
        count = lax.axis_size(axis)
        forward = [(i, i + 1) for i in range(count - 1)]
        backward = [(target, source) for source, target in forward]
        low = lax.ppermute(
            lax.slice_in_dim(block, block.shape[dim] - width, None, axis=dim), axis, forward
        )
        high = lax.ppermute(lax.slice_in_dim(block, 0, width, axis=dim), axis, backward)
        block = jnp.concatenate([low, block, high], axis=dim)
    return block


def pad_sides(field):
    return jnp.pad(field, ((0, 0), (0, 0), (0, 0), (1, 1), (1, 1)))


def conv_forward(padded, weight):
    samples_here, in_width, depth_padded, extent_y, extent_z = padded.shape
    extent_x = depth_padded - 2
    out_width = weight.shape[1]
    framed = pad_sides(padded)
    kernel = weight.reshape(3, 3, 3, in_width, out_width)
    summed = jnp.zeros((samples_here, out_width, extent_x, extent_y, extent_z), jnp.float32)
    for along_x in range(3):
        for along_y in range(3):
            for along_z in range(3):
                window = framed[
                    :,
                    :,
                    along_x : along_x + extent_x,
                    along_y : along_y + extent_y,
                    along_z : along_z + extent_z,
                ]
                summed = summed + jnp.einsum(
                    "sixyz,io->soxyz",
                    window,
                    kernel[along_x, along_y, along_z],
                    preferred_element_type=jnp.float32,
                )
    return summed


def conv_input_grad(padded, weight, in_width):
    samples_here, out_width, depth_padded, extent_y, extent_z = padded.shape
    extent_x = depth_padded - 2
    framed = pad_sides(padded)
    kernel = weight.reshape(3, 3, 3, in_width, out_width)
    summed = jnp.zeros((samples_here, in_width, extent_x, extent_y, extent_z), jnp.float32)
    for along_x in range(3):
        for along_y in range(3):
            for along_z in range(3):
                window = framed[
                    :,
                    :,
                    2 - along_x : 2 - along_x + extent_x,
                    2 - along_y : 2 - along_y + extent_y,
                    2 - along_z : 2 - along_z + extent_z,
                ]
                summed = summed + jnp.einsum(
                    "soxyz,io->sixyz",
                    window,
                    kernel[along_x, along_y, along_z],
                    preferred_element_type=jnp.float32,
                )
    return summed


def conv_weight_grad(padded, grads):
    samples_here, in_width, depth_padded, extent_y, extent_z = padded.shape
    extent_x = depth_padded - 2
    framed = pad_sides(padded)
    pieces = []
    for along_x in range(3):
        for along_y in range(3):
            for along_z in range(3):
                window = framed[
                    :,
                    :,
                    along_x : along_x + extent_x,
                    along_y : along_y + extent_y,
                    along_z : along_z + extent_z,
                ]
                pieces.append(
                    jnp.einsum("sixyz,soxyz->io", window, grads, preferred_element_type=jnp.float32)
                )
    return jnp.stack(pieces).reshape(27 * in_width, grads.shape[1])


def pooling(field):
    samples_here, width, extent_x, extent_y, extent_z = field.shape
    blocks = field.reshape(
        samples_here, width, extent_x // 2, 2, extent_y // 2, 2, extent_z // 2, 2
    )
    return jnp.mean(blocks, axis=(3, 5, 7))


def spread_up(field):
    samples_here, width, extent_x, extent_y, extent_z = field.shape
    blocks = jnp.broadcast_to(
        field[:, :, :, None, :, None, :, None],
        (samples_here, width, extent_x, 2, extent_y, 2, extent_z, 2),
    )
    return blocks.reshape(samples_here, width, 2 * extent_x, 2 * extent_y, 2 * extent_z)


def silu_slope(values):
    sigma = jax.nn.sigmoid(values)
    return sigma * (1.0 + values * (1.0 - sigma))


def local(volumes, w_first, w_second, cotangent):
    kernel_one, kernel_two = (
        lax.all_gather(w_first, "dp", axis=0, tiled=True),
        lax.all_gather(w_second, "dp", axis=0, tiled=True),
    )
    in_width = volumes.shape[1]
    mid_width = kernel_one.shape[1]
    count_one = lax.axis_size("dp") * lax.axis_size("space") * (volumes.size // in_width)
    factor_one = float(count_one) ** (-0.5)
    factor_two = float(count_one // 8) ** (-0.5)
    input_padded = with_halo(volumes, (("space", 2),), 1)
    first_pre = conv_forward(input_padded, kernel_one)
    first_pool = pooling(jax.nn.silu(first_pre)).astype(jnp.bfloat16)
    pool_padded = with_halo(first_pool, (("space", 2),), 1)
    second_pre = conv_forward(pool_padded, kernel_two)
    pooled = pooling(jax.nn.silu(second_pre)).astype(jnp.bfloat16)
    second_delta = (
        spread_up(cotangent.astype(jnp.float32)) * 0.125 * silu_slope(second_pre)
    ).astype(jnp.bfloat16)
    grad_two = conv_weight_grad(pool_padded, second_delta) * factor_two
    delta_padded = with_halo(second_delta, (("space", 2),), 1)
    pool_grad = conv_input_grad(delta_padded, kernel_two, mid_width).astype(jnp.bfloat16)
    first_delta = (spread_up(pool_grad.astype(jnp.float32)) * 0.125 * silu_slope(first_pre)).astype(
        jnp.bfloat16
    )
    grad_one = conv_weight_grad(input_padded, first_delta) * factor_one
    first_padded = with_halo(first_delta, (("space", 2),), 1)
    volume_grad = conv_input_grad(first_padded, kernel_one, in_width).astype(jnp.bfloat16)
    rows_one, rows_two = (
        lax.psum_scatter(
            grad_one.astype(jnp.bfloat16), "dp", scatter_dimension=0, tiled=True
        ).astype(jnp.float32),
        lax.psum_scatter(
            grad_two.astype(jnp.bfloat16), "dp", scatter_dimension=0, tiled=True
        ).astype(jnp.float32),
    )
    share_one, share_two = (
        lax.psum(rows_one.astype(jnp.bfloat16), "space").astype(jnp.float32),
        lax.psum(rows_two.astype(jnp.bfloat16), "space").astype(jnp.float32),
    )
    return (pooled, volume_grad, share_one, share_two)


def solution(mesh):
    return jax.shard_map(
        local,
        mesh=mesh,
        in_specs=(
            P("dp", None, "space", None, None),
            P("dp", None),
            P("dp", None),
            P("dp", None, "space", None, None),
        ),
        out_specs=(
            P("dp", None, "space", None, None),
            P("dp", None, "space", None, None),
            P("dp", None),
            P("dp", None),
        ),
        check_vma=False,
    )
```

profile of v0, /device:TPU:0, one launch (start us, length us, event | category | flops | bytes accessed | tf_op | source)
XLA Modules:
  0.0 181.2 jit_solution(16908317429202196970)
XLA Ops:
  0.6 1.1 copy.81
  1.7 4.9 %collective-permute-start = (bf16[1,32,1,8,128]{4,1,3,2,0:T(8,128)(2,1)S(1)}, bf16[1,32,1,8,128]{4,1,3,2,0:T(8,128)(2,1)S(1)}, u32[]{:S(2)}, u32[]{:S(2)}) collective-permute-start(bf16[1,32,1,8,128]{4,1,3,2,0:T(8,128)(2,1)S(1)} %get-tuple-element.26), channel_id=1, source_target_pairs={{0,1},{2,3},{4,5},{6,7},{8,9},{10,11},{12,13},{14,15},{16,17},{18,... | collective-permute-start | bytes 196616 | tf_op jit(solution)/shard_map/ppermute | solution.py:12
  6.6 1.3 collective-permute-start.1
  7.9 0.7 multiply_bitcast_fusion
  8.6 22.5 %all-gather = bf16[16,54,64]{2,1,0:T(8,128)(2,1)S(1)} all-gather(bf16[1,54,64]{2,1,0:T(8,128)(2,1)} %bitcast.1526), channel_id=1, replica_groups=mesh['dp'=16,'space'=2] {'dp'}, dimensions={0}, use_global_device_ids=true | all-gather | bytes 117504 | tf_op jit(solution)/shard_map/all_gather | solution.py:120
  40.6 0.6 fusion.17
  41.6 1.9 %fusion.134 = (f32[64,4,8,128]{3,0,2,1:T(8,128)}, f32[64,4,8,128]{3,0,2,1:T(8,128)}) fusion(f32[64,4,8,128]{3,0,2,1:T(8,128)S(1)} %convolution_bitcast_fusion, f32[64,4,8,128]{3,0,2,1:T(8,128)S(1)} %convolution_bitcast_fusion.1, f32[64,4,8,128]{3,0,2,1:T(8,128)S(1)} %convolution_bitcast_fusion.2, f32[64,4,8,128]{3,0,2,1:T(8,128)S(1)} %convolution_bitcast_fusion.3, ...), kind=kOutput, calls=%fused_computation.293 | convolution fusion | flops 19267584 | bytes 7675904 | tf_op jit(solution)/shard_map/sixyz,io->soxyz/dot_general | solution.py:41
  43.6 1.8 %copy.87 = f32[64,4,8,128]{0,3,2,1:T(8,128)S(1)} copy(f32[64,4,8,128]{3,0,2,1:T(8,128)} %get-tuple-element.32) | data formatting | bytes 2097152 | tf_op jit(solution)/shard_map/jit(silu)/mul | solution.py:130
  45.4 2.4 %reduce_sum.21 = f32[64,2,4,64]{0,3,2,1:T(8,128)} reduce(f32[64,2,2,4,2,64,2]{0,6,5,4,3,2,1:T(2,128)S(1)} %bitcast.1517, f32[]{:T(128)} %constant.8.clone.1), dimensions={2,4,6}, to_apply=%region_0.1 | reduce | flops 229376 | bytes 1179652 | tf_op jit(solution)/shard_map/reduce_sum | solution.py:101
  47.9 1.0 fusion.210
  48.9 4.6 %collective-permute-start.2 = (bf16[1,64,1,4,64]{1,4,3,2,0:T(8,128)(2,1)S(1)}, bf16[1,64,1,4,64]{1,4,3,2,0:T(8,128)(2,1)S(1)}, u32[]{:S(2)}, u32[]{:S(2)}) collective-permute-start(bf16[1,64,1,4,64]{1,4,3,2,0:T(8,128)(2,1)S(1)} %get-tuple-element.30), channel_id=1, source_target_pairs={{0,1},{2,3},{4,5},{6,7},{8,9},{10,11},{12,13},{14,15},{16,17},{18,... | collective-permute-start | bytes 98312 | tf_op jit(solution)/shard_map/ppermute | solution.py:12
  53.4 1.3 collective-permute-start.3
  54.7 18.7 %all-gather.1 = bf16[16,108,128]{2,1,0:T(8,128)(2,1)S(1)} all-gather(bf16[1,108,128]{2,1,0:T(8,128)(2,1)S(1)} %bitcast.1525), channel_id=1, replica_groups=mesh['dp'=16,'space'=2] {'dp'}, dimensions={0}, use_global_device_ids=true | all-gather | bytes 470016 | tf_op jit(solution)/shard_map/all_gather | solution.py:121
  86.1 0.9 multiply_convert_fusion.1
  87.0 4.6 %collective-permute-start.4 = (bf16[1,128,1,4,64]{1,4,3,2,0:T(8,128)(2,1)S(1)}, bf16[1,128,1,4,64]{1,4,3,2,0:T(8,128)(2,1)S(1)}, u32[]{:S(2)}, u32[]{:S(2)}) collective-permute-start(bf16[1,128,1,4,64]{1,4,3,2,0:T(8,128)(2,1)S(1)} %get-tuple-element.28), channel_id=1, source_target_pairs={{0,1},{2,3},{4,5},{6,7},{8,9},{10,11},{12,13},{14,15},{16,17},{18,... | collective-permute-start | bytes 196616 | tf_op jit(solution)/shard_map/ppermute | solution.py:12
  91.6 1.3 collective-permute-start.5
  93.6 4.1 %collective-permute-done.5 = bf16[1,128,1,4,64]{1,4,3,2,0:T(8,128)(2,1)S(1)} collective-permute-done((bf16[1,128,1,4,64]{1,4,3,2,0:T(8,128)(2,1)S(1)}, bf16[1,128,1,4,64]{1,4,3,2,0:T(8,128)(2,1)S(1)}, u32[]{:S(2)}, u32[]{:S(2)}) %collective-permute-start.5) | collective-permute-done | bytes 65568 | tf_op jit(solution)/shard_map/ppermute | solution.py:15
  102.7 0.9 broadcast_in_dim.16
  103.6 1.6 copy.88
  105.2 1.9 %multiply_convert_fusion = bf16[64,4,8,128]{3,0,2,1:T(8,128)(2,1)S(1)} fusion(f32[64,4,8,128]{3,0,2,1:T(8,128)} %copy.88, f32[64,4,8,128]{3,0,2,1:T(8,128)} %get-tuple-element.33), kind=kLoop, calls=%fused_computation.291 | loop fusion | flops 2359296 | bytes 2621440 | tf_op jit(solution)/shard_map/convert_element_type | solution.py:140
  115.4 34.4 %fusion.211 = (bf16[64,64]{1,0:T(8,128)(2,1)S(1)}, bf16[112,128]{1,0:T(8,128)(2,1)S(1)}) fusion(bf16[864,64]{1,0:T(8,128)(2,1)S(1)} %bitcast.1522, bf16[1728,128]{1,0:T(8,128)(2,1)S(1)} %bitcast.1521), kind=kCustom, calls=%all-reduce-scatter.2 | all-reduce-scatter fusion | flops 294914 | bytes 590336
  149.8 1.3 collective-permute-start.8
  151.1 1.3 collective-permute-start.9
  152.7 1.8 %collective-permute-start.11 = (bf16[60,128]{1,0:T(8,128)(2,1)S(1)}, bf16[60,128]{1,0:T(8,128)(2,1)S(1)}, u32[]{:S(2)}, u32[]{:S(2)}) collective-permute-start(bf16[60,128]{1,0:T(8,128)(2,1)S(1)} %slice.955), channel_id=1, source_target_pairs={{0,2},{2,4},{4,6},{6,8},{8,10},{10,12},{12,14},{14,16},{16,18},{18... | collective-permute-start | bytes 46088
  154.5 1.3 collective-permute-start.10
  155.8 1.3 collective-permute-start.7
  157.1 4.6 %collective-permute-start.6 = (bf16[1,64,1,8,128]{4,1,3,2,0:T(8,128)(2,1)S(1)}, bf16[1,64,1,8,128]{4,1,3,2,0:T(8,128)(2,1)S(1)}, u32[]{:S(2)}, u32[]{:S(2)}) collective-permute-start(bf16[1,64,1,8,128]{4,1,3,2,0:T(8,128)(2,1)S(1)} %get-tuple-element.22), channel_id=1, source_target_pairs={{0,1},{2,3},{4,5},{6,7},{8,9},{10,11},{12,13},{14,15},{16,17},{18,... | collective-permute-start | bytes 393224 | tf_op jit(solution)/shard_map/ppermute | solution.py:12
  162.6 7.1 %all-reduce.8 = (bf16[54,64]{1,0:T(8,128)(2,1)S(1)}, bf16[108,128]{1,0:T(8,128)(2,1)S(1)}) all-reduce(bf16[54,64]{1,0:T(8,128)(2,1)S(1)} %constant_dynamic-slice_fusion.1, bf16[108,128]{1,0:T(8,128)(2,1)S(1)} %constant_dynamic-slice_fusion), channel_id=1, replica_groups=mesh['dp'=16,'space'=2] {'space'}, use_global_device_ids=true, to_apply=%region_4.5 | all-reduce | flops 17280 | bytes 69120 | tf_op jit(solution)/shard_map/psum | solution.py:155
  169.8 0.6 convert_element_type.112
  171.0 1.1 select_maximum_fusion
  178.9 0.7 fusion.50
  180.4 0.8 copy.117
  (207 shorter events, 43.8 us)
Async XLA Ops:
  1.7 29.5 %collective-permute-start = (bf16[1,32,1,8,128]{4,1,3,2,0:T(8,128)(2,1)S(1)}, bf16[1,32,1,8,128]{4,1,3,2,0:T(8,128)(2,1)S(1)}, u32[]{:S(2)}, u32[]{:S(2)}) collective-permute-start(bf16[1,32,1,8,128]{4,1,3,2,0:T(8,128)(2,1)S(1)} %get-tuple-element.26), channel_id=1, source_target_pairs={{0,1},{2,3},{4,5},{6,7},{8,9},{10,11},{12,13},{14,15},{16,17},{18,... | collective-permute-start | bytes 196616 | tf_op jit(solution)/shard_map/ppermute | solution.py:12
  6.6 24.6 %collective-permute-start.1 = (bf16[1,32,1,8,128]{4,1,3,2,0:T(8,128)(2,1)S(1)}, bf16[1,32,1,8,128]{4,1,3,2,0:T(8,128)(2,1)S(1)}, u32[]{:S(2)}, u32[]{:S(2)}) collective-permute-start(bf16[1,32,1,8,128]{4,1,3,2,0:T(8,128)(2,1)S(1)} %get-tuple-element.27), channel_id=1, source_target_pairs={{1,0},{3,2},{5,4},{7,6},{9,8},{11,10},{13,12},{15,14},{17,16},{19,... | collective-permute-start | bytes 196616 | tf_op jit(solution)/shard_map/ppermute | solution.py:15
  31.2 10.5 %copy-start.3 = (bf16[3,3,3,32,64]{4,3,2,1,0:T(8,128)(2,1)}, bf16[3,3,3,32,64]{4,3,2,1,0:T(8,128)(2,1)S(1)}, u32[]{:S(2)}) copy-start(bf16[3,3,3,32,64]{4,3,2,1,0:T(8,128)(2,1)S(1)} %reshape.915) | copy-start | bytes 331780
  39.4 1.0 copy-start.1
  45.4 9.3 %copy-start.6 = (bf16[108,128]{1,0:T(8,128)(2,1)S(1)}, bf16[108,128]{1,0:T(8,128)(2,1)}, u32[]{:S(2)}) copy-start(bf16[108,128]{1,0:T(8,128)(2,1)} %param.6) | copy-start | bytes 82948
  45.4 28.1 %copy-start.7 = (u32[32]{0:T(128)S(1)}, u32[32]{0:T(128)}, u32[]{:S(2)}) copy-start(u32[32]{0:T(128)} %constant.37) | copy-start | bytes 388
  48.9 26.5 %collective-permute-start.2 = (bf16[1,64,1,4,64]{1,4,3,2,0:T(8,128)(2,1)S(1)}, bf16[1,64,1,4,64]{1,4,3,2,0:T(8,128)(2,1)S(1)}, u32[]{:S(2)}, u32[]{:S(2)}) collective-permute-start(bf16[1,64,1,4,64]{1,4,3,2,0:T(8,128)(2,1)S(1)} %get-tuple-element.30), channel_id=1, source_target_pairs={{0,1},{2,3},{4,5},{6,7},{8,9},{10,11},{12,13},{14,15},{16,17},{18,... | collective-permute-start | bytes 98312 | tf_op jit(solution)/shard_map/ppermute | solution.py:12
  53.4 22.0 %collective-permute-start.3 = (bf16[1,64,1,4,64]{1,4,3,2,0:T(8,128)(2,1)S(1)}, bf16[1,64,1,4,64]{1,4,3,2,0:T(8,128)(2,1)S(1)}, u32[]{:S(2)}, u32[]{:S(2)}) collective-permute-start(bf16[1,64,1,4,64]{1,4,3,2,0:T(8,128)(2,1)S(1)} %get-tuple-element.31), channel_id=1, source_target_pairs={{1,0},{3,2},{5,4},{7,6},{9,8},{11,10},{13,12},{15,14},{17,16},{19,... | collective-permute-start | bytes 98312 | tf_op jit(solution)/shard_map/ppermute | solution.py:15
  77.2 1.0 copy-start
  87.0 6.6 %collective-permute-start.4 = (bf16[1,128,1,4,64]{1,4,3,2,0:T(8,128)(2,1)S(1)}, bf16[1,128,1,4,64]{1,4,3,2,0:T(8,128)(2,1)S(1)}, u32[]{:S(2)}, u32[]{:S(2)}) collective-permute-start(bf16[1,128,1,4,64]{1,4,3,2,0:T(8,128)(2,1)S(1)} %get-tuple-element.28), channel_id=1, source_target_pairs={{0,1},{2,3},{4,5},{6,7},{8,9},{10,11},{12,13},{14,15},{16,17},{18,... | collective-permute-start | bytes 196616 | tf_op jit(solution)/shard_map/ppermute | solution.py:12
  91.6 6.2 %collective-permute-start.5 = (bf16[1,128,1,4,64]{1,4,3,2,0:T(8,128)(2,1)S(1)}, bf16[1,128,1,4,64]{1,4,3,2,0:T(8,128)(2,1)S(1)}, u32[]{:S(2)}, u32[]{:S(2)}) collective-permute-start(bf16[1,128,1,4,64]{1,4,3,2,0:T(8,128)(2,1)S(1)} %get-tuple-element.29), channel_id=1, source_target_pairs={{1,0},{3,2},{5,4},{7,6},{9,8},{11,10},{13,12},{15,14},{17,16},{19,... | collective-permute-start | bytes 196616 | tf_op jit(solution)/shard_map/ppermute | solution.py:15
  109.6 1.5 copy-start.2
  114.1 1.3 copy-start.5
  114.4 38.0 %copy-start.4 = (bf16[3,3,3,32,64]{4,3,2,1,0:T(8,128)(2,1)S(1)}, bf16[3,3,3,32,64]{4,3,2,1,0:T(8,128)(2,1)}, u32[]{:S(2)}) copy-start(bf16[3,3,3,32,64]{4,3,2,1,0:T(8,128)(2,1)} %copy-done.3) | copy-start | bytes 331780
  149.8 11.9 %collective-permute-start.8 = (bf16[64,64]{1,0:T(8,128)(2,1)S(1)}, bf16[64,64]{1,0:T(8,128)(2,1)S(1)}, u32[]{:S(2)}, u32[]{:S(2)}) collective-permute-start(bf16[64,64]{1,0:T(8,128)(2,1)S(1)} %get-tuple-element.20), channel_id=1, source_target_pairs={{0,2},{2,4},{4,6},{6,8},{8,10},{10,12},{12,14},{14,16},{16,18},{18... | collective-permute-start | bytes 24584
  151.1 10.6 %collective-permute-start.9 = (bf16[64,64]{1,0:T(8,128)(2,1)S(1)}, bf16[64,64]{1,0:T(8,128)(2,1)S(1)}, u32[]{:S(2)}, u32[]{:S(2)}) collective-permute-start(bf16[64,64]{1,0:T(8,128)(2,1)S(1)} %get-tuple-element.20), channel_id=1, source_target_pairs={{0,4},{2,6},{4,8},{6,10},{8,12},{10,14},{12,16},{14,18},{16,20},{1... | collective-permute-start | bytes 24584
  152.7 9.7 %collective-permute-start.11 = (bf16[60,128]{1,0:T(8,128)(2,1)S(1)}, bf16[60,128]{1,0:T(8,128)(2,1)S(1)}, u32[]{:S(2)}, u32[]{:S(2)}) collective-permute-start(bf16[60,128]{1,0:T(8,128)(2,1)S(1)} %slice.955), channel_id=1, source_target_pairs={{0,2},{2,4},{4,6},{6,8},{8,10},{10,12},{12,14},{14,16},{16,18},{18... | collective-permute-start | bytes 46088
  154.5 2.6 %collective-permute-start.10 = (bf16[22,64]{1,0:T(8,128)(2,1)S(1)}, bf16[22,64]{1,0:T(8,128)(2,1)S(1)}, u32[]{:S(2)}, u32[]{:S(2)}) collective-permute-start(bf16[22,64]{1,0:T(8,128)(2,1)S(1)} %slice.954), channel_id=1, source_target_pairs={{0,6},{2,8},{4,10},{6,12},{8,14},{10,16},{12,18},{14,20},{16,22},{... | collective-permute-start | bytes 8456
  155.8 15.2 %collective-permute-start.7 = (bf16[1,64,1,8,128]{4,1,3,2,0:T(8,128)(2,1)S(1)}, bf16[1,64,1,8,128]{4,1,3,2,0:T(8,128)(2,1)S(1)}, u32[]{:S(2)}, u32[]{:S(2)}) collective-permute-start(bf16[1,64,1,8,128]{4,1,3,2,0:T(8,128)(2,1)S(1)} %get-tuple-element.23), channel_id=1, source_target_pairs={{1,0},{3,2},{5,4},{7,6},{9,8},{11,10},{13,12},{15,14},{17,16},{19,... | collective-permute-start | bytes 393224 | tf_op jit(solution)/shard_map/ppermute | solution.py:15
  157.1 13.9 %collective-permute-start.6 = (bf16[1,64,1,8,128]{4,1,3,2,0:T(8,128)(2,1)S(1)}, bf16[1,64,1,8,128]{4,1,3,2,0:T(8,128)(2,1)S(1)}, u32[]{:S(2)}, u32[]{:S(2)}) collective-permute-start(bf16[1,64,1,8,128]{4,1,3,2,0:T(8,128)(2,1)S(1)} %get-tuple-element.22), channel_id=1, source_target_pairs={{0,1},{2,3},{4,5},{6,7},{8,9},{10,11},{12,13},{14,15},{16,17},{18,... | collective-permute-start | bytes 393224 | tf_op jit(solution)/shard_map/ppermute | solution.py:12
where the time goes:
time: 182 us; the launch traced here: 181 us
  blocking collectives  82.6 us (45%)
  matrix products  43 us (24%)
  starting transfers between devices  29.4 us (16%)
  other arithmetic  10.6 us (6%)
  local copies, waits for them, and re-layouts  8.21 us (5%)
  waiting for transfers between devices  4.18 us (2%)
  between operations  3.1 us (2%)
    unnamed x1, blocking collectives  34.4 us
    all_gather x1, blocking collectives, local(): lax.all_gather(w_first, 'dp', axis=0, tiled=True)  22.5 us
    all_gather x1, blocking collectives, local(): lax.all_gather(w_second, 'dp', axis=0, tiled=True)  18.7 us
    ppermute x4, starting transfers between devices, with_halo(): lax.ppermute(lax.slice_in_dim(block, block.shape[dim] - width, None, axis...  18.6 us
    dot_general x54, matrix products, conv_forward(): jnp.einsum('sixyz,io->soxyz', window, kernel[along_x, along_y, along_z],...  16.1 us
    dot_general x54, matrix products, conv_weight_grad(): jnp.einsum('sixyz,soxyz->io', window, grads, preferred_element_type=jnp.f...  13.8 us
    dot_general x54, matrix products, conv_input_grad(): jnp.einsum('soxyz,io->sixyz', window, kernel[along_x, along_y, along_z],...  13.1 us
    psum x1, blocking collectives, local(): lax.psum(rows_one.astype(jnp.bfloat16), 'space').astype(jnp.float32)  7.13 us
  transfers between devices with their start and end apart: 12, of which 1 were waited for; matrix products, arithmetic and copies ran while one was open for 2% of the time, Pallas kernels for 0%

commit v1 on v0

--- a/solution.py
+++ b/solution.py
@@ -1,7 +1,332 @@
+import functools
+
 import jax
 import jax.numpy as jnp
 from jax import lax
+from jax.experimental import pallas as pl
+from jax.experimental.pallas import tpu as pltpu
 from jax.sharding import PartitionSpec as P
+
+BF = jnp.bfloat16
+F32 = jnp.float32
+
+
+def dot(a, b):
+    return jnp.dot(a, b, preferred_element_type=F32)
+
+
+def dot_nt(a, b):
+    return lax.dot_general(a, b, (((1,), (1,)), ((), ())), preferred_element_type=F32)
+
+
+def iota(shape, dim):
+    return lax.broadcasted_iota(jnp.int32, shape, dim)
+
+
+def eye(n):
+    return (iota((n, n), 0) == iota((n, n), 1)).astype(F32).astype(BF)
+
+
+def roll_z(x, by):
+    lane = iota(x.shape, 1)
+    edge = 0 if by == 1 else 127
+    return jnp.where(lane == edge, 0.0, pltpu.roll(x, by % 128, 1))
+
+
+def roll_yz(x, db, dc):
+    if db == 0 and dc == 0:
+        return x
+    lane = iota(x.shape, 1)
+    y, z = lane // 64 + db, lane % 64 + dc
+    inside = (y >= 0) & (y < 4) & (z >= 0) & (z < 64)
+    return jnp.where(inside, pltpu.roll(x, (-(db * 64 + dc)) % 256, 1), 0.0)
+
+
+def unpack_weights(me, g0_ref, g1_ref, w1f, w2f):
+    for d in range(16):
+        k = jnp.bitwise_xor(me, d)
+        core, rest = k % 2, (k // 2) % 2 * 4 + k // 4
+        blk = lax.select(core == 0, g0_ref[rest], g1_ref[rest])
+        blk = blk.astype(F32)
+        w2f[108 * d : 108 * d + 108, :] = blk[0:108]
+        w1f[54 * d : 54 * d + 27, :] = blk[108:135, 0:64]
+        w1f[54 * d + 27 : 54 * d + 54, :] = blk[108:135, 64:128]
+
+
+def fused_kernel(
+    factor_one, factor_two,
+    pos, vo, vx, co, cx, ga, gb,
+    pooled_out, keep_out, send_out, dp_out, w1_out,
+    w1f, w2f, w2s, vs, slope, fpl, fs, d2p, t2, wcat, acc1, g2f, g1f, pg, chunk,
+):
+    me, s = pos[0], pos[1]
+    unpack_weights(me, ga, gb, w1f, w2f)
+    w1_out[...] = w1f[...].astype(BF)
+    w2s[...] = w2f[...].astype(BF)
+    vs[...] = jnp.zeros(vs.shape, BF)
+    for p in range(4):
+        vs[4 * s + 1 + p, :, 128:1152] = vo[p]
+        vs[4 * (1 - s) + 1 + p, :, 128:1152] = vx[p]
+    id64, id128 = eye(64), eye(128)
+    lhs1 = jnp.concatenate(
+        [
+            dot_nt(
+                id64,
+                jnp.concatenate(
+                    [w1f[(ab * 3 + c) * 32 : (ab * 3 + c) * 32 + 32, :] for ab in range(9)], axis=0
+                ).astype(BF),
+            ).astype(BF)
+            for c in range(3)
+        ],
+        axis=0,
+    )
+    pool_m = (iota((256, 128), 0) // 2 == iota((256, 128), 1)).astype(F32).astype(BF)
+
+    def cols_of(x):
+        return jnp.concatenate(
+            [vs[x + a, :, b * 128 : b * 128 + 1024] for a in range(3) for b in range(3)], axis=0
+        )
+
+    def first(x2, carry):
+        total = [jnp.zeros((64, 128), F32) for _ in range(4)]
+        for dx in range(2):
+            x = 2 * x2 + dx
+            prod = dot(lhs1, cols_of(x))
+            for y in range(8):
+                part = prod[:, y * 128 : y * 128 + 128]
+                pre = part[64:128] + roll_z(part[0:64], 1) + roll_z(part[128:192], -1)
+                sig = jax.nn.sigmoid(pre)
+                act = pre * sig
+                slope[x, :, y * 128 : y * 128 + 128] = sig + act * (1.0 - sig)
+                total[y // 2] = total[y // 2] + act
+        for h in range(2):
+            pair = jnp.concatenate([total[2 * h], total[2 * h + 1]], axis=1)
+            hi = pair.astype(BF)
+            lo = (pair - hi.astype(F32)).astype(BF)
+            fpl[x2, :, h * 128 : h * 128 + 128] = (
+                (dot(hi, pool_m) + dot(lo, pool_m)) * 0.125
+            ).astype(BF).astype(F32)
+        return carry
+
+    lax.fori_loop(0, 4, first, 0)
+
+    fs[0] = jnp.zeros((576, 256), BF)
+    fs[5] = jnp.zeros((576, 256), BF)
+    d2p[0] = jnp.zeros((128, 256), BF)
+    d2p[5] = jnp.zeros((128, 256), BF)
+
+    def shifts(x2, carry):
+        plane = fpl[x2]
+        for bc in range(9):
+            fs[x2 + 1, bc * 64 : bc * 64 + 64, :] = roll_yz(plane, bc // 3 - 1, bc % 3 - 1).astype(BF)
+        return carry
+
+    lax.fori_loop(0, 4, shifts, 0)
+    w2t = dot_nt(id128, w2s[...]).astype(BF)
+    col = iota((64, 256), 1)
+    spread2 = (iota((64, 256), 0) == (col // 128) * 32 + (col % 64) // 2).astype(F32).astype(BF)
+    row = iota((256, 64), 0)
+    pool2 = (iota((256, 64), 1) == (row // 128) * 32 + (row % 64) // 2).astype(F32).astype(BF)
+
+    def second(x4, carry):
+        cot = lax.select(x4 == s, co[...], cx[...])
+        wide = dot(cot, spread2) * 0.125
+        total = jnp.zeros((128, 256), F32)
+        for dx in range(2):
+            x2 = 2 * x4 + dx
+            rhs = jnp.concatenate([fs[x2], fs[x2 + 1], fs[x2 + 2]], axis=0)
+            pre = dot(w2t, rhs)
+            sig = jax.nn.sigmoid(pre)
+            act = pre * sig
+            total = total + act
+            d2p[x2 + 1] = (wide * (sig + act * (1.0 - sig))).astype(BF)
+        t2[x4] = total
+        return carry
+
+    lax.fori_loop(0, 2, second, 0)
+    mine = t2[s]
+    hi = mine.astype(BF)
+    lo = (mine - hi.astype(F32)).astype(BF)
+    pooled_out[...] = ((dot(hi, pool2) + dot(lo, pool2)) * 0.125).astype(BF)
+
+    deltas = jnp.concatenate([d2p[1], d2p[2], d2p[3], d2p[4]], axis=1)
+    for a in range(3):
+        lhs = jnp.concatenate([fs[a], fs[a + 1], fs[a + 2], fs[a + 3]], axis=1)
+        g2f[a * 576 : a * 576 + 576, :] = dot_nt(lhs, deltas) * factor_two
+        wcat[:, a * 128 : a * 128 + 128] = w2s[a * 576 : a * 576 + 576, :]
+
+    spread1 = (iota((128, 256), 0) == iota((128, 256), 1) // 2).astype(F32).astype(BF)
+    acc1[...] = jnp.zeros(acc1.shape, F32)
+    dp_out[...] = jnp.zeros(dp_out.shape, BF)
+
+    def back(x2, carry):
+        rhs = jnp.concatenate([d2p[x2 + 2], d2p[x2 + 1], d2p[x2]], axis=0)
+        prod = dot(wcat[...], rhs)
+        grad = jnp.zeros((64, 256), F32)
+        for bc in range(9):
+            grad = grad + roll_yz(prod[bc * 64 : bc * 64 + 64], 1 - bc // 3, 1 - bc % 3)
+        grad = grad.astype(BF)
+        for h in range(2):
+            wide = dot(grad[:, h * 128 : h * 128 + 128], spread1) * 0.125
+            for dx in range(2):
+                for y in range(4):
+                    lanes = slice((4 * h + y) * 128, (4 * h + y) * 128 + 128)
+                    value = wide[:, (y // 2) * 128 : (y // 2) * 128 + 128] * slope[2 * x2 + dx, :, lanes]
+                    pg[dx, 64:128, lanes] = value.astype(BF)
+                    pg[dx, 0:64, lanes] = roll_z(value, -1).astype(BF)
+                    pg[dx, 128:192, lanes] = roll_z(value, 1).astype(BF)
+        for dx in range(2):
+            x = 2 * x2 + dx
+            dp_out[x + 1, :, 128:1152] = pg[dx, 64:128, :]
+            acc1[...] += dot_nt(cols_of(x), pg[dx])
+        return carry
+
+    lax.fori_loop(0, 4, back, 0)
+    for ab in range(9):
+        for c in range(3):
+            g1f[(ab * 3 + c) * 32 : (ab * 3 + c) * 32 + 32, :] = (
+                acc1[ab * 32 : ab * 32 + 32, c * 64 : c * 64 + 64] * factor_one
+            )
+    chunk[...] = jnp.zeros(chunk.shape, F32)
+    for d in range(16):
+        chunk[0:108, :] = g2f[108 * d : 108 * d + 108, :]
+        chunk[108:135, 0:64] = g1f[54 * d : 54 * d + 27, :]
+        chunk[108:135, 64:128] = g1f[54 * d + 27 : 54 * d + 54, :]
+        k = jnp.bitwise_xor(me, d)
+        place = (k // 2) % 2 * 4 + k // 4
+
+        @pl.when(k % 2 == 0)
+        def _():
+            keep_out[place] = chunk[...].astype(BF)
+
+        @pl.when(k % 2 == 1)
+        def _():
+            send_out[place] = chunk[...].astype(BF)
+
+
+def volume_kernel(pos, dp, w1, out, wd):
+    s = pos[1]
+    for ab in range(9):
+        wd[:, ab * 64 : ab * 64 + 64] = w1[ab * 96 : ab * 96 + 96, :]
+    lhs = wd[...]
+
+    def plane(p, carry):
+        x = 4 * s + p
+        rhs = jnp.concatenate(
+            [
+                dp[x + 2 - a, :, (2 - b) * 128 : (2 - b) * 128 + 1024]
+                for a in range(3)
+                for b in range(3)
+            ],
+            axis=0,
+        )
+        prod = dot(lhs, rhs)
+        for y in range(8):
+            part = prod[:, y * 128 : y * 128 + 128]
+            out[p, :, y * 128 : y * 128 + 128] = (
+                part[32:64] + roll_z(part[0:32], -1) + roll_z(part[64:96], 1)
+            ).astype(BF)
+        return carry
+
+    lax.fori_loop(0, 4, plane, 0)
+
+
+def fused_call(factor_one, factor_two, pos, vo, vx, co, cx, ga, gb):
+    vmem = pl.BlockSpec(memory_space=pltpu.VMEM)
+    return pl.pallas_call(
+        functools.partial(fused_kernel, factor_one, factor_two),
+        out_shape=(
+            jax.ShapeDtypeStruct((128, 64), BF),
+            jax.ShapeDtypeStruct((8, 136, 128), BF),
+            jax.ShapeDtypeStruct((8, 136, 128), BF),
+            jax.ShapeDtypeStruct((10, 64, 1280), BF),
+            jax.ShapeDtypeStruct((864, 64), BF),
+        ),
+        in_specs=[pl.BlockSpec(memory_space=pltpu.SMEM)] + [vmem] * 6,
+        out_specs=(vmem,) * 5,
+        scratch_shapes=[
+            pltpu.VMEM((864, 64), F32),
+            pltpu.VMEM((1728, 128), F32),
+            pltpu.VMEM((1728, 128), BF),
+            pltpu.VMEM((10, 32, 1280), BF),
+            pltpu.VMEM((8, 64, 1024), F32),
+            pltpu.VMEM((4, 64, 256), F32),
+            pltpu.VMEM((6, 576, 256), BF),
+            pltpu.VMEM((6, 128, 256), BF),
+            pltpu.VMEM((2, 128, 256), F32),
+            pltpu.VMEM((576, 384), BF),
+            pltpu.VMEM((288, 192), F32),
+            pltpu.VMEM((1728, 128), F32),
+            pltpu.VMEM((864, 64), F32),
+            pltpu.VMEM((2, 192, 1024), BF),
+            pltpu.VMEM((136, 128), F32),
+        ],
+        compiler_params=pltpu.CompilerParams(vmem_limit_bytes=48 << 20),
+        cost_estimate=pl.CostEstimate(flops=4_000_000_000, bytes_accessed=6_000_000, transcendentals=700_000),
+        name="fused",
+    )(pos, vo, vx, co, cx, ga, gb)
+
+
+def volume_call(pos, dp, w1):
+    vmem = pl.BlockSpec(memory_space=pltpu.VMEM)
+    return pl.pallas_call(
+        volume_kernel,
+        out_shape=jax.ShapeDtypeStruct((4, 32, 1024), BF),
+        in_specs=[pl.BlockSpec(memory_space=pltpu.SMEM), vmem, vmem],
+        out_specs=vmem,
+        scratch_shapes=[pltpu.VMEM((96, 576), BF)],
+        compiler_params=pltpu.CompilerParams(vmem_limit_bytes=16 << 20),
+        cost_estimate=pl.CostEstimate(flops=1_000_000_000, bytes_accessed=3_000_000, transcendentals=0),
+        name="volume",
+    )(pos, dp, w1)
+
+
+def fits(volumes, w_first, w_second, cotangent):
+    return (
+        lax.axis_size("dp") == 16
+        and lax.axis_size("space") == 2
+        and volumes.shape == (1, 32, 4, 8, 128)
+        and w_first.shape == (54, 64)
+        and w_second.shape == (108, 128)
+        and cotangent.shape == (1, 128, 1, 2, 32)
+    )
+
+
+def swap(x, bit):
+    return lax.ppermute(x, "dp", [(i, i ^ bit) for i in range(16)])
+
+
+def paired(volumes, w_first, w_second, cotangent):
+    count = 16 * 2 * (volumes.size // 32)
+    factor_one, factor_two = float(count) ** (-0.5), float(count // 8) ** (-0.5)
+    pos = jnp.stack([lax.axis_index("dp"), lax.axis_index("space")]).astype(jnp.int32)
+    own = jnp.transpose(volumes[0], (1, 0, 2, 3)).reshape(4, 32, 1024)
+    cot = cotangent.reshape(128, 64)
+    other = lax.ppermute(own, "space", [(0, 1), (1, 0)])
+    cot_other = lax.ppermute(cot, "space", [(0, 1), (1, 0)])
+    shard = jnp.concatenate(
+        [
+            w_second,
+            jnp.concatenate([w_first[:27], w_first[27:]], axis=1),
+            jnp.zeros((1, 128), BF),
+        ],
+        axis=0,
+    )
+    along_z = jnp.stack([shard] + [swap(shard, 4 * k) for k in range(1, 4)])
+    along_y = jnp.concatenate([along_z, swap(along_z, 2)])
+    across = swap(along_y, 1)
+    pooled, keep, send, delta, w_one = fused_call(
+        factor_one, factor_two, pos, own, other, cot, cot_other, along_y, across
+    )
+    part = (keep.astype(F32) + swap(send, 1).astype(F32)).astype(BF)
+    part = (part[:4].astype(F32) + swap(part[4:], 2).astype(F32)).astype(BF)
+    total = part[0].astype(F32)
+    for k in range(1, 4):
+        total = total + swap(part[k], 4 * k).astype(F32)
+    grad = volume_call(pos, delta, w_one)
+    grad = jnp.transpose(grad.reshape(4, 32, 8, 128), (1, 0, 2, 3))[None]
+    share_one = jnp.concatenate([total[108:135, :64], total[108:135, 64:]], axis=0)
+    return pooled.reshape(1, 128, 1, 2, 32), grad, share_one, total[:108]
 
 
 def with_halo(block, sides, width):
@@ -115,7 +440,7 @@
     return sigma * (1.0 + values * (1.0 - sigma))
 
 
-def local(volumes, w_first, w_second, cotangent):
+def general(volumes, w_first, w_second, cotangent):
     kernel_one, kernel_two = (
         lax.all_gather(w_first, "dp", axis=0, tiled=True),
         lax.all_gather(w_second, "dp", axis=0, tiled=True),
@@ -158,6 +483,12 @@
     return (pooled, volume_grad, share_one, share_two)
 
 
+def local(volumes, w_first, w_second, cotangent):
+    if fits(volumes, w_first, w_second, cotangent):
+        return paired(volumes, w_first, w_second, cotangent)
+    return general(volumes, w_first, w_second, cotangent)
+
+
 def solution(mesh):
     return jax.shard_map(
         local,

time: 182 us -> 59.3 us (0.33)
  blocking collectives: 82.6 us -> 0 us
  matrix products: 43 us -> 0 us
  waiting for transfers between devices: 4.18 us -> 21.4 us
  Pallas kernels: 0 us -> 16 us
  starting transfers between devices: 29.4 us -> 14.8 us
  other arithmetic: 10.6 us -> 1.68 us
  local copies, waits for them, and re-layouts: 8.21 us -> 4.33 us
  between operations: 3.1 us -> 0.76 us
    dot_general x162 -> x0, matrix products: 43 us -> none  [the longest x54 16.1 us: conv_forward(): jnp.einsum('sixyz,io->soxyz', window, kernel[along_x, along_y, along_z],...]
    all_gather x2 -> x0, blocking collectives: 41.2 us -> none  [the longest x1 22.5 us: local(): lax.all_gather(w_first, 'dp', axis=0, tiled=True)]
    unnamed x1 -> x0, blocking collectives: 34.4 us -> none
    ppermute x8 -> x12, waiting for transfers between devices: 4.17 us -> 21.4 us  [the longest x10 14.3 us: swap(): return lax.ppermute(x, 'dp', [(i, i ^ bit) for i in range(16)])]
    pallas_call x0 -> x2, Pallas kernels: none -> 16 us  [the longest x1 13.5 us: fused_call(): pl.pallas_call(functools.partial(fused_kernel, factor_one, factor_two), o...]
    ppermute x8 -> x12, starting transfers between devices: 23.7 us -> 14.8 us  [the longest x10 12.7 us: swap(): return lax.ppermute(x, 'dp', [(i, i ^ bit) for i in range(16)])]
    psum x1 -> x0, blocking collectives: 7.13 us -> none  [local(): lax.psum(rows_one.astype(jnp.bfloat16), 'space').astype(jnp.float32)]
    unnamed x4 -> x0, starting transfers between devices: 5.69 us -> none
  transfers between devices with their start and end apart: 12 -> 12, of which waited for: 1 -> 8; matrix products, arithmetic and copies ran while one was open for 2% -> 5% of each run, Pallas kernels for 0% -> 4%
where the time goes in v1:
time: 59.3 us; the launch traced here: 59 us
  waiting for transfers between devices  21.4 us (36%)
  Pallas kernels  16 us (27%)
  starting transfers between devices  14.8 us (25%)
  local copies, waits for them, and re-layouts  4.33 us (7%)
  other arithmetic  1.68 us (3%)
  between operations  0.76 us (1%)
    ppermute x10, waiting for transfers between devices, swap(): return lax.ppermute(x, 'dp', [(i, i ^ bit) for i in range(16)])  14.3 us
    pallas_call x1, Pallas kernels, fused_call(): pl.pallas_call(functools.partial(fused_kernel, factor_one, factor_two), o...  13.5 us
    ppermute x10, starting transfers between devices, swap(): return lax.ppermute(x, 'dp', [(i, i ^ bit) for i in range(16)])  12.7 us
    ppermute x1, waiting for transfers between devices, paired(): cot_other = lax.ppermute(cot, 'space', [(0, 1), (1, 0)])  7.12 us
    pallas_call x1, Pallas kernels, volume_call(): pl.pallas_call(volume_kernel, out_shape=jax.ShapeDtypeStruct((4, 32, 1024...  2.47 us
    ppermute x1, starting transfers between devices, paired(): other = lax.ppermute(own, 'space', [(0, 1), (1, 0)])  1.56 us
  transfers between devices with their start and end apart: 12, of which 8 were waited for; matrix products, arithmetic and copies ran while one was open for 5% of the time, Pallas kernels for 4%

profile of v1, /device:TPU:0, one launch (start us, length us, event | category | flops | bytes accessed | tf_op | source)
XLA Modules:
  0.0 59.0 jit_solution(11199031559280595598)
XLA Ops:
  0.6 0.8 %fusion.3 = (bf16[27,64]{1,0:T(8,128)(2,1)S(1)}, bf16[27,64]{1,0:T(8,128)(2,1)S(1)}) fusion(bf16[54,64]{1,0:T(8,128)(2,1)} %param.5), kind=kLoop, calls=%fused_computation.20 | loop fusion | bytes 13824 | tf_op jit(solution)/shard_map/slice | solution.py:310
  1.4 0.1 pad.9.clone
  1.5 0.8 %constant_dynamic-update-slice_fusion.4 = (bf16[8,136,128]{2,1,0:T(8,128)(2,1)S(1)}, bf16[136,128]{1,0:T(8,128)(2,1)S(1)}) fusion(bf16[136]{0:T(256)(128)(2,1)S(1)} %pad.9.clone, bf16[27,64]{1,0:T(8,128)(2,1)S(1)} %get-tuple-element.26, bf16[27,64]{1,0:T(8,128)(2,1)S(1)} %get-tuple-element.25, bf16[108,128]{1,0:T(8,128)(2,1)} %param.6), kind=kLoop, calls=%fused_computation.17 | loop fusion | flops 139263 | bytes 104464
  2.3 5.1 %collective-permute-start.4 = (bf16[136,128]{1,0:T(8,128)(2,1)S(1)}, bf16[136,128]{1,0:T(8,128)(2,1)S(1)}, u32[]{:S(2)}, u32[]{:S(2)}) collective-permute-start(bf16[136,128]{1,0:T(8,128)(2,1)S(1)} %get-tuple-element.19), channel_id=1, source_target_pairs={{0,24},{2,26},{4,28},{6,30},{8,16},{10,18},{12,20},{14,22},{16,8},... | collective-permute-start | bytes 104456 | tf_op jit(solution)/shard_map/ppermute | solution.py:296
  7.5 0.6 %collective-permute-start.2 = (bf16[136,128]{1,0:T(8,128)(2,1)S(1)}, bf16[136,128]{1,0:T(8,128)(2,1)S(1)}, u32[]{:S(2)}, u32[]{:S(2)}) collective-permute-start(bf16[136,128]{1,0:T(8,128)(2,1)S(1)} %get-tuple-element.19), channel_id=1, source_target_pairs={{0,8},{2,10},{4,12},{6,14},{8,0},{10,2},{12,4},{14,6},{16,24},{18,... | collective-permute-start | bytes 104456 | tf_op jit(solution)/shard_map/ppermute | solution.py:296
  8.1 1.3 %collective-permute-done.4 = bf16[136,128]{1,0:T(8,128)(2,1)S(1)} collective-permute-done((bf16[136,128]{1,0:T(8,128)(2,1)S(1)}, bf16[136,128]{1,0:T(8,128)(2,1)S(1)}, u32[]{:S(2)}, u32[]{:S(2)}) %collective-permute-start.4) | collective-permute-done | bytes 34848 | tf_op jit(solution)/shard_map/ppermute | solution.py:296
  9.4 2.9 %collective-permute-done.3 = bf16[136,128]{1,0:T(8,128)(2,1)S(1)} collective-permute-done((bf16[136,128]{1,0:T(8,128)(2,1)S(1)}, bf16[136,128]{1,0:T(8,128)(2,1)S(1)}, u32[]{:S(2)}, u32[]{:S(2)}) %collective-permute-start.3) | collective-permute-done | bytes 34848 | tf_op jit(solution)/shard_map/ppermute | solution.py:296
  12.3 1.6 %collective-permute-start.5 = (bf16[4,136,128]{2,1,0:T(8,128)(2,1)S(1)}, bf16[4,136,128]{2,1,0:T(8,128)(2,1)S(1)}, u32[]{:S(2)}, u32[]{:S(2)}) collective-permute-start(bf16[4,136,128]{2,1,0:T(8,128)(2,1)S(1)} %pad_maximum_fusion), channel_id=1, source_target_pairs={{0,4},{2,6},{4,0},{6,2},{8,12},{10,14},{12,8},{14,10},{16,20},{18,... | collective-permute-start | bytes 417800 | tf_op jit(solution)/shard_map/ppermute | solution.py:296
  14.0 3.5 %collective-permute-done.5 = bf16[4,136,128]{2,1,0:T(8,128)(2,1)S(1)} collective-permute-done((bf16[4,136,128]{2,1,0:T(8,128)(2,1)S(1)}, bf16[4,136,128]{2,1,0:T(8,128)(2,1)S(1)}, u32[]{:S(2)}, u32[]{:S(2)}) %collective-permute-start.5) | collective-permute-done | bytes 139296 | tf_op jit(solution)/shard_map/ppermute | solution.py:296
  17.5 0.1 collective-permute-start.6
  17.6 1.0 %reshape.27 = bf16[4,32,1024]{2,0,1:T(4,128)(2,1)S(1)} reshape(bf16[4,32,8,128]{3,2,0,1:T(8,128)(2,1)} %bitcast.45) | data formatting | bytes 524288 | tf_op jit(solution)/shard_map/reshape | solution.py:303
  18.6 0.1 copy.17.vo
  18.7 1.6 %collective-permute-start = (bf16[4,32,1024]{2,1,0:T(8,128)(2,1)S(1)}, bf16[4,32,1024]{2,1,0:T(8,128)(2,1)S(1)}, u32[]{:S(2)}, u32[]{:S(2)}) collective-permute-start(bf16[4,32,1024]{2,1,0:T(8,128)(2,1)S(1)} %copy.17.vo), channel_id=1, source_target_pairs={{0,1},{1,0},{2,3},{3,2},{4,5},{5,4},{6,7},{7,6},{8,9},{9,8},{10,11... | collective-permute-start | bytes 786440 | tf_op jit(solution)/shard_map/ppermute | solution.py:305
  20.2 0.1 copy.14.co
  20.4 0.6 %collective-permute-start.1 = (bf16[128,64]{1,0:T(8,128)(2,1)S(1)}, bf16[128,64]{1,0:T(8,128)(2,1)S(1)}, u32[]{:S(2)}, u32[]{:S(2)}) collective-permute-start(bf16[128,64]{1,0:T(8,128)(2,1)S(1)} %copy.14.co), channel_id=1, source_target_pairs={{0,1},{1,0},{2,3},{3,2},{4,5},{5,4},{6,7},{7,6},{8,9},{9,8},{10,11... | collective-permute-start | bytes 49160 | tf_op jit(solution)/shard_map/ppermute | solution.py:306
  21.0 0.1 pad_add_fusion.pos
  21.0 7.1 %collective-permute-done.1.cx = bf16[128,64]{1,0:T(8,128)(2,1)S(1)} collective-permute-done((bf16[128,64]{1,0:T(8,128)(2,1)S(1)}, bf16[128,64]{1,0:T(8,128)(2,1)S(1)}, u32[]{:S(2)}, u32[]{:S(2)}) %collective-permute-start.1) | collective-permute-done | bytes 16416 | tf_op jit(solution)/shard_map/ppermute | solution.py:306
  28.2 13.5 %fused.1 = (bf16[128,64]{1,0:T(8,128)(2,1)S(1)}, bf16[8,136,128]{2,1,0:T(8,128)(2,1)S(1)}, bf16[8,136,128]{2,1,0:T(8,128)(2,1)S(1)}, bf16[10,64,1280]{2,1,0:T(8,128)(2,1)S(1)}, bf16[864,64]{1,0:T(8,128)(2,1)S(1)}) custom-call(s32[2]{0:T(128)S(1)} %pad_add_fusion.pos, bf16[4,32,1024]{2,1,0:T(8,128)(2,1)S(1)} %copy.17.vo, ...), custom_call_target="tpu_custom_call" | custom-call | flops 4000000000 | bytes 6000000 | tf_op jit(solution)/shard_map/fused/pallas_call | solution.py:236
  41.7 1.5 %collective-permute-done.7 = bf16[8,136,128]{2,1,0:T(8,128)(2,1)S(1)} collective-permute-done((bf16[8,136,128]{2,1,0:T(8,128)(2,1)S(1)}, bf16[8,136,128]{2,1,0:T(8,128)(2,1)S(1)}, u32[]{:S(2)}, u32[]{:S(2)}) %collective-permute-start.7) | collective-permute-done | bytes 278560 | tf_op jit(solution)/shard_map/ppermute | solution.py:296
  43.3 0.1 add_convert_fusion
  43.4 1.6 %collective-permute-start.8 = (bf16[4,136,128]{2,1,0:T(8,128)(2,1)S(1)}, bf16[4,136,128]{2,1,0:T(8,128)(2,1)S(1)}, u32[]{:S(2)}, u32[]{:S(2)}) collective-permute-start(bf16[4,136,128]{2,1,0:T(8,128)(2,1)S(1)} %slice.45), channel_id=1, source_target_pairs={{0,4},{2,6},{4,0},{6,2},{8,12},{10,14},{12,8},{14,10},{16,20},{18,... | collective-permute-start | bytes 417800 | tf_op jit(solution)/shard_map/ppermute | solution.py:296
  45.0 2.5 %volume.1 = bf16[4,32,1024]{2,1,0:T(8,128)(2,1)S(1)} custom-call(s32[2]{0:T(128)S(1)} %pad_add_fusion.pos, bf16[10,64,1280]{2,1,0:T(8,128)(2,1)S(1)} %get-tuple-element.10.dp, bf16[864,64]{1,0:T(8,128)(2,1)S(1)} %get-tuple-element.11.w1), custom_call_target="tpu_custom_call" | custom-call | flops 1000000000 | bytes 3000000 | tf_op jit(solution)/shard_map/volume/pallas_call | solution.py:272
  47.5 1.7 %collective-permute-done.8 = bf16[4,136,128]{2,1,0:T(8,128)(2,1)S(1)} collective-permute-done((bf16[4,136,128]{2,1,0:T(8,128)(2,1)S(1)}, bf16[4,136,128]{2,1,0:T(8,128)(2,1)S(1)}, u32[]{:S(2)}, u32[]{:S(2)}) %collective-permute-start.8) | collective-permute-done | bytes 139296 | tf_op jit(solution)/shard_map/ppermute | solution.py:296
  49.2 0.1 collective-permute-start.9
  49.3 3.5 %collective-permute-start.11 = (bf16[136,128]{1,0:T(8,128)(2,1)S(1)}, bf16[136,128]{1,0:T(8,128)(2,1)S(1)}, u32[]{:S(2)}, u32[]{:S(2)}) collective-permute-start(bf16[136,128]{1,0:T(8,128)(2,1)S(1)} %get-tuple-element.21), channel_id=1, source_target_pairs={{0,24},{2,26},{4,28},{6,30},{8,16},{10,18},{12,20},{14,22},{16,8},... | collective-permute-start | bytes 104456 | tf_op jit(solution)/shard_map/ppermute | solution.py:296
  52.8 0.7 %copy_bitcast_fusion = bf16[1,32,4,8,128]{4,3,2,1,0:T(8,128)(2,1)} fusion(bf16[4,32,8,128]{3,2,1,0:T(8,128)(2,1)S(1)} %bitcast.44), kind=kLoop, calls=%fused_computation.2 | loop fusion | bytes 524288 | tf_op jit(solution)/shard_map/broadcast_in_dim | solution.py:327
  53.6 0.7 %copy.15 = bf16[128,64]{0,1:T(8,128)(2,1)} copy(bf16[128,64]{1,0:T(8,128)(2,1)S(1)} %get-tuple-element.9) | data formatting | bytes 32768 | tf_op jit(solution)/shard_map/fused/pallas_call | solution.py:236
  54.3 0.8 %collective-permute-done.11 = bf16[136,128]{1,0:T(8,128)(2,1)S(1)} collective-permute-done((bf16[136,128]{1,0:T(8,128)(2,1)S(1)}, bf16[136,128]{1,0:T(8,128)(2,1)S(1)}, u32[]{:S(2)}, u32[]{:S(2)}) %collective-permute-start.11) | collective-permute-done | bytes 34848 | tf_op jit(solution)/shard_map/ppermute | solution.py:296
  55.1 2.5 %collective-permute-done.10 = bf16[136,128]{1,0:T(8,128)(2,1)S(1)} collective-permute-done((bf16[136,128]{1,0:T(8,128)(2,1)S(1)}, bf16[136,128]{1,0:T(8,128)(2,1)S(1)}, u32[]{:S(2)}, u32[]{:S(2)}) %collective-permute-start.10) | collective-permute-done | bytes 34848 | tf_op jit(solution)/shard_map/ppermute | solution.py:296
  57.7 0.1 fusion.2
  57.8 0.6 %slice.52 = f32[108,128]{1,0:T(8,128)} slice(f32[136,128]{1,0:T(8,128)S(1)} %fusion.1), slice={[0:108], [0:128]} | slice | bytes 110592 | tf_op jit(solution)/shard_map/slice | solution.py:329
  58.4 0.6 %pad_maximum_fusion.1 = f32[54,64]{1,0:T(8,128)} fusion(f32[27,64]{1,0:T(8,128)S(1)} %get-tuple-element.24, f32[27,64]{1,0:T(8,128)S(1)} %get-tuple-element.23), kind=kLoop, calls=%fused_computation.12 | loop fusion | flops 3456 | bytes 27648 | tf_op jit(solution)/shard_map/concatenate | solution.py:328
  (19 shorter events, 0.3 us)
Async XLA Ops:
  0.6 19.6 %copy-start = (bf16[1,128,1,2,32]{1,4,3,2,0:T(8,128)(2,1)S(1)}, bf16[1,128,1,2,32]{1,4,3,2,0:T(8,128)(2,1)}, u32[]{:S(2)}) copy-start(bf16[1,128,1,2,32]{1,4,3,2,0:T(8,128)(2,1)} %param.7) | copy-start | bytes 49156
  2.3 7.1 %collective-permute-start.4 = (bf16[136,128]{1,0:T(8,128)(2,1)S(1)}, bf16[136,128]{1,0:T(8,128)(2,1)S(1)}, u32[]{:S(2)}, u32[]{:S(2)}) collective-permute-start(bf16[136,128]{1,0:T(8,128)(2,1)S(1)} %get-tuple-element.19), channel_id=1, source_target_pairs={{0,24},{2,26},{4,28},{6,30},{8,16},{10,18},{12,20},{14,22},{16,8},... | collective-permute-start | bytes 104456 | tf_op jit(solution)/shard_map/ppermute | solution.py:296
  7.5 4.8 %collective-permute-start.3 = (bf16[136,128]{1,0:T(8,128)(2,1)S(1)}, bf16[136,128]{1,0:T(8,128)(2,1)S(1)}, u32[]{:S(2)}, u32[]{:S(2)}) collective-permute-start(bf16[136,128]{1,0:T(8,128)(2,1)S(1)} %get-tuple-element.19), channel_id=1, source_target_pairs={{0,16},{2,18},{4,20},{6,22},{8,24},{10,26},{12,28},{14,30},{16,0},... | collective-permute-start | bytes 104456 | tf_op jit(solution)/shard_map/ppermute | solution.py:296
  7.5 4.8 %collective-permute-start.2 = (bf16[136,128]{1,0:T(8,128)(2,1)S(1)}, bf16[136,128]{1,0:T(8,128)(2,1)S(1)}, u32[]{:S(2)}, u32[]{:S(2)}) collective-permute-start(bf16[136,128]{1,0:T(8,128)(2,1)S(1)} %get-tuple-element.19), channel_id=1, source_target_pairs={{0,8},{2,10},{4,12},{6,14},{8,0},{10,2},{12,4},{14,6},{16,24},{18,... | collective-permute-start | bytes 104456 | tf_op jit(solution)/shard_map/ppermute | solution.py:296
  12.3 5.1 %collective-permute-start.5 = (bf16[4,136,128]{2,1,0:T(8,128)(2,1)S(1)}, bf16[4,136,128]{2,1,0:T(8,128)(2,1)S(1)}, u32[]{:S(2)}, u32[]{:S(2)}) collective-permute-start(bf16[4,136,128]{2,1,0:T(8,128)(2,1)S(1)} %pad_maximum_fusion), channel_id=1, source_target_pairs={{0,4},{2,6},{4,0},{6,2},{8,12},{10,14},{12,8},{14,10},{16,20},{18,... | collective-permute-start | bytes 417800 | tf_op jit(solution)/shard_map/ppermute | solution.py:296
  17.5 10.7 %collective-permute-start.6 = (bf16[8,136,128]{2,1,0:T(8,128)(2,1)S(1)}, bf16[8,136,128]{2,1,0:T(8,128)(2,1)S(1)}, u32[]{:S(2)}, u32[]{:S(2)}) collective-permute-start(bf16[8,136,128]{2,1,0:T(8,128)(2,1)S(1)} %constant_dynamic-update-slice_fusion.ga), channel_id=1, source_target_pairs={{0,2},{2,0},{4,6},{6,4},{8,10},{10,8},{12,14},{14,12},{16,18},{18,... | collective-permute-start | bytes 835592 | tf_op jit(solution)/shard_map/ppermute | solution.py:296
  18.7 9.5 %collective-permute-start = (bf16[4,32,1024]{2,1,0:T(8,128)(2,1)S(1)}, bf16[4,32,1024]{2,1,0:T(8,128)(2,1)S(1)}, u32[]{:S(2)}, u32[]{:S(2)}) collective-permute-start(bf16[4,32,1024]{2,1,0:T(8,128)(2,1)S(1)} %copy.17.vo), channel_id=1, source_target_pairs={{0,1},{1,0},{2,3},{3,2},{4,5},{5,4},{6,7},{7,6},{8,9},{9,8},{10,11... | collective-permute-start | bytes 786440 | tf_op jit(solution)/shard_map/ppermute | solution.py:305
  20.4 7.8 %collective-permute-start.1 = (bf16[128,64]{1,0:T(8,128)(2,1)S(1)}, bf16[128,64]{1,0:T(8,128)(2,1)S(1)}, u32[]{:S(2)}, u32[]{:S(2)}) collective-permute-start(bf16[128,64]{1,0:T(8,128)(2,1)S(1)} %copy.14.co), channel_id=1, source_target_pairs={{0,1},{1,0},{2,3},{3,2},{4,5},{5,4},{6,7},{7,6},{8,9},{9,8},{10,11... | collective-permute-start | bytes 49160 | tf_op jit(solution)/shard_map/ppermute | solution.py:306
  41.7 1.6 %collective-permute-start.7 = (bf16[8,136,128]{2,1,0:T(8,128)(2,1)S(1)}, bf16[8,136,128]{2,1,0:T(8,128)(2,1)S(1)}, u32[]{:S(2)}, u32[]{:S(2)}) collective-permute-start(bf16[8,136,128]{2,1,0:T(8,128)(2,1)S(1)} %get-tuple-element.13), channel_id=1, source_target_pairs={{0,2},{2,0},{4,6},{6,4},{8,10},{10,8},{12,14},{14,12},{16,18},{18,... | collective-permute-start | bytes 835592 | tf_op jit(solution)/shard_map/ppermute | solution.py:296
  43.4 5.8 %collective-permute-start.8 = (bf16[4,136,128]{2,1,0:T(8,128)(2,1)S(1)}, bf16[4,136,128]{2,1,0:T(8,128)(2,1)S(1)}, u32[]{:S(2)}, u32[]{:S(2)}) collective-permute-start(bf16[4,136,128]{2,1,0:T(8,128)(2,1)S(1)} %slice.45), channel_id=1, source_target_pairs={{0,4},{2,6},{4,0},{6,2},{8,12},{10,14},{12,8},{14,10},{16,20},{18,... | collective-permute-start | bytes 417800 | tf_op jit(solution)/shard_map/ppermute | solution.py:296
  49.2 5.0 %collective-permute-start.9 = (bf16[136,128]{1,0:T(8,128)(2,1)S(1)}, bf16[136,128]{1,0:T(8,128)(2,1)S(1)}, u32[]{:S(2)}, u32[]{:S(2)}) collective-permute-start(bf16[136,128]{1,0:T(8,128)(2,1)S(1)} %get-tuple-element.20), channel_id=1, source_target_pairs={{0,8},{2,10},{4,12},{6,14},{8,0},{10,2},{12,4},{14,6},{16,24},{18,... | collective-permute-start | bytes 104456 | tf_op jit(solution)/shard_map/ppermute | solution.py:296
  49.3 5.8 %collective-permute-start.11 = (bf16[136,128]{1,0:T(8,128)(2,1)S(1)}, bf16[136,128]{1,0:T(8,128)(2,1)S(1)}, u32[]{:S(2)}, u32[]{:S(2)}) collective-permute-start(bf16[136,128]{1,0:T(8,128)(2,1)S(1)} %get-tuple-element.21), channel_id=1, source_target_pairs={{0,24},{2,26},{4,28},{6,30},{8,16},{10,18},{12,20},{14,22},{16,8},... | collective-permute-start | bytes 104456 | tf_op jit(solution)/shard_map/ppermute | solution.py:296
  52.8 4.8 %collective-permute-start.10 = (bf16[136,128]{1,0:T(8,128)(2,1)S(1)}, bf16[136,128]{1,0:T(8,128)(2,1)S(1)}, u32[]{:S(2)}, u32[]{:S(2)}) collective-permute-start(bf16[136,128]{1,0:T(8,128)(2,1)S(1)} %get-tuple-element.22), channel_id=1, source_target_pairs={{0,16},{2,18},{4,20},{6,22},{8,24},{10,26},{12,28},{14,30},{16,0},... | collective-permute-start | bytes 104456 | tf_op jit(solution)/shard_map/ppermute | solution.py:296

commit v2 on v1

--- a/solution.py
+++ b/solution.py
@@ -7,8 +7,11 @@
 from jax.experimental.pallas import tpu as pltpu
 from jax.sharding import PartitionSpec as P
 
+
 BF = jnp.bfloat16
 F32 = jnp.float32
+VMEM = pl.BlockSpec(memory_space=pltpu.VMEM)
+SMEM = pl.BlockSpec(memory_space=pltpu.SMEM)
 
 
 def dot(a, b):
@@ -23,8 +26,17 @@
     return lax.broadcasted_iota(jnp.int32, shape, dim)
 
 
+def where_one(mask):
+    return mask.astype(F32).astype(BF)
+
+
 def eye(n):
-    return (iota((n, n), 0) == iota((n, n), 1)).astype(F32).astype(BF)
+    return where_one(iota((n, n), 0) == iota((n, n), 1))
+
+
+def halves(x):
+    hi = x.astype(BF)
+    return hi, (x - hi.astype(F32)).astype(BF)
 
 
 def roll_z(x, by):
@@ -42,95 +54,159 @@
     return jnp.where(inside, pltpu.roll(x, (-(db * 64 + dc)) % 256, 1), 0.0)
 
 
-def unpack_weights(me, g0_ref, g1_ref, w1f, w2f):
-    for d in range(16):
-        k = jnp.bitwise_xor(me, d)
-        core, rest = k % 2, (k // 2) % 2 * 4 + k // 4
-        blk = lax.select(core == 0, g0_ref[rest], g1_ref[rest])
-        blk = blk.astype(F32)
-        w2f[108 * d : 108 * d + 108, :] = blk[0:108]
-        w1f[54 * d : 54 * d + 27, :] = blk[108:135, 0:64]
-        w1f[54 * d + 27 : 54 * d + 54, :] = blk[108:135, 64:128]
+def pack_kernel(first, second, out, wide, narrow):
+    wide[...] = jnp.zeros(wide.shape, F32)
+    wide[0:108, :] = second[...].astype(F32)
+    narrow[...] = first[...].astype(F32)
+    wide[112:139, 0:64] = narrow[0:27, :]
+    wide[112:139, 64:128] = narrow[27:54, :]
+    out[...] = wide[...].astype(BF)
+
+
+def pack_call(first, second):
+    return pl.pallas_call(
+        pack_kernel,
+        out_shape=jax.ShapeDtypeStruct((144, 128), BF),
+        in_specs=[VMEM] * 2,
+        out_specs=VMEM,
+        scratch_shapes=[pltpu.VMEM((144, 128), F32), pltpu.VMEM((54, 64), F32)],
+        compiler_params=pltpu.CompilerParams(vmem_limit_bytes=2 << 20),
+        cost_estimate=pl.CostEstimate(flops=40_000, bytes_accessed=80_000, transcendentals=0),
+        name="pack",
+    )(first, second)
+
+
+def finish_kernel(kept, one, two, three, first, second, total):
+    total[...] = (
+        kept[0].astype(F32) + one[...].astype(F32) + two[...].astype(F32) + three[...].astype(F32)
+    )
+    second[...] = total[0:108, :]
+    first[0:27, :] = total[112:139, 0:64]
+    first[27:54, :] = total[112:139, 64:128]
+
+
+def finish_call(kept, pieces):
+    return pl.pallas_call(
+        finish_kernel,
+        out_shape=(
+            jax.ShapeDtypeStruct((54, 64), F32),
+            jax.ShapeDtypeStruct((108, 128), F32),
+        ),
+        in_specs=[VMEM] * 4,
+        out_specs=(VMEM,) * 2,
+        scratch_shapes=[pltpu.VMEM((144, 128), F32)],
+        compiler_params=pltpu.CompilerParams(vmem_limit_bytes=2 << 20),
+        cost_estimate=pl.CostEstimate(flops=80_000, bytes_accessed=300_000, transcendentals=0),
+        name="finish",
+    )(kept, *pieces)
+
+
+def shift_kernel(pos, own, other, out):
+    s = pos[1]
+    out[0] = jnp.zeros((96, 1024), BF)
+    out[9] = jnp.zeros((96, 1024), BF)
+    for p in range(4):
+        for block, place in ((own, 4 * s + 1 + p), (other, 4 * (1 - s) + 1 + p)):
+            out[place, 32:64, :] = block[p]
+            for y in range(8):
+                lanes = slice(y * 128, y * 128 + 128)
+                line = block[p, :, lanes].astype(F32)
+                out[place, 0:32, lanes] = roll_z(line, 1).astype(BF)
+                out[place, 64:96, lanes] = roll_z(line, -1).astype(BF)
+
+
+def shift_call(pos, own, other):
+    return pl.pallas_call(
+        shift_kernel,
+        out_shape=jax.ShapeDtypeStruct((10, 96, 1024), BF),
+        in_specs=[SMEM, VMEM, VMEM],
+        out_specs=VMEM,
+        compiler_params=pltpu.CompilerParams(vmem_limit_bytes=8 << 20),
+        cost_estimate=pl.CostEstimate(flops=600_000, bytes_accessed=2_500_000, transcendentals=0),
+        name="shift",
+    )(pos, own, other)
+
+
+def unpack_weights(me, near, far, w1f, w2f):
+    for parity in range(2):
+
+        @pl.when(me % 2 == parity)
+        def _():
+            for d in range(16):
+                k = jnp.bitwise_xor(me, d)
+                ref = near if d % 2 == parity else far
+                blk = ref[(k // 2) % 2 * 4 + k // 4].astype(F32)
+                w2f[108 * d : 108 * d + 108, :] = blk[0:108]
+                w1f[54 * d : 54 * d + 27, :] = blk[112:139, 0:64]
+                w1f[54 * d + 27 : 54 * d + 54, :] = blk[112:139, 64:128]
 
 
 def fused_kernel(
     factor_one, factor_two,
-    pos, vo, vx, co, cx, ga, gb,
-    pooled_out, keep_out, send_out, dp_out, w1_out,
-    w1f, w2f, w2s, vs, slope, fpl, fs, d2p, t2, wcat, acc1, g2f, g1f, pg, chunk,
+    pos, v3, co, cx, near, far,
+    pooled_out, keep_out, send_out, dp, w1_out,
+    w1f, w2f, w2s, slope, fpl, fs, d2p, t2, g2f, g1w,
 ):
     me, s = pos[0], pos[1]
-    unpack_weights(me, ga, gb, w1f, w2f)
+    unpack_weights(me, near, far, w1f, w2f)
     w1_out[...] = w1f[...].astype(BF)
     w2s[...] = w2f[...].astype(BF)
-    vs[...] = jnp.zeros(vs.shape, BF)
-    for p in range(4):
-        vs[4 * s + 1 + p, :, 128:1152] = vo[p]
-        vs[4 * (1 - s) + 1 + p, :, 128:1152] = vx[p]
     id64, id128 = eye(64), eye(128)
     lhs1 = jnp.concatenate(
         [
             dot_nt(
                 id64,
                 jnp.concatenate(
-                    [w1f[(ab * 3 + c) * 32 : (ab * 3 + c) * 32 + 32, :] for ab in range(9)], axis=0
+                    [w1f[(a * 3 + b) * 96 : (a * 3 + b) * 96 + 96, :] for a in range(3)], axis=0
                 ).astype(BF),
             ).astype(BF)
-            for c in range(3)
+            for b in range(3)
         ],
         axis=0,
     )
-    pool_m = (iota((256, 128), 0) // 2 == iota((256, 128), 1)).astype(F32).astype(BF)
+    pool1 = where_one(iota((256, 128), 0) // 2 == iota((256, 128), 1))
 
     def cols_of(x):
-        return jnp.concatenate(
-            [vs[x + a, :, b * 128 : b * 128 + 1024] for a in range(3) for b in range(3)], axis=0
-        )
-
-    def first(x2, carry):
+        return jnp.concatenate([v3[x], v3[x + 1], v3[x + 2]], axis=0)
+
+    for x2 in range(4):
         total = [jnp.zeros((64, 128), F32) for _ in range(4)]
         for dx in range(2):
             x = 2 * x2 + dx
             prod = dot(lhs1, cols_of(x))
             for y in range(8):
-                part = prod[:, y * 128 : y * 128 + 128]
-                pre = part[64:128] + roll_z(part[0:64], 1) + roll_z(part[128:192], -1)
+                lanes = slice(y * 128, y * 128 + 128)
+                pre = prod[64:128, lanes]
+                if y > 0:
+                    pre = pre + prod[0:64, (y - 1) * 128 : y * 128]
+                if y < 7:
+                    pre = pre + prod[128:192, (y + 1) * 128 : (y + 2) * 128]
                 sig = jax.nn.sigmoid(pre)
                 act = pre * sig
-                slope[x, :, y * 128 : y * 128 + 128] = sig + act * (1.0 - sig)
+                slope[x, :, lanes] = sig + act * (1.0 - sig)
                 total[y // 2] = total[y // 2] + act
         for h in range(2):
-            pair = jnp.concatenate([total[2 * h], total[2 * h + 1]], axis=1)
-            hi = pair.astype(BF)
-            lo = (pair - hi.astype(F32)).astype(BF)
+            hi, lo = halves(jnp.concatenate([total[2 * h], total[2 * h + 1]], axis=1))
             fpl[x2, :, h * 128 : h * 128 + 128] = (
-                (dot(hi, pool_m) + dot(lo, pool_m)) * 0.125
+                (dot(hi, pool1) + dot(lo, pool1)) * 0.125
             ).astype(BF).astype(F32)
-        return carry
-
-    lax.fori_loop(0, 4, first, 0)
 
     fs[0] = jnp.zeros((576, 256), BF)
     fs[5] = jnp.zeros((576, 256), BF)
     d2p[0] = jnp.zeros((128, 256), BF)
     d2p[5] = jnp.zeros((128, 256), BF)
-
-    def shifts(x2, carry):
+    for x2 in range(4):
         plane = fpl[x2]
         for bc in range(9):
             fs[x2 + 1, bc * 64 : bc * 64 + 64, :] = roll_yz(plane, bc // 3 - 1, bc % 3 - 1).astype(BF)
-        return carry
-
-    lax.fori_loop(0, 4, shifts, 0)
     w2t = dot_nt(id128, w2s[...]).astype(BF)
     col = iota((64, 256), 1)
-    spread2 = (iota((64, 256), 0) == (col // 128) * 32 + (col % 64) // 2).astype(F32).astype(BF)
-    row = iota((256, 64), 0)
-    pool2 = (iota((256, 64), 1) == (row // 128) * 32 + (row % 64) // 2).astype(F32).astype(BF)
-
-    def second(x4, carry):
+    spread2 = where_one(iota((64, 256), 0) == (col // 128) * 32 + (col % 64) // 2)
+    col = iota((64, 256), 1)
+    pool2 = where_one(iota((64, 256), 0) == (col // 128) * 32 + (col % 64) // 2)
+    for x4 in range(2):
         cot = lax.select(x4 == s, co[...], cx[...])
-        wide = dot(cot, spread2) * 0.125
+        wide = dot(dot_nt(id128, cot).astype(BF), spread2) * 0.125
         total = jnp.zeros((128, 256), F32)
         for dx in range(2):
             x2 = 2 * x4 + dx
@@ -141,67 +217,67 @@
             total = total + act
             d2p[x2 + 1] = (wide * (sig + act * (1.0 - sig))).astype(BF)
         t2[x4] = total
-        return carry
-
-    lax.fori_loop(0, 2, second, 0)
-    mine = t2[s]
-    hi = mine.astype(BF)
-    lo = (mine - hi.astype(F32)).astype(BF)
-    pooled_out[...] = ((dot(hi, pool2) + dot(lo, pool2)) * 0.125).astype(BF)
-
-    deltas = jnp.concatenate([d2p[1], d2p[2], d2p[3], d2p[4]], axis=1)
+    hi, lo = halves(t2[s])
+    pooled_out[...] = ((dot_nt(pool2, hi) + dot_nt(pool2, lo)) * 0.125).astype(BF)
+
+    lhs = jnp.concatenate([fs[p] for p in range(1, 5)], axis=1)
+    rhs = jnp.concatenate(
+        [jnp.concatenate([d2p[p + 1 - a] for p in range(1, 5)], axis=1) for a in range(3)], axis=0
+    )
+    prod = dot_nt(lhs, rhs) * factor_two
     for a in range(3):
-        lhs = jnp.concatenate([fs[a], fs[a + 1], fs[a + 2], fs[a + 3]], axis=1)
-        g2f[a * 576 : a * 576 + 576, :] = dot_nt(lhs, deltas) * factor_two
-        wcat[:, a * 128 : a * 128 + 128] = w2s[a * 576 : a * 576 + 576, :]
-
-    spread1 = (iota((128, 256), 0) == iota((128, 256), 1) // 2).astype(F32).astype(BF)
-    acc1[...] = jnp.zeros(acc1.shape, F32)
-    dp_out[...] = jnp.zeros(dp_out.shape, BF)
-
-    def back(x2, carry):
+        g2f[a * 576 : a * 576 + 576, :] = prod[:, a * 128 : a * 128 + 128]
+    g2f[1728:1736, :] = jnp.zeros((8, 128), F32)
+
+    spread1 = where_one(iota((128, 256), 0) == iota((128, 256), 1) // 2)
+    dp[0] = jnp.zeros((64, 1280), BF)
+    dp[9] = jnp.zeros((64, 1280), BF)
+    for x in range(8):
+        dp[x + 1, :, 0:128] = jnp.zeros((64, 128), BF)
+        dp[x + 1, :, 1152:1280] = jnp.zeros((64, 128), BF)
+    back = jnp.concatenate([w2s[a * 576 : a * 576 + 576, :] for a in range(3)], axis=1)
+    for x2 in range(4):
         rhs = jnp.concatenate([d2p[x2 + 2], d2p[x2 + 1], d2p[x2]], axis=0)
-        prod = dot(wcat[...], rhs)
-        grad = jnp.zeros((64, 256), F32)
+        prod = dot(back, rhs)
+        grad = prod[256:320]
         for bc in range(9):
-            grad = grad + roll_yz(prod[bc * 64 : bc * 64 + 64], 1 - bc // 3, 1 - bc % 3)
+            if bc != 4:
+                grad = grad + roll_yz(prod[bc * 64 : bc * 64 + 64], 1 - bc // 3, 1 - bc % 3)
         grad = grad.astype(BF)
         for h in range(2):
             wide = dot(grad[:, h * 128 : h * 128 + 128], spread1) * 0.125
             for dx in range(2):
                 for y in range(4):
-                    lanes = slice((4 * h + y) * 128, (4 * h + y) * 128 + 128)
-                    value = wide[:, (y // 2) * 128 : (y // 2) * 128 + 128] * slope[2 * x2 + dx, :, lanes]
-                    pg[dx, 64:128, lanes] = value.astype(BF)
-                    pg[dx, 0:64, lanes] = roll_z(value, -1).astype(BF)
-                    pg[dx, 128:192, lanes] = roll_z(value, 1).astype(BF)
-        for dx in range(2):
-            x = 2 * x2 + dx
-            dp_out[x + 1, :, 128:1152] = pg[dx, 64:128, :]
-            acc1[...] += dot_nt(cols_of(x), pg[dx])
-        return carry
-
-    lax.fori_loop(0, 4, back, 0)
-    for ab in range(9):
-        for c in range(3):
-            g1f[(ab * 3 + c) * 32 : (ab * 3 + c) * 32 + 32, :] = (
-                acc1[ab * 32 : ab * 32 + 32, c * 64 : c * 64 + 64] * factor_one
-            )
-    chunk[...] = jnp.zeros(chunk.shape, F32)
-    for d in range(16):
-        chunk[0:108, :] = g2f[108 * d : 108 * d + 108, :]
-        chunk[108:135, 0:64] = g1f[54 * d : 54 * d + 27, :]
-        chunk[108:135, 64:128] = g1f[54 * d + 27 : 54 * d + 54, :]
-        k = jnp.bitwise_xor(me, d)
-        place = (k // 2) % 2 * 4 + k // 4
-
-        @pl.when(k % 2 == 0)
+                    at = (4 * h + y) * 128
+                    part = wide[:, (y // 2) * 128 : (y // 2) * 128 + 128]
+                    dp[2 * x2 + dx + 1, :, at + 128 : at + 256] = (
+                        part * slope[2 * x2 + dx, :, at : at + 128]
+                    ).astype(BF)
+
+    prod = jnp.zeros((288, 192), F32)
+    for x in range(8):
+        rhs = jnp.concatenate([dp[x + 1, :, (2 - b) * 128 : (2 - b) * 128 + 1024] for b in range(3)], axis=0)
+        prod = prod + dot_nt(cols_of(x), rhs)
+    prod = prod * factor_one
+    g1w[0:32, :] = jnp.zeros((32, 128), F32)
+    g1w[896:904, :] = jnp.zeros((8, 128), F32)
+    g1w[864:896, :] = jnp.zeros((32, 128), F32)
+    for a in range(3):
+        for b in range(3):
+            block = prod[a * 96 : a * 96 + 96, b * 64 : b * 64 + 64]
+            row = (a * 3 + b) * 96 + 32
+            g1w[row : row + 96, 0:64] = block
+            g1w[row - 27 : row + 69, 64:128] = block
+    for parity in range(2):
+
+        @pl.when(me % 2 == parity)
         def _():
-            keep_out[place] = chunk[...].astype(BF)
-
-        @pl.when(k % 2 == 1)
-        def _():
-            send_out[place] = chunk[...].astype(BF)
+            for d in range(16):
+                k = jnp.bitwise_xor(me, d)
+                ref = keep_out if d % 2 == parity else send_out
+                place = (k // 2) % 2 * 4 + k // 4
+                ref[place, 0:112, :] = g2f[108 * d : 108 * d + 112, :].astype(BF)
+                ref[place, 112:144, :] = g1w[54 * d + 32 : 54 * d + 64, :].astype(BF)
 
 
 def volume_kernel(pos, dp, w1, out, wd):
@@ -209,8 +285,7 @@
     for ab in range(9):
         wd[:, ab * 64 : ab * 64 + 64] = w1[ab * 96 : ab * 96 + 96, :]
     lhs = wd[...]
-
-    def plane(p, carry):
+    for p in range(4):
         x = 4 * s + p
         rhs = jnp.concatenate(
             [
@@ -226,54 +301,44 @@
             out[p, :, y * 128 : y * 128 + 128] = (
                 part[32:64] + roll_z(part[0:32], -1) + roll_z(part[64:96], 1)
             ).astype(BF)
-        return carry
-
-    lax.fori_loop(0, 4, plane, 0)
-
-
-def fused_call(factor_one, factor_two, pos, vo, vx, co, cx, ga, gb):
-    vmem = pl.BlockSpec(memory_space=pltpu.VMEM)
+
+
+def fused_call(factor_one, factor_two, pos, v3, co, cx, near, far):
     return pl.pallas_call(
         functools.partial(fused_kernel, factor_one, factor_two),
         out_shape=(
-            jax.ShapeDtypeStruct((128, 64), BF),
-            jax.ShapeDtypeStruct((8, 136, 128), BF),
-            jax.ShapeDtypeStruct((8, 136, 128), BF),
+            jax.ShapeDtypeStruct((64, 128), BF),
+            jax.ShapeDtypeStruct((8, 144, 128), BF),
+            jax.ShapeDtypeStruct((8, 144, 128), BF),
             jax.ShapeDtypeStruct((10, 64, 1280), BF),
             jax.ShapeDtypeStruct((864, 64), BF),
         ),
-        in_specs=[pl.BlockSpec(memory_space=pltpu.SMEM)] + [vmem] * 6,
-        out_specs=(vmem,) * 5,
+        in_specs=[SMEM] + [VMEM] * 5,
+        out_specs=(VMEM,) * 5,
         scratch_shapes=[
             pltpu.VMEM((864, 64), F32),
             pltpu.VMEM((1728, 128), F32),
             pltpu.VMEM((1728, 128), BF),
-            pltpu.VMEM((10, 32, 1280), BF),
             pltpu.VMEM((8, 64, 1024), F32),
             pltpu.VMEM((4, 64, 256), F32),
             pltpu.VMEM((6, 576, 256), BF),
             pltpu.VMEM((6, 128, 256), BF),
             pltpu.VMEM((2, 128, 256), F32),
-            pltpu.VMEM((576, 384), BF),
-            pltpu.VMEM((288, 192), F32),
-            pltpu.VMEM((1728, 128), F32),
-            pltpu.VMEM((864, 64), F32),
-            pltpu.VMEM((2, 192, 1024), BF),
-            pltpu.VMEM((136, 128), F32),
+            pltpu.VMEM((1736, 128), F32),
+            pltpu.VMEM((904, 128), F32),
         ],
         compiler_params=pltpu.CompilerParams(vmem_limit_bytes=48 << 20),
         cost_estimate=pl.CostEstimate(flops=4_000_000_000, bytes_accessed=6_000_000, transcendentals=700_000),
         name="fused",
-    )(pos, vo, vx, co, cx, ga, gb)
+    )(pos, v3, co, cx, near, far)
 
 
 def volume_call(pos, dp, w1):
-    vmem = pl.BlockSpec(memory_space=pltpu.VMEM)
     return pl.pallas_call(
         volume_kernel,
         out_shape=jax.ShapeDtypeStruct((4, 32, 1024), BF),
-        in_specs=[pl.BlockSpec(memory_space=pltpu.SMEM), vmem, vmem],
-        out_specs=vmem,
+        in_specs=[SMEM, VMEM, VMEM],
+        out_specs=VMEM,
         scratch_shapes=[pltpu.VMEM((96, 576), BF)],
         compiler_params=pltpu.CompilerParams(vmem_limit_bytes=16 << 20),
         cost_estimate=pl.CostEstimate(flops=1_000_000_000, bytes_accessed=3_000_000, transcendentals=0),
@@ -296,37 +361,40 @@
     return lax.ppermute(x, "dp", [(i, i ^ bit) for i in range(16)])
 
 
+def plane_major(block):
+    return jnp.transpose(block[0], (1, 0, 2, 3)).reshape(4, 32, 1024)
+
+
 def paired(volumes, w_first, w_second, cotangent):
     count = 16 * 2 * (volumes.size // 32)
     factor_one, factor_two = float(count) ** (-0.5), float(count // 8) ** (-0.5)
+    across_space = [(0, 1), (1, 0)]
     pos = jnp.stack([lax.axis_index("dp"), lax.axis_index("space")]).astype(jnp.int32)
-    own = jnp.transpose(volumes[0], (1, 0, 2, 3)).reshape(4, 32, 1024)
-    cot = cotangent.reshape(128, 64)
-    other = lax.ppermute(own, "space", [(0, 1), (1, 0)])
-    cot_other = lax.ppermute(cot, "space", [(0, 1), (1, 0)])
-    shard = jnp.concatenate(
-        [
-            w_second,
-            jnp.concatenate([w_first[:27], w_first[27:]], axis=1),
-            jnp.zeros((1, 128), BF),
-        ],
-        axis=0,
-    )
-    along_z = jnp.stack([shard] + [swap(shard, 4 * k) for k in range(1, 4)])
-    along_y = jnp.concatenate([along_z, swap(along_z, 2)])
+    volumes_other = lax.ppermute(volumes, "space", across_space)
+    cot = jnp.transpose(cotangent, (0, 2, 3, 4, 1)).reshape(64, 128)
+    cot_other = lax.ppermute(cot, "space", across_space)
+    shard = pack_call(w_first, w_second)
+    pieces = [swap(shard, 4 * k) for k in range(1, 4)]
+    along_z = jnp.stack([shard] + pieces)
+    piece = swap(along_z, 2)
+    along_y = jnp.concatenate([along_z, piece])
     across = swap(along_y, 1)
+    own = plane_major(volumes)
+    other = plane_major(volumes_other)
+    moved = shift_call(pos, own, other)
     pooled, keep, send, delta, w_one = fused_call(
-        factor_one, factor_two, pos, own, other, cot, cot_other, along_y, across
-    )
-    part = (keep.astype(F32) + swap(send, 1).astype(F32)).astype(BF)
-    part = (part[:4].astype(F32) + swap(part[4:], 2).astype(F32)).astype(BF)
-    total = part[0].astype(F32)
-    for k in range(1, 4):
-        total = total + swap(part[k], 4 * k).astype(F32)
+        factor_one, factor_two, pos, moved, cot, cot_other, along_y, across
+    )
+    got = swap(send, 1)
+    part = (keep.astype(F32) + got.astype(F32)).astype(BF)
+    got = swap(part[4:], 2)
+    part = (part[:4].astype(F32) + got.astype(F32)).astype(BF)
+    pieces = [swap(part[k], 4 * k) for k in range(1, 4)]
+    share_one, share_two = finish_call(part, pieces)
     grad = volume_call(pos, delta, w_one)
     grad = jnp.transpose(grad.reshape(4, 32, 8, 128), (1, 0, 2, 3))[None]
-    share_one = jnp.concatenate([total[108:135, :64], total[108:135, 64:]], axis=0)
-    return pooled.reshape(1, 128, 1, 2, 32), grad, share_one, total[:108]
+    pooled = jnp.transpose(pooled.reshape(1, 1, 2, 32, 128), (0, 4, 1, 2, 3))
+    return pooled, grad, share_one, share_two
 
 
 def with_halo(block, sides, width):
@@ -398,7 +466,7 @@
 
 
 def conv_weight_grad(padded, grads):
-    samples_here, in_width, depth_padded, extent_y, extent_z = padded.shape
+    _, in_width, depth_padded, extent_y, extent_z = padded.shape
     extent_x = depth_padded - 2
     framed = pad_sides(padded)
     pieces = []

time: 59.3 us -> 54.3 us (0.916)
  waiting for transfers between devices: 21.4 us -> 19.4 us
  other arithmetic: 1.68 us -> 0.22 us
  Pallas kernels: 16 us -> 14.6 us
  local copies, waits for them, and re-layouts: 4.33 us -> 3.57 us
  starting transfers between devices: 14.8 us -> 15.5 us
    pallas_call x1, Pallas kernels: 13.5 us -> 11.2 us  [fused_call(): pl.pallas_call(functools.partial(fused_kernel, factor_one, factor_two), o...]
    pallas_call x0 -> x3, Pallas kernels: none -> 1.66 us  [the longest x1 0.88 us: shift_call(): pl.pallas_call(shift_kernel, out_shape=jax.ShapeDtypeStruct((10, 96, 1024...]
    slice x4 -> x1, local copies, waits for them, and re-layouts: 1.49 us -> 0.01 us  [paired(): got = swap(part[4:], 2)]
    unnamed x6 -> x11, local copies, waits for them, and re-layouts: 0.08 us -> 1.54 us
    ppermute x2, waiting for transfers between devices: 7.12 us -> 5.81 us  [the longest x1 5.81 us: paired(): volumes_other = lax.ppermute(volumes, 'space', across_space)]
    unnamed x1 -> x0, other arithmetic: 0.83 us -> none
    pallas_call x1, Pallas kernels: 2.47 us -> 1.72 us  [volume_call(): pl.pallas_call(volume_kernel, out_shape=jax.ShapeDtypeStruct((4, 32, 1024...]
    ppermute x10, starting transfers between devices: 12.7 us -> 13.4 us  [swap(): return lax.ppermute(x, 'dp', [(i, i ^ bit) for i in range(16)])]
  transfers between devices with their start and end apart: 12 -> 12, of which waited for: 8 -> 9; matrix products, arithmetic and copies ran while one was open for 5% -> 4% of each run, Pallas kernels for 4% -> 5%
where the time goes in v2:
time: 54.3 us; the launch traced here: 54 us
  waiting for transfers between devices  19.4 us (36%)
  starting transfers between devices  15.5 us (29%)
  Pallas kernels  14.6 us (27%)
  local copies, waits for them, and re-layouts  3.57 us (7%)
  between operations  0.78 us (1%)
    ppermute x10, waiting for transfers between devices, swap(): return lax.ppermute(x, 'dp', [(i, i ^ bit) for i in range(16)])  13.6 us
    ppermute x10, starting transfers between devices, swap(): return lax.ppermute(x, 'dp', [(i, i ^ bit) for i in range(16)])  13.4 us
    pallas_call x1, Pallas kernels, fused_call(): pl.pallas_call(functools.partial(fused_kernel, factor_one, factor_two), o...  11.2 us
    ppermute x1, waiting for transfers between devices, paired(): volumes_other = lax.ppermute(volumes, 'space', across_space)  5.81 us
    pallas_call x1, Pallas kernels, volume_call(): pl.pallas_call(volume_kernel, out_shape=jax.ShapeDtypeStruct((4, 32, 1024...  1.72 us
    ppermute x1, starting transfers between devices, paired(): volumes_other = lax.ppermute(volumes, 'space', across_space)  1.56 us
    unnamed x11, local copies, waits for them, and re-layouts  1.54 us
    reshape x4, local copies, waits for them, and re-layouts, plane_major(): return jnp.transpose(block[0], (1, 0, 2, 3)).reshape(4, 32, 1024)  1.24 us
  transfers between devices with their start and end apart: 12, of which 9 were waited for; matrix products, arithmetic and copies ran while one was open for 4% of the time, Pallas kernels for 5%

profile of v2, /device:TPU:0, one launch (start us, length us, event | category | flops | bytes accessed | tf_op | source)
XLA Modules:
  0.0 54.0 jit_solution(17186095874812538237)
XLA Ops:
  0.6 0.7 %copy-done = bf16[108,128]{1,0:T(8,128)(2,1)S(1)} copy-done((bf16[108,128]{1,0:T(8,128)(2,1)S(1)}, bf16[108,128]{1,0:T(8,128)(2,1)}, u32[]{:S(2)}) %copy-start) | copy-done | bytes 27672
  1.4 0.7 %copy-done.1 = bf16[54,64]{1,0:T(8,128)(2,1)S(1)} copy-done((bf16[54,64]{1,0:T(8,128)(2,1)S(1)}, bf16[54,64]{1,0:T(8,128)(2,1)}, u32[]{:S(2)}) %copy-start.1) | copy-done | bytes 6936
  2.1 0.1 pack.1
  2.2 5.1 %collective-permute-start.4 = (bf16[144,128]{1,0:T(8,128)(2,1)S(1)}, bf16[144,128]{1,0:T(8,128)(2,1)S(1)}, u32[]{:S(2)}, u32[]{:S(2)}) collective-permute-start(bf16[144,128]{1,0:T(8,128)(2,1)S(1)} %pack.1), channel_id=1, source_target_pairs={{0,24},{2,26},{4,28},{6,30},{8,16},{10,18},{12,20},{14,22},{16,8},... | collective-permute-start | bytes 110600 | tf_op jit(solution)/shard_map/ppermute | solution.py:361
  7.3 0.6 %collective-permute-start.2 = (bf16[144,128]{1,0:T(8,128)(2,1)S(1)}, bf16[144,128]{1,0:T(8,128)(2,1)S(1)}, u32[]{:S(2)}, u32[]{:S(2)}) collective-permute-start(bf16[144,128]{1,0:T(8,128)(2,1)S(1)} %pack.1), channel_id=1, source_target_pairs={{0,8},{2,10},{4,12},{6,14},{8,0},{10,2},{12,4},{14,6},{16,24},{18,... | collective-permute-start | bytes 110600 | tf_op jit(solution)/shard_map/ppermute | solution.py:361
  7.9 1.3 %collective-permute-done.4 = bf16[144,128]{1,0:T(8,128)(2,1)S(1)} collective-permute-done((bf16[144,128]{1,0:T(8,128)(2,1)S(1)}, bf16[144,128]{1,0:T(8,128)(2,1)S(1)}, u32[]{:S(2)}, u32[]{:S(2)}) %collective-permute-start.4) | collective-permute-done | bytes 36896 | tf_op jit(solution)/shard_map/ppermute | solution.py:361
  9.2 2.9 %collective-permute-done.3 = bf16[144,128]{1,0:T(8,128)(2,1)S(1)} collective-permute-done((bf16[144,128]{1,0:T(8,128)(2,1)S(1)}, bf16[144,128]{1,0:T(8,128)(2,1)S(1)}, u32[]{:S(2)}, u32[]{:S(2)}) %collective-permute-start.3) | collective-permute-done | bytes 36896 | tf_op jit(solution)/shard_map/ppermute | solution.py:361
  12.1 1.6 %collective-permute-start.5 = (bf16[4,144,128]{2,1,0:T(8,128)(2,1)S(1)}, bf16[4,144,128]{2,1,0:T(8,128)(2,1)S(1)}, u32[]{:S(2)}, u32[]{:S(2)}) collective-permute-start(bf16[4,144,128]{2,1,0:T(8,128)(2,1)S(1)} %pad_maximum_fusion), channel_id=1, source_target_pairs={{0,4},{2,6},{4,0},{6,2},{8,12},{10,14},{12,8},{14,10},{16,20},{18,... | collective-permute-start | bytes 442376 | tf_op jit(solution)/shard_map/ppermute | solution.py:361
  13.8 3.6 %collective-permute-done.5 = bf16[4,144,128]{2,1,0:T(8,128)(2,1)S(1)} collective-permute-done((bf16[4,144,128]{2,1,0:T(8,128)(2,1)S(1)}, bf16[4,144,128]{2,1,0:T(8,128)(2,1)S(1)}, u32[]{:S(2)}, u32[]{:S(2)}) %collective-permute-start.5) | collective-permute-done | bytes 147488 | tf_op jit(solution)/shard_map/ppermute | solution.py:361
  17.4 0.1 collective-permute-start.6
  17.5 1.6 %collective-permute-start = (bf16[1,32,4,8,128]{4,3,2,1,0:T(8,128)(2,1)}, bf16[1,32,4,8,128]{4,3,2,1,0:T(8,128)(2,1)S(1)}, u32[]{:S(2)}, u32[]{:S(2)}) collective-permute-start(bf16[1,32,4,8,128]{4,3,2,1,0:T(8,128)(2,1)} %param.4), channel_id=1, source_target_pairs={{0,1},{1,0},{2,3},{3,2},{4,5},{5,4},{6,7},{7,6},{8,9},{9,8},{10,11... | collective-permute-start | bytes 786440 | tf_op jit(solution)/shard_map/ppermute | solution.py:373
  19.0 0.5 collective-permute-start.1
  19.5 0.1 pad_add_fusion.pos
  19.6 1.0 %reshape.28 = bf16[4,32,1024]{2,0,1:T(4,128)(2,1)S(1)} reshape(bf16[4,32,8,128]{3,2,0,1:T(8,128)(2,1)} %bitcast.53) | data formatting | bytes 524288 | tf_op jit(solution)/shard_map/reshape | solution.py:365
  20.7 0.1 copy.11.own
  20.7 5.8 %collective-permute-done = bf16[1,32,4,8,128]{4,3,2,1,0:T(8,128)(2,1)S(1)} collective-permute-done((bf16[1,32,4,8,128]{4,3,2,1,0:T(8,128)(2,1)}, bf16[1,32,4,8,128]{4,3,2,1,0:T(8,128)(2,1)S(1)}, u32[]{:S(2)}, u32[]{:S(2)}) %collective-permute-start) | collective-permute-done | bytes 262176 | tf_op jit(solution)/shard_map/ppermute | solution.py:373
  26.6 0.1 copy.12.other
  26.7 0.9 %shift.1.v3 = bf16[10,96,1024]{2,1,0:T(8,128)(2,1)S(1)} custom-call(s32[2]{0:T(128)S(1)} %pad_add_fusion.pos, bf16[4,32,1024]{2,1,0:T(8,128)(2,1)S(1)} %copy.11.own, bf16[4,32,1024]{2,1,0:T(8,128)(2,1)S(1)} %copy.12.other), custom_call_target="tpu_custom_call" | custom-call | flops 600000 | bytes 2500000 | tf_op jit(solution)/shard_map/shift/pallas_call | solution.py:119
  27.6 11.2 %fused.1 = (bf16[64,128]{1,0:T(8,128)(2,1)}, bf16[8,144,128]{2,1,0:T(8,128)(2,1)S(1)}, bf16[8,144,128]{2,1,0:T(8,128)(2,1)S(1)}, bf16[10,64,1280]{2,1,0:T(8,128)(2,1)S(1)}, bf16[864,64]{1,0:T(8,128)(2,1)S(1)}) custom-call(s32[2]{0:T(128)S(1)} %pad_add_fusion.pos, bf16[10,96,1024]{2,1,0:T(8,128)(2,1)S(1)} %shift.1.v3, bf16[64,128]{1,0:T(8,128)(2,1)S(1)} %bitcast.51, ...), custom_call_target="tpu_custom_call" | custom-call | flops 4000000000 | bytes 6000000 | tf_op jit(solution)/shard_map/fused/pallas_call | solution.py:307
  38.8 1.6 %collective-permute-done.7 = bf16[8,144,128]{2,1,0:T(8,128)(2,1)S(1)} collective-permute-done((bf16[8,144,128]{2,1,0:T(8,128)(2,1)S(1)}, bf16[8,144,128]{2,1,0:T(8,128)(2,1)S(1)}, u32[]{:S(2)}, u32[]{:S(2)}) %collective-permute-start.7) | collective-permute-done | bytes 294944 | tf_op jit(solution)/shard_map/ppermute | solution.py:361
  40.4 0.1 add_convert_fusion
  40.5 1.6 %collective-permute-start.8 = (bf16[4,144,128]{2,1,0:T(8,128)(2,1)S(1)}, bf16[4,144,128]{2,1,0:T(8,128)(2,1)S(1)}, u32[]{:S(2)}, u32[]{:S(2)}) collective-permute-start(bf16[4,144,128]{2,1,0:T(8,128)(2,1)S(1)} %slice.21), channel_id=1, source_target_pairs={{0,4},{2,6},{4,0},{6,2},{8,12},{10,14},{12,8},{14,10},{16,20},{18,... | collective-permute-start | bytes 442376 | tf_op jit(solution)/shard_map/ppermute | solution.py:361
  42.1 1.7 %volume.1 = bf16[4,32,1024]{2,1,0:T(8,128)(2,1)S(1)} custom-call(s32[2]{0:T(128)S(1)} %pad_add_fusion.pos, bf16[10,64,1280]{2,1,0:T(8,128)(2,1)S(1)} %get-tuple-element.12.dp, bf16[864,64]{1,0:T(8,128)(2,1)S(1)} %get-tuple-element.13.w1), custom_call_target="tpu_custom_call" | custom-call | flops 1000000000 | bytes 3000000 | tf_op jit(solution)/shard_map/volume/pallas_call | solution.py:337
  43.9 2.6 %collective-permute-done.8 = bf16[4,144,128]{2,1,0:T(8,128)(2,1)S(1)} collective-permute-done((bf16[4,144,128]{2,1,0:T(8,128)(2,1)S(1)}, bf16[4,144,128]{2,1,0:T(8,128)(2,1)S(1)}, u32[]{:S(2)}, u32[]{:S(2)}) %collective-permute-start.8) | collective-permute-done | bytes 147488 | tf_op jit(solution)/shard_map/ppermute | solution.py:361
  46.5 1.5 %collective-permute-start.11 = (bf16[144,128]{1,0:T(8,128)(2,1)S(1)}, bf16[144,128]{1,0:T(8,128)(2,1)S(1)}, u32[]{:S(2)}, u32[]{:S(2)}) collective-permute-start(bf16[144,128]{1,0:T(8,128)(2,1)S(1)} %get-tuple-element.18), channel_id=1, source_target_pairs={{0,24},{2,26},{4,28},{6,30},{8,16},{10,18},{12,20},{14,22},{16,8},... | collective-permute-start | bytes 110600 | tf_op jit(solution)/shard_map/ppermute | solution.py:361
  48.0 0.6 %collective-permute-start.10 = (bf16[144,128]{1,0:T(8,128)(2,1)S(1)}, bf16[144,128]{1,0:T(8,128)(2,1)S(1)}, u32[]{:S(2)}, u32[]{:S(2)}) collective-permute-start(bf16[144,128]{1,0:T(8,128)(2,1)S(1)} %get-tuple-element.19), channel_id=1, source_target_pairs={{0,16},{2,18},{4,20},{6,22},{8,24},{10,26},{12,28},{14,30},{16,0},... | collective-permute-start | bytes 110600 | tf_op jit(solution)/shard_map/ppermute | solution.py:361
  48.7 2.3 %collective-permute-start.9 = (bf16[144,128]{1,0:T(8,128)(2,1)S(1)}, bf16[144,128]{1,0:T(8,128)(2,1)S(1)}, u32[]{:S(2)}, u32[]{:S(2)}) collective-permute-start(bf16[144,128]{1,0:T(8,128)(2,1)S(1)} %get-tuple-element.20), channel_id=1, source_target_pairs={{0,8},{2,10},{4,12},{6,14},{8,0},{10,2},{12,4},{14,6},{16,24},{18,... | collective-permute-start | bytes 110600 | tf_op jit(solution)/shard_map/ppermute | solution.py:361
  51.0 0.7 %copy_bitcast_fusion = bf16[1,32,4,8,128]{4,3,2,1,0:T(8,128)(2,1)} fusion(bf16[4,32,8,128]{3,2,1,0:T(8,128)(2,1)S(1)} %bitcast.52), kind=kLoop, calls=%fused_computation.2 | loop fusion | bytes 524288 | tf_op jit(solution)/shard_map/broadcast_in_dim | solution.py:395
  51.7 0.8 %collective-permute-done.11.three = bf16[144,128]{1,0:T(8,128)(2,1)S(1)} collective-permute-done((bf16[144,128]{1,0:T(8,128)(2,1)S(1)}, bf16[144,128]{1,0:T(8,128)(2,1)S(1)}, u32[]{:S(2)}, u32[]{:S(2)}) %collective-permute-start.11) | collective-permute-done | bytes 36896 | tf_op jit(solution)/shard_map/ppermute | solution.py:361
  52.5 0.4 collective-permute-done.10.two
  52.9 0.4 collective-permute-done.9.one
  53.3 0.7 %finish.1 = (f32[54,64]{1,0:T(8,128)}, f32[108,128]{1,0:T(8,128)}) custom-call(bf16[4,144,128]{2,1,0:T(8,128)(2,1)S(1)} %add_convert_fusion.1.kept, bf16[144,128]{1,0:T(8,128)(2,1)S(1)} %collective-permute-done.9.one, bf16[144,128]{1,0:T(8,128)(2,1)S(1)} %collective-permute-done.10.two, bf16[144,128]{1,0:T(8,128)(2,1)S(1)} %collective-permute-done.11.three), custom_call_target="tpu_custom_call" | custom-call | flops 80000 | bytes 300000 | tf_op jit(solution)/shard_map/finish/pallas_call | solution.py:89
  (20 shorter events, 0.3 us)
Async XLA Ops:
  0.6 0.7 %copy-start = (bf16[108,128]{1,0:T(8,128)(2,1)S(1)}, bf16[108,128]{1,0:T(8,128)(2,1)}, u32[]{:S(2)}) copy-start(bf16[108,128]{1,0:T(8,128)(2,1)} %second.1) | copy-start | bytes 82948
  1.4 0.7 %copy-start.1 = (bf16[54,64]{1,0:T(8,128)(2,1)S(1)}, bf16[54,64]{1,0:T(8,128)(2,1)}, u32[]{:S(2)}) copy-start(bf16[54,64]{1,0:T(8,128)(2,1)} %first.1) | copy-start | bytes 20740
  2.2 7.0 %collective-permute-start.4 = (bf16[144,128]{1,0:T(8,128)(2,1)S(1)}, bf16[144,128]{1,0:T(8,128)(2,1)S(1)}, u32[]{:S(2)}, u32[]{:S(2)}) collective-permute-start(bf16[144,128]{1,0:T(8,128)(2,1)S(1)} %pack.1), channel_id=1, source_target_pairs={{0,24},{2,26},{4,28},{6,30},{8,16},{10,18},{12,20},{14,22},{16,8},... | collective-permute-start | bytes 110600 | tf_op jit(solution)/shard_map/ppermute | solution.py:361
  7.3 4.9 %collective-permute-start.3 = (bf16[144,128]{1,0:T(8,128)(2,1)S(1)}, bf16[144,128]{1,0:T(8,128)(2,1)S(1)}, u32[]{:S(2)}, u32[]{:S(2)}) collective-permute-start(bf16[144,128]{1,0:T(8,128)(2,1)S(1)} %pack.1), channel_id=1, source_target_pairs={{0,16},{2,18},{4,20},{6,22},{8,24},{10,26},{12,28},{14,30},{16,0},... | collective-permute-start | bytes 110600 | tf_op jit(solution)/shard_map/ppermute | solution.py:361
  7.3 4.9 %collective-permute-start.2 = (bf16[144,128]{1,0:T(8,128)(2,1)S(1)}, bf16[144,128]{1,0:T(8,128)(2,1)S(1)}, u32[]{:S(2)}, u32[]{:S(2)}) collective-permute-start(bf16[144,128]{1,0:T(8,128)(2,1)S(1)} %pack.1), channel_id=1, source_target_pairs={{0,8},{2,10},{4,12},{6,14},{8,0},{10,2},{12,4},{14,6},{16,24},{18,... | collective-permute-start | bytes 110600 | tf_op jit(solution)/shard_map/ppermute | solution.py:361
  12.1 5.2 %collective-permute-start.5 = (bf16[4,144,128]{2,1,0:T(8,128)(2,1)S(1)}, bf16[4,144,128]{2,1,0:T(8,128)(2,1)S(1)}, u32[]{:S(2)}, u32[]{:S(2)}) collective-permute-start(bf16[4,144,128]{2,1,0:T(8,128)(2,1)S(1)} %pad_maximum_fusion), channel_id=1, source_target_pairs={{0,4},{2,6},{4,0},{6,2},{8,12},{10,14},{12,8},{14,10},{16,20},{18,... | collective-permute-start | bytes 442376 | tf_op jit(solution)/shard_map/ppermute | solution.py:361
  17.4 10.2 %collective-permute-start.6 = (bf16[8,144,128]{2,1,0:T(8,128)(2,1)S(1)}, bf16[8,144,128]{2,1,0:T(8,128)(2,1)S(1)}, u32[]{:S(2)}, u32[]{:S(2)}) collective-permute-start(bf16[8,144,128]{2,1,0:T(8,128)(2,1)S(1)} %constant_dynamic-update-slice_fusion.near), channel_id=1, source_target_pairs={{0,2},{2,0},{4,6},{6,4},{8,10},{10,8},{12,14},{14,12},{16,18},{18,... | collective-permute-start | bytes 884744 | tf_op jit(solution)/shard_map/ppermute | solution.py:361
  17.5 9.1 %collective-permute-start = (bf16[1,32,4,8,128]{4,3,2,1,0:T(8,128)(2,1)}, bf16[1,32,4,8,128]{4,3,2,1,0:T(8,128)(2,1)S(1)}, u32[]{:S(2)}, u32[]{:S(2)}) collective-permute-start(bf16[1,32,4,8,128]{4,3,2,1,0:T(8,128)(2,1)} %param.4), channel_id=1, source_target_pairs={{0,1},{1,0},{2,3},{3,2},{4,5},{5,4},{6,7},{7,6},{8,9},{9,8},{10,11... | collective-permute-start | bytes 786440 | tf_op jit(solution)/shard_map/ppermute | solution.py:373
  19.0 8.6 %collective-permute-start.1 = (bf16[64,128]{1,0:T(8,128)(2,1)}, bf16[64,128]{1,0:T(8,128)(2,1)S(1)}, u32[]{:S(2)}, u32[]{:S(2)}) collective-permute-start(bf16[64,128]{1,0:T(8,128)(2,1)} %bitcast.50), channel_id=1, source_target_pairs={{0,1},{1,0},{2,3},{3,2},{4,5},{5,4},{6,7},{7,6},{8,9},{9,8},{10,11... | collective-permute-start | bytes 49160 | tf_op jit(solution)/shard_map/ppermute | solution.py:375
  20.6 7.0 %copy-start.2 = (bf16[1,128,1,2,32]{1,4,3,2,0:T(8,128)(2,1)S(1)}, bf16[1,128,1,2,32]{1,4,3,2,0:T(8,128)(2,1)}, u32[]{:S(2)}) copy-start(bf16[1,128,1,2,32]{1,4,3,2,0:T(8,128)(2,1)} %param.7) | copy-start | bytes 49156
  38.8 1.6 %collective-permute-start.7 = (bf16[8,144,128]{2,1,0:T(8,128)(2,1)S(1)}, bf16[8,144,128]{2,1,0:T(8,128)(2,1)S(1)}, u32[]{:S(2)}, u32[]{:S(2)}) collective-permute-start(bf16[8,144,128]{2,1,0:T(8,128)(2,1)S(1)} %get-tuple-element.15), channel_id=1, source_target_pairs={{0,2},{2,0},{4,6},{6,4},{8,10},{10,8},{12,14},{14,12},{16,18},{18,... | collective-permute-start | bytes 884744 | tf_op jit(solution)/shard_map/ppermute | solution.py:361
  40.5 6.0 %collective-permute-start.8 = (bf16[4,144,128]{2,1,0:T(8,128)(2,1)S(1)}, bf16[4,144,128]{2,1,0:T(8,128)(2,1)S(1)}, u32[]{:S(2)}, u32[]{:S(2)}) collective-permute-start(bf16[4,144,128]{2,1,0:T(8,128)(2,1)S(1)} %slice.21), channel_id=1, source_target_pairs={{0,4},{2,6},{4,0},{6,2},{8,12},{10,14},{12,8},{14,10},{16,20},{18,... | collective-permute-start | bytes 442376 | tf_op jit(solution)/shard_map/ppermute | solution.py:361
  46.5 6.0 %collective-permute-start.11 = (bf16[144,128]{1,0:T(8,128)(2,1)S(1)}, bf16[144,128]{1,0:T(8,128)(2,1)S(1)}, u32[]{:S(2)}, u32[]{:S(2)}) collective-permute-start(bf16[144,128]{1,0:T(8,128)(2,1)S(1)} %get-tuple-element.18), channel_id=1, source_target_pairs={{0,24},{2,26},{4,28},{6,30},{8,16},{10,18},{12,20},{14,22},{16,8},... | collective-permute-start | bytes 110600 | tf_op jit(solution)/shard_map/ppermute | solution.py:361
  48.0 4.9 %collective-permute-start.10 = (bf16[144,128]{1,0:T(8,128)(2,1)S(1)}, bf16[144,128]{1,0:T(8,128)(2,1)S(1)}, u32[]{:S(2)}, u32[]{:S(2)}) collective-permute-start(bf16[144,128]{1,0:T(8,128)(2,1)S(1)} %get-tuple-element.19), channel_id=1, source_target_pairs={{0,16},{2,18},{4,20},{6,22},{8,24},{10,26},{12,28},{14,30},{16,0},... | collective-permute-start | bytes 110600 | tf_op jit(solution)/shard_map/ppermute | solution.py:361
  48.7 4.6 %collective-permute-start.9 = (bf16[144,128]{1,0:T(8,128)(2,1)S(1)}, bf16[144,128]{1,0:T(8,128)(2,1)S(1)}, u32[]{:S(2)}, u32[]{:S(2)}) collective-permute-start(bf16[144,128]{1,0:T(8,128)(2,1)S(1)} %get-tuple-element.20), channel_id=1, source_target_pairs={{0,8},{2,10},{4,12},{6,14},{8,0},{10,2},{12,4},{14,6},{16,24},{18,... | collective-permute-start | bytes 110600 | tf_op jit(solution)/shard_map/ppermute | solution.py:361

commit v3 on v2

--- a/solution.py
+++ b/solution.py
@@ -54,12 +54,20 @@
     return jnp.where(inside, pltpu.roll(x, (-(db * 64 + dc)) % 256, 1), 0.0)
 
 
-def pack_kernel(first, second, out, wide, narrow):
+def pack_kernel(first, second, out, wide, narrow, first_here, second_here, sems):
+    copies = (
+        pltpu.make_async_copy(first, first_here, sems.at[0]),
+        pltpu.make_async_copy(second, second_here, sems.at[1]),
+    )
+    for copy in copies:
+        copy.start()
     wide[...] = jnp.zeros(wide.shape, F32)
-    wide[0:108, :] = second[...].astype(F32)
-    narrow[...] = first[...].astype(F32)
-    wide[112:139, 0:64] = narrow[0:27, :]
-    wide[112:139, 64:128] = narrow[27:54, :]
+    for copy in copies:
+        copy.wait()
+    wide[0:108, :] = second_here[...].astype(F32)
+    narrow[...] = first_here[...].astype(F32)
+    wide[112:140, 0:64] = narrow[0:28, :]
+    wide[112:138, 64:128] = narrow[28:54, :]
     out[...] = wide[...].astype(BF)
 
 
@@ -67,9 +75,15 @@
     return pl.pallas_call(
         pack_kernel,
         out_shape=jax.ShapeDtypeStruct((144, 128), BF),
-        in_specs=[VMEM] * 2,
+        in_specs=[pl.BlockSpec(memory_space=pltpu.HBM)] * 2,
         out_specs=VMEM,
-        scratch_shapes=[pltpu.VMEM((144, 128), F32), pltpu.VMEM((54, 64), F32)],
+        scratch_shapes=[
+            pltpu.VMEM((144, 128), F32),
+            pltpu.VMEM((54, 64), F32),
+            pltpu.VMEM((54, 64), BF),
+            pltpu.VMEM((108, 128), BF),
+            pltpu.SemaphoreType.DMA((2,)),
+        ],
         compiler_params=pltpu.CompilerParams(vmem_limit_bytes=2 << 20),
         cost_estimate=pl.CostEstimate(flops=40_000, bytes_accessed=80_000, transcendentals=0),
         name="pack",
@@ -81,8 +95,8 @@
         kept[0].astype(F32) + one[...].astype(F32) + two[...].astype(F32) + three[...].astype(F32)
     )
     second[...] = total[0:108, :]
-    first[0:27, :] = total[112:139, 0:64]
-    first[27:54, :] = total[112:139, 64:128]
+    first[0:28, :] = total[112:140, 0:64]
+    first[28:54, :] = total[112:138, 64:128]
 
 
 def finish_call(kept, pieces):
@@ -127,38 +141,32 @@
     )(pos, own, other)
 
 
-def unpack_weights(me, near, far, w1f, w2f):
-    for parity in range(2):
-
-        @pl.when(me % 2 == parity)
-        def _():
-            for d in range(16):
-                k = jnp.bitwise_xor(me, d)
-                ref = near if d % 2 == parity else far
-                blk = ref[(k // 2) % 2 * 4 + k // 4].astype(F32)
-                w2f[108 * d : 108 * d + 108, :] = blk[0:108]
-                w1f[54 * d : 54 * d + 27, :] = blk[112:139, 0:64]
-                w1f[54 * d + 27 : 54 * d + 54, :] = blk[112:139, 64:128]
+def unpack_weights(me, near, far, w1s, w2s):
+    for d in range(16):
+        k = jnp.bitwise_xor(me, d)
+        place = (k // 2) % 2 * 4 + k // 4
+        blk = lax.select(k % 2 == 0, near[place], far[place])
+        w2s[108 * d : 108 * d + 108, :] = blk[0:108]
+        w1s[54 * d : 54 * d + 28, :] = blk[112:140, 0:64]
+        w1s[54 * d + 28 : 54 * d + 54, :] = blk[112:138, 64:128]
 
 
 def fused_kernel(
     factor_one, factor_two,
     pos, v3, co, cx, near, far,
-    pooled_out, keep_out, send_out, dp, w1_out,
-    w1f, w2f, w2s, slope, fpl, fs, d2p, t2, g2f, g1w,
+    pooled_out, wire_out, dp, w1_out,
+    w2s, slope, fpl, fs, d2p, t2, g2s, g1s, acc1,
 ):
     me, s = pos[0], pos[1]
-    unpack_weights(me, near, far, w1f, w2f)
-    w1_out[...] = w1f[...].astype(BF)
-    w2s[...] = w2f[...].astype(BF)
+    unpack_weights(me, near, far, w1_out, w2s)
     id64, id128 = eye(64), eye(128)
     lhs1 = jnp.concatenate(
         [
             dot_nt(
                 id64,
                 jnp.concatenate(
-                    [w1f[(a * 3 + b) * 96 : (a * 3 + b) * 96 + 96, :] for a in range(3)], axis=0
-                ).astype(BF),
+                    [w1_out[(a * 3 + b) * 96 : (a * 3 + b) * 96 + 96, :] for a in range(3)], axis=0
+                ),
             ).astype(BF)
             for b in range(3)
         ],
@@ -221,13 +229,14 @@
     pooled_out[...] = ((dot_nt(pool2, hi) + dot_nt(pool2, lo)) * 0.125).astype(BF)
 
     lhs = jnp.concatenate([fs[p] for p in range(1, 5)], axis=1)
-    rhs = jnp.concatenate(
-        [jnp.concatenate([d2p[p + 1 - a] for p in range(1, 5)], axis=1) for a in range(3)], axis=0
-    )
-    prod = dot_nt(lhs, rhs) * factor_two
-    for a in range(3):
-        g2f[a * 576 : a * 576 + 576, :] = prod[:, a * 128 : a * 128 + 128]
-    g2f[1728:1736, :] = jnp.zeros((8, 128), F32)
+    for some in ((0, 1), (2,)):
+        rhs = jnp.concatenate(
+            [jnp.concatenate([d2p[p + 1 - a] for p in range(1, 5)], axis=1) for a in some], axis=0
+        )
+        prod = dot_nt(lhs, rhs) * factor_two
+        for n, a in enumerate(some):
+            g2s[a * 576 : a * 576 + 576, :] = prod[:, n * 128 : n * 128 + 128].astype(BF)
+    g2s[1728:1744, :] = jnp.zeros((16, 128), BF)
 
     spread1 = where_one(iota((128, 256), 0) == iota((128, 256), 1) // 2)
     dp[0] = jnp.zeros((64, 1280), BF)
@@ -236,9 +245,12 @@
         dp[x + 1, :, 0:128] = jnp.zeros((64, 128), BF)
         dp[x + 1, :, 1152:1280] = jnp.zeros((64, 128), BF)
     back = jnp.concatenate([w2s[a * 576 : a * 576 + 576, :] for a in range(3)], axis=1)
+    rhs = jnp.concatenate(
+        [jnp.concatenate([d2p[x2 + 2 - a] for x2 in range(4)], axis=1) for a in range(3)], axis=0
+    )
+    spread_all = dot(back, rhs)
     for x2 in range(4):
-        rhs = jnp.concatenate([d2p[x2 + 2], d2p[x2 + 1], d2p[x2]], axis=0)
-        prod = dot(back, rhs)
+        prod = spread_all[:, x2 * 256 : x2 * 256 + 256]
         grad = prod[256:320]
         for bc in range(9):
             if bc != 4:
@@ -254,30 +266,32 @@
                         part * slope[2 * x2 + dx, :, at : at + 128]
                     ).astype(BF)
 
-    prod = jnp.zeros((288, 192), F32)
-    for x in range(8):
-        rhs = jnp.concatenate([dp[x + 1, :, (2 - b) * 128 : (2 - b) * 128 + 1024] for b in range(3)], axis=0)
-        prod = prod + dot_nt(cols_of(x), rhs)
-    prod = prod * factor_one
-    g1w[0:32, :] = jnp.zeros((32, 128), F32)
-    g1w[896:904, :] = jnp.zeros((8, 128), F32)
-    g1w[864:896, :] = jnp.zeros((32, 128), F32)
+    acc1[...] = jnp.zeros(acc1.shape, F32)
+
+    def first_grads(i, carry):
+        for n in range(4):
+            x = 4 * i + n
+            rhs = jnp.concatenate(
+                [dp[x + 1, :, (2 - b) * 128 : (2 - b) * 128 + 1024] for b in range(3)], axis=0
+            )
+            acc1[n % 2] += dot_nt(cols_of(x), rhs)
+        return carry
+
+    lax.fori_loop(0, 2, first_grads, 0)
+    prod = (acc1[0] + acc1[1]) * factor_one
+    g1s[0:32, :] = jnp.zeros((32, 128), BF)
+    g1s[864:912, :] = jnp.zeros((48, 128), BF)
     for a in range(3):
         for b in range(3):
-            block = prod[a * 96 : a * 96 + 96, b * 64 : b * 64 + 64]
+            block = prod[a * 96 : a * 96 + 96, b * 64 : b * 64 + 64].astype(BF)
             row = (a * 3 + b) * 96 + 32
-            g1w[row : row + 96, 0:64] = block
-            g1w[row - 27 : row + 69, 64:128] = block
-    for parity in range(2):
-
-        @pl.when(me % 2 == parity)
-        def _():
-            for d in range(16):
-                k = jnp.bitwise_xor(me, d)
-                ref = keep_out if d % 2 == parity else send_out
-                place = (k // 2) % 2 * 4 + k // 4
-                ref[place, 0:112, :] = g2f[108 * d : 108 * d + 112, :].astype(BF)
-                ref[place, 112:144, :] = g1w[54 * d + 32 : 54 * d + 64, :].astype(BF)
+            g1s[row : row + 96, 0:64] = block
+            g1s[row - 28 : row + 68, 64:128] = block
+    for d in range(16):
+        k = jnp.bitwise_xor(me, d)
+        place = k % 2 * 8 + (k // 2) % 2 * 4 + k // 4
+        wire_out[place, 0:112, :] = g2s[108 * d : 108 * d + 112, :]
+        wire_out[place, 112:144, :] = g1s[54 * d + 32 : 54 * d + 64, :]
 
 
 def volume_kernel(pos, dp, w1, out, wd):
@@ -308,24 +322,22 @@
         functools.partial(fused_kernel, factor_one, factor_two),
         out_shape=(
             jax.ShapeDtypeStruct((64, 128), BF),
-            jax.ShapeDtypeStruct((8, 144, 128), BF),
-            jax.ShapeDtypeStruct((8, 144, 128), BF),
+            jax.ShapeDtypeStruct((16, 144, 128), BF),
             jax.ShapeDtypeStruct((10, 64, 1280), BF),
             jax.ShapeDtypeStruct((864, 64), BF),
         ),
         in_specs=[SMEM] + [VMEM] * 5,
-        out_specs=(VMEM,) * 5,
+        out_specs=(VMEM,) * 4,
         scratch_shapes=[
-            pltpu.VMEM((864, 64), F32),
-            pltpu.VMEM((1728, 128), F32),
             pltpu.VMEM((1728, 128), BF),
             pltpu.VMEM((8, 64, 1024), F32),
             pltpu.VMEM((4, 64, 256), F32),
             pltpu.VMEM((6, 576, 256), BF),
             pltpu.VMEM((6, 128, 256), BF),
             pltpu.VMEM((2, 128, 256), F32),
-            pltpu.VMEM((1736, 128), F32),
-            pltpu.VMEM((904, 128), F32),
+            pltpu.VMEM((1744, 128), BF),
+            pltpu.VMEM((912, 128), BF),
+            pltpu.VMEM((2, 288, 192), F32),
         ],
         compiler_params=pltpu.CompilerParams(vmem_limit_bytes=48 << 20),
         cost_estimate=pl.CostEstimate(flops=4_000_000_000, bytes_accessed=6_000_000, transcendentals=700_000),
@@ -382,11 +394,11 @@
     own = plane_major(volumes)
     other = plane_major(volumes_other)
     moved = shift_call(pos, own, other)
-    pooled, keep, send, delta, w_one = fused_call(
+    pooled, wire, delta, w_one = fused_call(
         factor_one, factor_two, pos, moved, cot, cot_other, along_y, across
     )
-    got = swap(send, 1)
-    part = (keep.astype(F32) + got.astype(F32)).astype(BF)
+    got = swap(wire[8:], 1)
+    part = (wire[:8].astype(F32) + got.astype(F32)).astype(BF)
     got = swap(part[4:], 2)
     part = (part[:4].astype(F32) + got.astype(F32)).astype(BF)
     pieces = [swap(part[k], 4 * k) for k in range(1, 4)]

time: 54.3 us -> 51.9 us (0.956)
  Pallas kernels: 14.6 us -> 12 us
    pallas_call x1, Pallas kernels: 11.2 us -> 8.58 us  [fused_call(): pl.pallas_call(functools.partial(fused_kernel, factor_one, factor_two), o...]
where the time goes in v3:
time: 51.9 us; the launch traced here: 51.6 us
  waiting for transfers between devices  19.4 us (37%)
  starting transfers between devices  15.6 us (30%)
  Pallas kernels  12 us (23%)
  local copies, waits for them, and re-layouts  3.59 us (7%)
  between operations  0.79 us (2%)
    ppermute x10, waiting for transfers between devices, swap(): return lax.ppermute(x, 'dp', [(i, i ^ bit) for i in range(16)])  13.5 us
    ppermute x10, starting transfers between devices, swap(): return lax.ppermute(x, 'dp', [(i, i ^ bit) for i in range(16)])  13.5 us
    pallas_call x1, Pallas kernels, fused_call(): pl.pallas_call(functools.partial(fused_kernel, factor_one, factor_two), o...  8.58 us
    ppermute x1, waiting for transfers between devices, paired(): volumes_other = lax.ppermute(volumes, 'space', across_space)  5.81 us
    pallas_call x1, Pallas kernels, volume_call(): pl.pallas_call(volume_kernel, out_shape=jax.ShapeDtypeStruct((4, 32, 1024...  1.72 us
    ppermute x1, starting transfers between devices, paired(): volumes_other = lax.ppermute(volumes, 'space', across_space)  1.56 us
    unnamed x11, local copies, waits for them, and re-layouts  1.54 us
    reshape x4, local copies, waits for them, and re-layouts, plane_major(): return jnp.transpose(block[0], (1, 0, 2, 3)).reshape(4, 32, 1024)  1.24 us
  transfers between devices with their start and end apart: 12, of which 9 were waited for; matrix products, arithmetic and copies ran while one was open for 4% of the time, Pallas kernels for 5%

profile of v3, /device:TPU:0, one launch (start us, length us, event | category | flops | bytes accessed | tf_op | source)
XLA Modules:
  0.0 51.6 jit_solution(569722206130701292)
XLA Ops:
  0.6 0.7 %copy-done = bf16[108,128]{1,0:T(8,128)(2,1)S(1)} copy-done((bf16[108,128]{1,0:T(8,128)(2,1)S(1)}, bf16[108,128]{1,0:T(8,128)(2,1)}, u32[]{:S(2)}) %copy-start) | copy-done | bytes 27672
  1.4 0.7 %copy-done.1 = bf16[54,64]{1,0:T(8,128)(2,1)S(1)} copy-done((bf16[54,64]{1,0:T(8,128)(2,1)S(1)}, bf16[54,64]{1,0:T(8,128)(2,1)}, u32[]{:S(2)}) %copy-start.1) | copy-done | bytes 6936
  2.1 0.1 pack.1
  2.2 5.1 %collective-permute-start.4 = (bf16[144,128]{1,0:T(8,128)(2,1)S(1)}, bf16[144,128]{1,0:T(8,128)(2,1)S(1)}, u32[]{:S(2)}, u32[]{:S(2)}) collective-permute-start(bf16[144,128]{1,0:T(8,128)(2,1)S(1)} %pack.1), channel_id=1, source_target_pairs={{0,24},{2,26},{4,28},{6,30},{8,16},{10,18},{12,20},{14,22},{16,8},... | collective-permute-start | bytes 110600 | tf_op jit(solution)/shard_map/ppermute | solution.py:373
  7.4 0.6 %collective-permute-start.2 = (bf16[144,128]{1,0:T(8,128)(2,1)S(1)}, bf16[144,128]{1,0:T(8,128)(2,1)S(1)}, u32[]{:S(2)}, u32[]{:S(2)}) collective-permute-start(bf16[144,128]{1,0:T(8,128)(2,1)S(1)} %pack.1), channel_id=1, source_target_pairs={{0,8},{2,10},{4,12},{6,14},{8,0},{10,2},{12,4},{14,6},{16,24},{18,... | collective-permute-start | bytes 110600 | tf_op jit(solution)/shard_map/ppermute | solution.py:373
  8.0 1.3 %collective-permute-done.4 = bf16[144,128]{1,0:T(8,128)(2,1)S(1)} collective-permute-done((bf16[144,128]{1,0:T(8,128)(2,1)S(1)}, bf16[144,128]{1,0:T(8,128)(2,1)S(1)}, u32[]{:S(2)}, u32[]{:S(2)}) %collective-permute-start.4) | collective-permute-done | bytes 36896 | tf_op jit(solution)/shard_map/ppermute | solution.py:373
  9.3 2.9 %collective-permute-done.3 = bf16[144,128]{1,0:T(8,128)(2,1)S(1)} collective-permute-done((bf16[144,128]{1,0:T(8,128)(2,1)S(1)}, bf16[144,128]{1,0:T(8,128)(2,1)S(1)}, u32[]{:S(2)}, u32[]{:S(2)}) %collective-permute-start.3) | collective-permute-done | bytes 36896 | tf_op jit(solution)/shard_map/ppermute | solution.py:373
  12.3 1.6 %collective-permute-start.5 = (bf16[4,144,128]{2,1,0:T(8,128)(2,1)S(1)}, bf16[4,144,128]{2,1,0:T(8,128)(2,1)S(1)}, u32[]{:S(2)}, u32[]{:S(2)}) collective-permute-start(bf16[4,144,128]{2,1,0:T(8,128)(2,1)S(1)} %pad_maximum_fusion), channel_id=1, source_target_pairs={{0,4},{2,6},{4,0},{6,2},{8,12},{10,14},{12,8},{14,10},{16,20},{18,... | collective-permute-start | bytes 442376 | tf_op jit(solution)/shard_map/ppermute | solution.py:373
  13.9 3.6 %collective-permute-done.5 = bf16[4,144,128]{2,1,0:T(8,128)(2,1)S(1)} collective-permute-done((bf16[4,144,128]{2,1,0:T(8,128)(2,1)S(1)}, bf16[4,144,128]{2,1,0:T(8,128)(2,1)S(1)}, u32[]{:S(2)}, u32[]{:S(2)}) %collective-permute-start.5) | collective-permute-done | bytes 147488 | tf_op jit(solution)/shard_map/ppermute | solution.py:373
  17.5 0.1 collective-permute-start.6
  17.6 1.6 %collective-permute-start = (bf16[1,32,4,8,128]{4,3,2,1,0:T(8,128)(2,1)}, bf16[1,32,4,8,128]{4,3,2,1,0:T(8,128)(2,1)S(1)}, u32[]{:S(2)}, u32[]{:S(2)}) collective-permute-start(bf16[1,32,4,8,128]{4,3,2,1,0:T(8,128)(2,1)} %param.4), channel_id=1, source_target_pairs={{0,1},{1,0},{2,3},{3,2},{4,5},{5,4},{6,7},{7,6},{8,9},{9,8},{10,11... | collective-permute-start | bytes 786440 | tf_op jit(solution)/shard_map/ppermute | solution.py:385
  19.1 0.5 %collective-permute-start.1 = (bf16[64,128]{1,0:T(8,128)(2,1)}, bf16[64,128]{1,0:T(8,128)(2,1)S(1)}, u32[]{:S(2)}, u32[]{:S(2)}) collective-permute-start(bf16[64,128]{1,0:T(8,128)(2,1)} %bitcast.50), channel_id=1, source_target_pairs={{0,1},{1,0},{2,3},{3,2},{4,5},{5,4},{6,7},{7,6},{8,9},{9,8},{10,11... | collective-permute-start | bytes 49160 | tf_op jit(solution)/shard_map/ppermute | solution.py:387
  19.7 0.1 pad_add_fusion.pos
  19.7 1.0 %reshape.28 = bf16[4,32,1024]{2,0,1:T(4,128)(2,1)S(1)} reshape(bf16[4,32,8,128]{3,2,0,1:T(8,128)(2,1)} %bitcast.53) | data formatting | bytes 524288 | tf_op jit(solution)/shard_map/reshape | solution.py:377
  20.8 0.1 copy.11.own
  20.9 5.8 %collective-permute-done = bf16[1,32,4,8,128]{4,3,2,1,0:T(8,128)(2,1)S(1)} collective-permute-done((bf16[1,32,4,8,128]{4,3,2,1,0:T(8,128)(2,1)}, bf16[1,32,4,8,128]{4,3,2,1,0:T(8,128)(2,1)S(1)}, u32[]{:S(2)}, u32[]{:S(2)}) %collective-permute-start) | collective-permute-done | bytes 262176 | tf_op jit(solution)/shard_map/ppermute | solution.py:385
  26.7 0.1 copy.12.other
  26.8 0.9 %shift.1.v3 = bf16[10,96,1024]{2,1,0:T(8,128)(2,1)S(1)} custom-call(s32[2]{0:T(128)S(1)} %pad_add_fusion.pos, bf16[4,32,1024]{2,1,0:T(8,128)(2,1)S(1)} %copy.11.own, bf16[4,32,1024]{2,1,0:T(8,128)(2,1)S(1)} %copy.12.other), custom_call_target="tpu_custom_call" | custom-call | flops 600000 | bytes 2500000 | tf_op jit(solution)/shard_map/shift/pallas_call | solution.py:133
  27.8 8.6 %fused.1 = (bf16[64,128]{1,0:T(8,128)(2,1)}, bf16[16,144,128]{2,1,0:T(8,128)(2,1)S(1)}, bf16[10,64,1280]{2,1,0:T(8,128)(2,1)S(1)}, bf16[864,64]{1,0:T(8,128)(2,1)S(1)}) custom-call(s32[2]{0:T(128)S(1)} %pad_add_fusion.pos, bf16[10,96,1024]{2,1,0:T(8,128)(2,1)S(1)} %shift.1.v3, bf16[64,128]{1,0:T(8,128)(2,1)S(1)} %bitcast.51, ...), custom_call_target="tpu_custom_call" | custom-call | flops 4000000000 | bytes 6000000 | tf_op jit(solution)/shard_map/fused/pallas_call | solution.py:321
  36.4 1.6 %collective-permute-done.7 = bf16[8,144,128]{2,1,0:T(8,128)(2,1)S(1)} collective-permute-done((bf16[8,144,128]{2,1,0:T(8,128)(2,1)S(1)}, bf16[8,144,128]{2,1,0:T(8,128)(2,1)S(1)}, u32[]{:S(2)}, u32[]{:S(2)}) %collective-permute-start.7) | collective-permute-done | bytes 294944 | tf_op jit(solution)/shard_map/ppermute | solution.py:373
  38.0 0.1 add_convert_fusion
  38.1 1.6 %collective-permute-start.8 = (bf16[4,144,128]{2,1,0:T(8,128)(2,1)S(1)}, bf16[4,144,128]{2,1,0:T(8,128)(2,1)S(1)}, u32[]{:S(2)}, u32[]{:S(2)}) collective-permute-start(bf16[4,144,128]{2,1,0:T(8,128)(2,1)S(1)} %slice.29), channel_id=1, source_target_pairs={{0,4},{2,6},{4,0},{6,2},{8,12},{10,14},{12,8},{14,10},{16,20},{18,... | collective-permute-start | bytes 442376 | tf_op jit(solution)/shard_map/ppermute | solution.py:373
  39.7 1.7 %volume.1 = bf16[4,32,1024]{2,1,0:T(8,128)(2,1)S(1)} custom-call(s32[2]{0:T(128)S(1)} %pad_add_fusion.pos, bf16[10,64,1280]{2,1,0:T(8,128)(2,1)S(1)} %get-tuple-element.11.dp, bf16[864,64]{1,0:T(8,128)(2,1)S(1)} %get-tuple-element.12.w1), custom_call_target="tpu_custom_call" | custom-call | flops 1000000000 | bytes 3000000 | tf_op jit(solution)/shard_map/volume/pallas_call | solution.py:349
  41.5 2.6 %collective-permute-done.8 = bf16[4,144,128]{2,1,0:T(8,128)(2,1)S(1)} collective-permute-done((bf16[4,144,128]{2,1,0:T(8,128)(2,1)S(1)}, bf16[4,144,128]{2,1,0:T(8,128)(2,1)S(1)}, u32[]{:S(2)}, u32[]{:S(2)}) %collective-permute-start.8) | collective-permute-done | bytes 147488 | tf_op jit(solution)/shard_map/ppermute | solution.py:373
  44.1 1.5 %collective-permute-start.11 = (bf16[144,128]{1,0:T(8,128)(2,1)S(1)}, bf16[144,128]{1,0:T(8,128)(2,1)S(1)}, u32[]{:S(2)}, u32[]{:S(2)}) collective-permute-start(bf16[144,128]{1,0:T(8,128)(2,1)S(1)} %get-tuple-element.16), channel_id=1, source_target_pairs={{0,24},{2,26},{4,28},{6,30},{8,16},{10,18},{12,20},{14,22},{16,8},... | collective-permute-start | bytes 110600 | tf_op jit(solution)/shard_map/ppermute | solution.py:373
  45.7 0.6 %collective-permute-start.10 = (bf16[144,128]{1,0:T(8,128)(2,1)S(1)}, bf16[144,128]{1,0:T(8,128)(2,1)S(1)}, u32[]{:S(2)}, u32[]{:S(2)}) collective-permute-start(bf16[144,128]{1,0:T(8,128)(2,1)S(1)} %get-tuple-element.17), channel_id=1, source_target_pairs={{0,16},{2,18},{4,20},{6,22},{8,24},{10,26},{12,28},{14,30},{16,0},... | collective-permute-start | bytes 110600 | tf_op jit(solution)/shard_map/ppermute | solution.py:373
  46.3 2.3 %collective-permute-start.9 = (bf16[144,128]{1,0:T(8,128)(2,1)S(1)}, bf16[144,128]{1,0:T(8,128)(2,1)S(1)}, u32[]{:S(2)}, u32[]{:S(2)}) collective-permute-start(bf16[144,128]{1,0:T(8,128)(2,1)S(1)} %get-tuple-element.18), channel_id=1, source_target_pairs={{0,8},{2,10},{4,12},{6,14},{8,0},{10,2},{12,4},{14,6},{16,24},{18,... | collective-permute-start | bytes 110600 | tf_op jit(solution)/shard_map/ppermute | solution.py:373
  48.6 0.7 %copy_bitcast_fusion = bf16[1,32,4,8,128]{4,3,2,1,0:T(8,128)(2,1)} fusion(bf16[4,32,8,128]{3,2,1,0:T(8,128)(2,1)S(1)} %bitcast.52), kind=kLoop, calls=%fused_computation.2 | loop fusion | bytes 524288 | tf_op jit(solution)/shard_map/broadcast_in_dim | solution.py:407
  49.3 0.8 %collective-permute-done.11.three = bf16[144,128]{1,0:T(8,128)(2,1)S(1)} collective-permute-done((bf16[144,128]{1,0:T(8,128)(2,1)S(1)}, bf16[144,128]{1,0:T(8,128)(2,1)S(1)}, u32[]{:S(2)}, u32[]{:S(2)}) %collective-permute-start.11) | collective-permute-done | bytes 36896 | tf_op jit(solution)/shard_map/ppermute | solution.py:373
  50.1 0.4 collective-permute-done.10.two
  50.5 0.4 collective-permute-done.9.one
  50.9 0.7 %finish.1 = (f32[54,64]{1,0:T(8,128)}, f32[108,128]{1,0:T(8,128)}) custom-call(bf16[4,144,128]{2,1,0:T(8,128)(2,1)S(1)} %add_convert_fusion.1.kept, bf16[144,128]{1,0:T(8,128)(2,1)S(1)} %collective-permute-done.9.one, bf16[144,128]{1,0:T(8,128)(2,1)S(1)} %collective-permute-done.10.two, bf16[144,128]{1,0:T(8,128)(2,1)S(1)} %collective-permute-done.11.three), custom_call_target="tpu_custom_call" | custom-call | flops 80000 | bytes 300000 | tf_op jit(solution)/shard_map/finish/pallas_call | solution.py:103
  (21 shorter events, 0.4 us)
Async XLA Ops:
  0.6 0.7 %copy-start = (bf16[108,128]{1,0:T(8,128)(2,1)S(1)}, bf16[108,128]{1,0:T(8,128)(2,1)}, u32[]{:S(2)}) copy-start(bf16[108,128]{1,0:T(8,128)(2,1)} %second.1) | copy-start | bytes 82948
  1.4 0.7 %copy-start.1 = (bf16[54,64]{1,0:T(8,128)(2,1)S(1)}, bf16[54,64]{1,0:T(8,128)(2,1)}, u32[]{:S(2)}) copy-start(bf16[54,64]{1,0:T(8,128)(2,1)} %first.1) | copy-start | bytes 20740
  2.2 7.1 %collective-permute-start.4 = (bf16[144,128]{1,0:T(8,128)(2,1)S(1)}, bf16[144,128]{1,0:T(8,128)(2,1)S(1)}, u32[]{:S(2)}, u32[]{:S(2)}) collective-permute-start(bf16[144,128]{1,0:T(8,128)(2,1)S(1)} %pack.1), channel_id=1, source_target_pairs={{0,24},{2,26},{4,28},{6,30},{8,16},{10,18},{12,20},{14,22},{16,8},... | collective-permute-start | bytes 110600 | tf_op jit(solution)/shard_map/ppermute | solution.py:373
  7.4 4.9 %collective-permute-start.3 = (bf16[144,128]{1,0:T(8,128)(2,1)S(1)}, bf16[144,128]{1,0:T(8,128)(2,1)S(1)}, u32[]{:S(2)}, u32[]{:S(2)}) collective-permute-start(bf16[144,128]{1,0:T(8,128)(2,1)S(1)} %pack.1), channel_id=1, source_target_pairs={{0,16},{2,18},{4,20},{6,22},{8,24},{10,26},{12,28},{14,30},{16,0},... | collective-permute-start | bytes 110600 | tf_op jit(solution)/shard_map/ppermute | solution.py:373
  7.4 4.9 %collective-permute-start.2 = (bf16[144,128]{1,0:T(8,128)(2,1)S(1)}, bf16[144,128]{1,0:T(8,128)(2,1)S(1)}, u32[]{:S(2)}, u32[]{:S(2)}) collective-permute-start(bf16[144,128]{1,0:T(8,128)(2,1)S(1)} %pack.1), channel_id=1, source_target_pairs={{0,8},{2,10},{4,12},{6,14},{8,0},{10,2},{12,4},{14,6},{16,24},{18,... | collective-permute-start | bytes 110600 | tf_op jit(solution)/shard_map/ppermute | solution.py:373
  12.3 5.2 %collective-permute-start.5 = (bf16[4,144,128]{2,1,0:T(8,128)(2,1)S(1)}, bf16[4,144,128]{2,1,0:T(8,128)(2,1)S(1)}, u32[]{:S(2)}, u32[]{:S(2)}) collective-permute-start(bf16[4,144,128]{2,1,0:T(8,128)(2,1)S(1)} %pad_maximum_fusion), channel_id=1, source_target_pairs={{0,4},{2,6},{4,0},{6,2},{8,12},{10,14},{12,8},{14,10},{16,20},{18,... | collective-permute-start | bytes 442376 | tf_op jit(solution)/shard_map/ppermute | solution.py:373
  17.5 10.2 %collective-permute-start.6 = (bf16[8,144,128]{2,1,0:T(8,128)(2,1)S(1)}, bf16[8,144,128]{2,1,0:T(8,128)(2,1)S(1)}, u32[]{:S(2)}, u32[]{:S(2)}) collective-permute-start(bf16[8,144,128]{2,1,0:T(8,128)(2,1)S(1)} %constant_dynamic-update-slice_fusion.near), channel_id=1, source_target_pairs={{0,2},{2,0},{4,6},{6,4},{8,10},{10,8},{12,14},{14,12},{16,18},{18,... | collective-permute-start | bytes 884744 | tf_op jit(solution)/shard_map/ppermute | solution.py:373
  17.6 9.1 %collective-permute-start = (bf16[1,32,4,8,128]{4,3,2,1,0:T(8,128)(2,1)}, bf16[1,32,4,8,128]{4,3,2,1,0:T(8,128)(2,1)S(1)}, u32[]{:S(2)}, u32[]{:S(2)}) collective-permute-start(bf16[1,32,4,8,128]{4,3,2,1,0:T(8,128)(2,1)} %param.4), channel_id=1, source_target_pairs={{0,1},{1,0},{2,3},{3,2},{4,5},{5,4},{6,7},{7,6},{8,9},{9,8},{10,11... | collective-permute-start | bytes 786440 | tf_op jit(solution)/shard_map/ppermute | solution.py:385
  19.1 8.6 %collective-permute-start.1 = (bf16[64,128]{1,0:T(8,128)(2,1)}, bf16[64,128]{1,0:T(8,128)(2,1)S(1)}, u32[]{:S(2)}, u32[]{:S(2)}) collective-permute-start(bf16[64,128]{1,0:T(8,128)(2,1)} %bitcast.50), channel_id=1, source_target_pairs={{0,1},{1,0},{2,3},{3,2},{4,5},{5,4},{6,7},{7,6},{8,9},{9,8},{10,11... | collective-permute-start | bytes 49160 | tf_op jit(solution)/shard_map/ppermute | solution.py:387
  20.8 7.0 %copy-start.2 = (bf16[1,128,1,2,32]{1,4,3,2,0:T(8,128)(2,1)S(1)}, bf16[1,128,1,2,32]{1,4,3,2,0:T(8,128)(2,1)}, u32[]{:S(2)}) copy-start(bf16[1,128,1,2,32]{1,4,3,2,0:T(8,128)(2,1)} %param.7) | copy-start | bytes 49156
  36.4 1.6 %collective-permute-start.7 = (bf16[8,144,128]{2,1,0:T(8,128)(2,1)S(1)}, bf16[8,144,128]{2,1,0:T(8,128)(2,1)S(1)}, u32[]{:S(2)}, u32[]{:S(2)}) collective-permute-start(bf16[8,144,128]{2,1,0:T(8,128)(2,1)S(1)} %slice.22), channel_id=1, source_target_pairs={{0,2},{2,0},{4,6},{6,4},{8,10},{10,8},{12,14},{14,12},{16,18},{18,... | collective-permute-start | bytes 884744 | tf_op jit(solution)/shard_map/ppermute | solution.py:373
  38.1 6.0 %collective-permute-start.8 = (bf16[4,144,128]{2,1,0:T(8,128)(2,1)S(1)}, bf16[4,144,128]{2,1,0:T(8,128)(2,1)S(1)}, u32[]{:S(2)}, u32[]{:S(2)}) collective-permute-start(bf16[4,144,128]{2,1,0:T(8,128)(2,1)S(1)} %slice.29), channel_id=1, source_target_pairs={{0,4},{2,6},{4,0},{6,2},{8,12},{10,14},{12,8},{14,10},{16,20},{18,... | collective-permute-start | bytes 442376 | tf_op jit(solution)/shard_map/ppermute | solution.py:373
  44.1 6.0 %collective-permute-start.11 = (bf16[144,128]{1,0:T(8,128)(2,1)S(1)}, bf16[144,128]{1,0:T(8,128)(2,1)S(1)}, u32[]{:S(2)}, u32[]{:S(2)}) collective-permute-start(bf16[144,128]{1,0:T(8,128)(2,1)S(1)} %get-tuple-element.16), channel_id=1, source_target_pairs={{0,24},{2,26},{4,28},{6,30},{8,16},{10,18},{12,20},{14,22},{16,8},... | collective-permute-start | bytes 110600 | tf_op jit(solution)/shard_map/ppermute | solution.py:373
  45.7 4.9 %collective-permute-start.10 = (bf16[144,128]{1,0:T(8,128)(2,1)S(1)}, bf16[144,128]{1,0:T(8,128)(2,1)S(1)}, u32[]{:S(2)}, u32[]{:S(2)}) collective-permute-start(bf16[144,128]{1,0:T(8,128)(2,1)S(1)} %get-tuple-element.17), channel_id=1, source_target_pairs={{0,16},{2,18},{4,20},{6,22},{8,24},{10,26},{12,28},{14,30},{16,0},... | collective-permute-start | bytes 110600 | tf_op jit(solution)/shard_map/ppermute | solution.py:373
  46.3 4.6 %collective-permute-start.9 = (bf16[144,128]{1,0:T(8,128)(2,1)S(1)}, bf16[144,128]{1,0:T(8,128)(2,1)S(1)}, u32[]{:S(2)}, u32[]{:S(2)}) collective-permute-start(bf16[144,128]{1,0:T(8,128)(2,1)S(1)} %get-tuple-element.18), channel_id=1, source_target_pairs={{0,8},{2,10},{4,12},{6,14},{8,0},{10,2},{12,4},{14,6},{16,24},{18,... | collective-permute-start | bytes 110600 | tf_op jit(solution)/shard_map/ppermute | solution.py:373

commit v4 on v3

--- a/solution.py
+++ b/solution.py
@@ -90,29 +90,28 @@
     )(first, second)
 
 
-def finish_kernel(kept, one, two, three, first, second, total):
-    total[...] = (
-        kept[0].astype(F32) + one[...].astype(F32) + two[...].astype(F32) + three[...].astype(F32)
-    )
+def finish_kernel(wire, crossed, beside, one, two, three, first, second, total):
+    total[...] = wire[0].astype(F32) + crossed[0].astype(F32) + beside[...].astype(F32)
+    total[...] += one[...].astype(F32) + two[...].astype(F32) + three[...].astype(F32)
     second[...] = total[0:108, :]
     first[0:28, :] = total[112:140, 0:64]
     first[28:54, :] = total[112:138, 64:128]
 
 
-def finish_call(kept, pieces):
+def finish_call(wire, crossed, beside, pieces):
     return pl.pallas_call(
         finish_kernel,
         out_shape=(
             jax.ShapeDtypeStruct((54, 64), F32),
             jax.ShapeDtypeStruct((108, 128), F32),
         ),
-        in_specs=[VMEM] * 4,
+        in_specs=[VMEM] * 6,
         out_specs=(VMEM,) * 2,
         scratch_shapes=[pltpu.VMEM((144, 128), F32)],
-        compiler_params=pltpu.CompilerParams(vmem_limit_bytes=2 << 20),
-        cost_estimate=pl.CostEstimate(flops=80_000, bytes_accessed=300_000, transcendentals=0),
+        compiler_params=pltpu.CompilerParams(vmem_limit_bytes=4 << 20),
+        cost_estimate=pl.CostEstimate(flops=120_000, bytes_accessed=300_000, transcendentals=0),
         name="finish",
-    )(kept, *pieces)
+    )(wire, crossed, beside, *pieces)
 
 
 def shift_kernel(pos, own, other, out):
@@ -387,22 +386,31 @@
     cot_other = lax.ppermute(cot, "space", across_space)
     shard = pack_call(w_first, w_second)
     pieces = [swap(shard, 4 * k) for k in range(1, 4)]
-    along_z = jnp.stack([shard] + pieces)
-    piece = swap(along_z, 2)
-    along_y = jnp.concatenate([along_z, piece])
-    across = swap(along_y, 1)
+    beside = swap(shard, 2)
+    along_z = jnp.stack(pieces)
+    rest = swap(along_z, 2)
+    early = jnp.concatenate([shard[None], along_z, beside[None]])
+    early_across = swap(early, 1)
+    late_across = swap(rest, 1)
+    near = jnp.concatenate([early, rest])
+    far = jnp.concatenate([early_across, late_across])
     own = plane_major(volumes)
     other = plane_major(volumes_other)
     moved = shift_call(pos, own, other)
     pooled, wire, delta, w_one = fused_call(
-        factor_one, factor_two, pos, moved, cot, cot_other, along_y, across
-    )
-    got = swap(wire[8:], 1)
-    part = (wire[:8].astype(F32) + got.astype(F32)).astype(BF)
-    got = swap(part[4:], 2)
-    part = (part[:4].astype(F32) + got.astype(F32)).astype(BF)
-    pieces = [swap(part[k], 4 * k) for k in range(1, 4)]
-    share_one, share_two = finish_call(part, pieces)
+        factor_one, factor_two, pos, moved, cot, cot_other, near, far
+    )
+    got = swap(wire[13:16], 1)
+    crossed = swap(wire[8:13], 1)
+    far_y = (wire[5:8].astype(F32) + got.astype(F32)).astype(BF)
+    got = swap(far_y, 2)
+    near_y = (wire[4].astype(F32) + crossed[4].astype(F32)).astype(BF)
+    beside = swap(near_y, 2)
+    along_z = (wire[1:4].astype(F32) + crossed[1:4].astype(F32) + got.astype(F32)).astype(BF)
+    pieces = []
+    for k in range(1, 4):
+        pieces.append(swap(along_z[k - 1], 4 * k))
+    share_one, share_two = finish_call(wire, crossed, beside, pieces)
     grad = volume_call(pos, delta, w_one)
     grad = jnp.transpose(grad.reshape(4, 32, 8, 128), (1, 0, 2, 3))[None]
     pooled = jnp.transpose(pooled.reshape(1, 1, 2, 32, 128), (0, 4, 1, 2, 3))

time: 51.9 us -> 46.1 us (0.89)
  waiting for transfers between devices: 19.4 us -> 10.8 us
  starting transfers between devices: 15.6 us -> 18.3 us
    ppermute x1, waiting for transfers between devices: 5.81 us -> 0.01 us  [paired(): volumes_other = lax.ppermute(volumes, 'space', across_space)]
    ppermute x10 -> x14, waiting for transfers between devices: 13.5 us -> 10.8 us  [swap(): return lax.ppermute(x, 'dp', [(i, i ^ bit) for i in range(16)])]
    ppermute x10 -> x14, starting transfers between devices: 13.5 us -> 15.3 us  [swap(): return lax.ppermute(x, 'dp', [(i, i ^ bit) for i in range(16)])]
    ppermute x1, starting transfers between devices: 0.53 us -> 1.49 us  [paired(): cot_other = lax.ppermute(cot, 'space', across_space)]
  transfers between devices with their start and end apart: 12 -> 16, of which waited for: 9 -> 7; matrix products, arithmetic and copies ran while one was open for 4% -> 5% of each run, Pallas kernels for 5% -> 6%
where the time goes in v4:
time: 46.1 us; the launch traced here: 45.8 us
  starting transfers between devices  18.3 us (40%)
  Pallas kernels  12 us (26%)
  waiting for transfers between devices  10.8 us (23%)
  local copies, waits for them, and re-layouts  3.61 us (8%)
  between operations  0.83 us (2%)
    ppermute x14, starting transfers between devices, swap(): return lax.ppermute(x, 'dp', [(i, i ^ bit) for i in range(16)])  15.3 us
    ppermute x14, waiting for transfers between devices, swap(): return lax.ppermute(x, 'dp', [(i, i ^ bit) for i in range(16)])  10.8 us
    pallas_call x1, Pallas kernels, fused_call(): pl.pallas_call(functools.partial(fused_kernel, factor_one, factor_two), o...  8.58 us
    pallas_call x1, Pallas kernels, volume_call(): pl.pallas_call(volume_kernel, out_shape=jax.ShapeDtypeStruct((4, 32, 1024...  1.72 us
    unnamed x11, local copies, waits for them, and re-layouts  1.56 us
    ppermute x1, starting transfers between devices, paired(): cot_other = lax.ppermute(cot, 'space', across_space)  1.49 us
    ppermute x1, starting transfers between devices, paired(): volumes_other = lax.ppermute(volumes, 'space', across_space)  1.49 us
    reshape x4, local copies, waits for them, and re-layouts, plane_major(): return jnp.transpose(block[0], (1, 0, 2, 3)).reshape(4, 32, 1024)  1.24 us
  transfers between devices with their start and end apart: 16, of which 7 were waited for; matrix products, arithmetic and copies ran while one was open for 5% of the time, Pallas kernels for 6%

profile of v4, /device:TPU:0, one launch (start us, length us, event | category | flops | bytes accessed | tf_op | source)
XLA Modules:
  0.0 45.8 jit_solution(247904125047321806)
XLA Ops:
  0.6 0.7 %copy-done = bf16[108,128]{1,0:T(8,128)(2,1)S(1)} copy-done((bf16[108,128]{1,0:T(8,128)(2,1)S(1)}, bf16[108,128]{1,0:T(8,128)(2,1)}, u32[]{:S(2)}) %copy-start) | copy-done | bytes 27672
  1.4 0.7 %copy-done.1 = bf16[54,64]{1,0:T(8,128)(2,1)S(1)} copy-done((bf16[54,64]{1,0:T(8,128)(2,1)S(1)}, bf16[54,64]{1,0:T(8,128)(2,1)}, u32[]{:S(2)}) %copy-start.1) | copy-done | bytes 6936
  2.1 0.1 pack.1
  2.2 3.1 %collective-permute-start.5 = (bf16[144,128]{1,0:T(8,128)(2,1)S(1)}, bf16[144,128]{1,0:T(8,128)(2,1)S(1)}, u32[]{:S(2)}, u32[]{:S(2)}) collective-permute-start(bf16[144,128]{1,0:T(8,128)(2,1)S(1)} %pack.1), channel_id=1, source_target_pairs={{0,4},{2,6},{4,0},{6,2},{8,12},{10,14},{12,8},{14,10},{16,20},{18,... | collective-permute-start | bytes 110600 | tf_op jit(solution)/shard_map/ppermute | solution.py:372
  5.3 3.6 %collective-permute-start.4 = (bf16[144,128]{1,0:T(8,128)(2,1)S(1)}, bf16[144,128]{1,0:T(8,128)(2,1)S(1)}, u32[]{:S(2)}, u32[]{:S(2)}) collective-permute-start(bf16[144,128]{1,0:T(8,128)(2,1)S(1)} %pack.1), channel_id=1, source_target_pairs={{0,24},{2,26},{4,28},{6,30},{8,16},{10,18},{12,20},{14,22},{16,8},... | collective-permute-start | bytes 110600 | tf_op jit(solution)/shard_map/ppermute | solution.py:372
  8.9 0.8 %collective-permute-start.2 = (bf16[144,128]{1,0:T(8,128)(2,1)S(1)}, bf16[144,128]{1,0:T(8,128)(2,1)S(1)}, u32[]{:S(2)}, u32[]{:S(2)}) collective-permute-start(bf16[144,128]{1,0:T(8,128)(2,1)S(1)} %pack.1), channel_id=1, source_target_pairs={{0,8},{2,10},{4,12},{6,14},{8,0},{10,2},{12,4},{14,6},{16,24},{18,... | collective-permute-start | bytes 110600 | tf_op jit(solution)/shard_map/ppermute | solution.py:372
  9.7 1.5 %collective-permute-start.1 = (bf16[64,128]{1,0:T(8,128)(2,1)}, bf16[64,128]{1,0:T(8,128)(2,1)S(1)}, u32[]{:S(2)}, u32[]{:S(2)}) collective-permute-start(bf16[64,128]{1,0:T(8,128)(2,1)} %bitcast.58), channel_id=1, source_target_pairs={{0,1},{1,0},{2,3},{3,2},{4,5},{5,4},{6,7},{7,6},{8,9},{9,8},{10,11... | collective-permute-start | bytes 49160 | tf_op jit(solution)/shard_map/ppermute | solution.py:386
  11.2 0.3 collective-permute-done.4
  11.4 1.5 %collective-permute-start = (bf16[1,32,4,8,128]{4,3,2,1,0:T(8,128)(2,1)}, bf16[1,32,4,8,128]{4,3,2,1,0:T(8,128)(2,1)S(1)}, u32[]{:S(2)}, u32[]{:S(2)}) collective-permute-start(bf16[1,32,4,8,128]{4,3,2,1,0:T(8,128)(2,1)} %param.4), channel_id=1, source_target_pairs={{0,1},{1,0},{2,3},{3,2},{4,5},{5,4},{6,7},{7,6},{8,9},{9,8},{10,11... | collective-permute-start | bytes 786440 | tf_op jit(solution)/shard_map/ppermute | solution.py:384
  12.9 0.8 %collective-permute-done.3 = bf16[144,128]{1,0:T(8,128)(2,1)S(1)} collective-permute-done((bf16[144,128]{1,0:T(8,128)(2,1)S(1)}, bf16[144,128]{1,0:T(8,128)(2,1)S(1)}, u32[]{:S(2)}, u32[]{:S(2)}) %collective-permute-start.3) | collective-permute-done | bytes 36896 | tf_op jit(solution)/shard_map/ppermute | solution.py:372
  13.8 0.6 %collective-permute-start.6 = (bf16[3,144,128]{2,1,0:T(8,128)(2,1)S(1)}, bf16[3,144,128]{2,1,0:T(8,128)(2,1)S(1)}, u32[]{:S(2)}, u32[]{:S(2)}) collective-permute-start(bf16[3,144,128]{2,1,0:T(8,128)(2,1)S(1)} %pad_maximum_fusion.1), channel_id=1, source_target_pairs={{0,4},{2,6},{4,0},{6,2},{8,12},{10,14},{12,8},{14,10},{16,20},{18,... | collective-permute-start | bytes 331784 | tf_op jit(solution)/shard_map/ppermute | solution.py:372
  14.4 0.1 collective-permute-start.7
  14.5 0.1 pad_add_fusion.pos
  14.6 1.0 %reshape.32 = bf16[4,32,1024]{2,0,1:T(4,128)(2,1)S(1)} reshape(bf16[4,32,8,128]{3,2,0,1:T(8,128)(2,1)} %bitcast.61) | data formatting | bytes 524288 | tf_op jit(solution)/shard_map/reshape | solution.py:376
  15.6 0.1 copy.11.own
  15.7 2.9 %collective-permute-done.6 = bf16[3,144,128]{2,1,0:T(8,128)(2,1)S(1)} collective-permute-done((bf16[3,144,128]{2,1,0:T(8,128)(2,1)S(1)}, bf16[3,144,128]{2,1,0:T(8,128)(2,1)S(1)}, u32[]{:S(2)}, u32[]{:S(2)}) %collective-permute-start.6) | collective-permute-done | bytes 110624 | tf_op jit(solution)/shard_map/ppermute | solution.py:372
  18.6 1.3 %collective-permute-done.8 = bf16[3,144,128]{2,1,0:T(8,128)(2,1)S(1)} collective-permute-done((bf16[3,144,128]{2,1,0:T(8,128)(2,1)S(1)}, bf16[3,144,128]{2,1,0:T(8,128)(2,1)S(1)}, u32[]{:S(2)}, u32[]{:S(2)}) %collective-permute-start.8) | collective-permute-done | bytes 110624 | tf_op jit(solution)/shard_map/ppermute | solution.py:372
  20.0 0.1 copy.12.other
  20.1 0.9 %shift.1.v3 = bf16[10,96,1024]{2,1,0:T(8,128)(2,1)S(1)} custom-call(s32[2]{0:T(128)S(1)} %pad_add_fusion.pos, bf16[4,32,1024]{2,1,0:T(8,128)(2,1)S(1)} %copy.11.own, bf16[4,32,1024]{2,1,0:T(8,128)(2,1)S(1)} %copy.12.other), custom_call_target="tpu_custom_call" | custom-call | flops 600000 | bytes 2500000 | tf_op jit(solution)/shard_map/shift/pallas_call | solution.py:132
  21.0 8.6 %fused.1 = (bf16[64,128]{1,0:T(8,128)(2,1)}, bf16[16,144,128]{2,1,0:T(8,128)(2,1)S(1)}, bf16[10,64,1280]{2,1,0:T(8,128)(2,1)S(1)}, bf16[864,64]{1,0:T(8,128)(2,1)S(1)}) custom-call(s32[2]{0:T(128)S(1)} %pad_add_fusion.pos, bf16[10,96,1024]{2,1,0:T(8,128)(2,1)S(1)} %shift.1.v3, bf16[64,128]{1,0:T(8,128)(2,1)S(1)} %bitcast.59, ...), custom_call_target="tpu_custom_call" | custom-call | flops 4000000000 | bytes 6000000 | tf_op jit(solution)/shard_map/fused/pallas_call | solution.py:320
  29.6 0.2 collective-permute-start.11
  29.9 0.4 collective-permute-start.9
  30.3 1.7 %volume.1 = bf16[4,32,1024]{2,1,0:T(8,128)(2,1)S(1)} custom-call(s32[2]{0:T(128)S(1)} %pad_add_fusion.pos, bf16[10,64,1280]{2,1,0:T(8,128)(2,1)S(1)} %get-tuple-element.11.dp, bf16[864,64]{1,0:T(8,128)(2,1)S(1)} %get-tuple-element.12.w1), custom_call_target="tpu_custom_call" | custom-call | flops 1000000000 | bytes 3000000 | tf_op jit(solution)/shard_map/volume/pallas_call | solution.py:348
  32.1 0.6 %collective-permute-start.12 = (bf16[3,144,128]{2,1,0:T(8,128)(2,1)S(1)}, bf16[3,144,128]{2,1,0:T(8,128)(2,1)S(1)}, u32[]{:S(2)}, u32[]{:S(2)}) collective-permute-start(bf16[3,144,128]{2,1,0:T(8,128)(2,1)S(1)} %add_convert_fusion.1), channel_id=1, source_target_pairs={{0,4},{2,6},{4,0},{6,2},{8,12},{10,14},{12,8},{14,10},{16,20},{18,... | collective-permute-start | bytes 331784 | tf_op jit(solution)/shard_map/ppermute | solution.py:372
  32.7 1.6 %collective-permute-start.10 = (bf16[144,128]{1,0:T(8,128)(2,1)S(1)}, bf16[144,128]{1,0:T(8,128)(2,1)S(1)}, u32[]{:S(2)}, u32[]{:S(2)}) collective-permute-start(bf16[144,128]{1,0:T(8,128)(2,1)S(1)} %fusion), channel_id=1, source_target_pairs={{0,4},{2,6},{4,0},{6,2},{8,12},{10,14},{12,8},{14,10},{16,20},{18,... | collective-permute-start | bytes 110600 | tf_op jit(solution)/shard_map/ppermute | solution.py:372
  34.3 3.4 %collective-permute-done.12 = bf16[3,144,128]{2,1,0:T(8,128)(2,1)S(1)} collective-permute-done((bf16[3,144,128]{2,1,0:T(8,128)(2,1)S(1)}, bf16[3,144,128]{2,1,0:T(8,128)(2,1)S(1)}, u32[]{:S(2)}, u32[]{:S(2)}) %collective-permute-start.12) | collective-permute-done | bytes 110624 | tf_op jit(solution)/shard_map/ppermute | solution.py:372
  37.8 2.5 %collective-permute-start.15 = (bf16[144,128]{1,0:T(8,128)(2,1)S(1)}, bf16[144,128]{1,0:T(8,128)(2,1)S(1)}, u32[]{:S(2)}, u32[]{:S(2)}) collective-permute-start(bf16[144,128]{1,0:T(8,128)(2,1)S(1)} %get-tuple-element.16), channel_id=1, source_target_pairs={{0,24},{2,26},{4,28},{6,30},{8,16},{10,18},{12,20},{14,22},{16,8},... | collective-permute-start | bytes 110600 | tf_op jit(solution)/shard_map/ppermute | solution.py:372
  40.2 2.0 %collective-permute-start.13 = (bf16[144,128]{1,0:T(8,128)(2,1)S(1)}, bf16[144,128]{1,0:T(8,128)(2,1)S(1)}, u32[]{:S(2)}, u32[]{:S(2)}) collective-permute-start(bf16[144,128]{1,0:T(8,128)(2,1)S(1)} %get-tuple-element.18), channel_id=1, source_target_pairs={{0,8},{2,10},{4,12},{6,14},{8,0},{10,2},{12,4},{14,6},{16,24},{18,... | collective-permute-start | bytes 110600 | tf_op jit(solution)/shard_map/ppermute | solution.py:372
  42.2 0.7 %copy_bitcast_fusion = bf16[1,32,4,8,128]{4,3,2,1,0:T(8,128)(2,1)} fusion(bf16[4,32,8,128]{3,2,1,0:T(8,128)(2,1)S(1)} %bitcast.60), kind=kLoop, calls=%fused_computation.1 | loop fusion | bytes 524288 | tf_op jit(solution)/shard_map/broadcast_in_dim | solution.py:415
  43.0 0.7 %collective-permute-done.15.three = bf16[144,128]{1,0:T(8,128)(2,1)S(1)} collective-permute-done((bf16[144,128]{1,0:T(8,128)(2,1)S(1)}, bf16[144,128]{1,0:T(8,128)(2,1)S(1)}, u32[]{:S(2)}, u32[]{:S(2)}) %collective-permute-start.15) | collective-permute-done | bytes 36896 | tf_op jit(solution)/shard_map/ppermute | solution.py:372
  43.7 1.4 %collective-permute-done.14.two = bf16[144,128]{1,0:T(8,128)(2,1)S(1)} collective-permute-done((bf16[144,128]{1,0:T(8,128)(2,1)S(1)}, bf16[144,128]{1,0:T(8,128)(2,1)S(1)}, u32[]{:S(2)}, u32[]{:S(2)}) %collective-permute-start.14) | collective-permute-done | bytes 36896 | tf_op jit(solution)/shard_map/ppermute | solution.py:372
  45.1 0.7 %finish.1 = (f32[54,64]{1,0:T(8,128)}, f32[108,128]{1,0:T(8,128)}) custom-call(bf16[16,144,128]{2,1,0:T(8,128)(2,1)S(1)} %get-tuple-element.13.wire, bf16[5,144,128]{2,1,0:T(8,128)(2,1)S(1)} %collective-permute-done.9.crossed, bf16[144,128]{1,0:T(8,128)(2,1)S(1)} %collective-permute-done.10.beside, bf16[144,128]{1,0:T(8,128)(2,1)S(1)} %collective-permute-done.13.one, ...), custom_call_target="tpu_custom_call" | custom-call | flops 120000 | bytes 300000 | tf_op jit(solution)/shard_map/finish/pallas_call | solution.py:102
  (32 shorter events, 0.4 us)
Async XLA Ops:
  0.6 0.7 %copy-start = (bf16[108,128]{1,0:T(8,128)(2,1)S(1)}, bf16[108,128]{1,0:T(8,128)(2,1)}, u32[]{:S(2)}) copy-start(bf16[108,128]{1,0:T(8,128)(2,1)} %second.1) | copy-start | bytes 82948
  1.4 0.7 %copy-start.1 = (bf16[54,64]{1,0:T(8,128)(2,1)S(1)}, bf16[54,64]{1,0:T(8,128)(2,1)}, u32[]{:S(2)}) copy-start(bf16[54,64]{1,0:T(8,128)(2,1)} %first.1) | copy-start | bytes 20740
  2.2 12.2 %collective-permute-start.5 = (bf16[144,128]{1,0:T(8,128)(2,1)S(1)}, bf16[144,128]{1,0:T(8,128)(2,1)S(1)}, u32[]{:S(2)}, u32[]{:S(2)}) collective-permute-start(bf16[144,128]{1,0:T(8,128)(2,1)S(1)} %pack.1), channel_id=1, source_target_pairs={{0,4},{2,6},{4,0},{6,2},{8,12},{10,14},{12,8},{14,10},{16,20},{18,... | collective-permute-start | bytes 110600 | tf_op jit(solution)/shard_map/ppermute | solution.py:372
  5.3 6.1 %collective-permute-start.4 = (bf16[144,128]{1,0:T(8,128)(2,1)S(1)}, bf16[144,128]{1,0:T(8,128)(2,1)S(1)}, u32[]{:S(2)}, u32[]{:S(2)}) collective-permute-start(bf16[144,128]{1,0:T(8,128)(2,1)S(1)} %pack.1), channel_id=1, source_target_pairs={{0,24},{2,26},{4,28},{6,30},{8,16},{10,18},{12,20},{14,22},{16,8},... | collective-permute-start | bytes 110600 | tf_op jit(solution)/shard_map/ppermute | solution.py:372
  8.9 4.9 %collective-permute-start.3 = (bf16[144,128]{1,0:T(8,128)(2,1)S(1)}, bf16[144,128]{1,0:T(8,128)(2,1)S(1)}, u32[]{:S(2)}, u32[]{:S(2)}) collective-permute-start(bf16[144,128]{1,0:T(8,128)(2,1)S(1)} %pack.1), channel_id=1, source_target_pairs={{0,16},{2,18},{4,20},{6,22},{8,24},{10,26},{12,28},{14,30},{16,0},... | collective-permute-start | bytes 110600 | tf_op jit(solution)/shard_map/ppermute | solution.py:372
  8.9 4.9 %collective-permute-start.2 = (bf16[144,128]{1,0:T(8,128)(2,1)S(1)}, bf16[144,128]{1,0:T(8,128)(2,1)S(1)}, u32[]{:S(2)}, u32[]{:S(2)}) collective-permute-start(bf16[144,128]{1,0:T(8,128)(2,1)S(1)} %pack.1), channel_id=1, source_target_pairs={{0,8},{2,10},{4,12},{6,14},{8,0},{10,2},{12,4},{14,6},{16,24},{18,... | collective-permute-start | bytes 110600 | tf_op jit(solution)/shard_map/ppermute | solution.py:372
  9.7 11.3 %collective-permute-start.1 = (bf16[64,128]{1,0:T(8,128)(2,1)}, bf16[64,128]{1,0:T(8,128)(2,1)S(1)}, u32[]{:S(2)}, u32[]{:S(2)}) collective-permute-start(bf16[64,128]{1,0:T(8,128)(2,1)} %bitcast.58), channel_id=1, source_target_pairs={{0,1},{1,0},{2,3},{3,2},{4,5},{5,4},{6,7},{7,6},{8,9},{9,8},{10,11... | collective-permute-start | bytes 49160 | tf_op jit(solution)/shard_map/ppermute | solution.py:386
  11.4 8.5 %collective-permute-start = (bf16[1,32,4,8,128]{4,3,2,1,0:T(8,128)(2,1)}, bf16[1,32,4,8,128]{4,3,2,1,0:T(8,128)(2,1)S(1)}, u32[]{:S(2)}, u32[]{:S(2)}) collective-permute-start(bf16[1,32,4,8,128]{4,3,2,1,0:T(8,128)(2,1)} %param.4), channel_id=1, source_target_pairs={{0,1},{1,0},{2,3},{3,2},{4,5},{5,4},{6,7},{7,6},{8,9},{9,8},{10,11... | collective-permute-start | bytes 786440 | tf_op jit(solution)/shard_map/ppermute | solution.py:384
  13.8 4.8 %collective-permute-start.6 = (bf16[3,144,128]{2,1,0:T(8,128)(2,1)S(1)}, bf16[3,144,128]{2,1,0:T(8,128)(2,1)S(1)}, u32[]{:S(2)}, u32[]{:S(2)}) collective-permute-start(bf16[3,144,128]{2,1,0:T(8,128)(2,1)S(1)} %pad_maximum_fusion.1), channel_id=1, source_target_pairs={{0,4},{2,6},{4,0},{6,2},{8,12},{10,14},{12,8},{14,10},{16,20},{18,... | collective-permute-start | bytes 331784 | tf_op jit(solution)/shard_map/ppermute | solution.py:372
  14.4 4.2 %collective-permute-start.7 = (bf16[5,144,128]{2,1,0:T(8,128)(2,1)S(1)}, bf16[5,144,128]{2,1,0:T(8,128)(2,1)S(1)}, u32[]{:S(2)}, u32[]{:S(2)}) collective-permute-start(bf16[5,144,128]{2,1,0:T(8,128)(2,1)S(1)} %get-tuple-element.19), channel_id=1, source_target_pairs={{0,2},{2,0},{4,6},{6,4},{8,10},{10,8},{12,14},{14,12},{16,18},{18,... | collective-permute-start | bytes 552968 | tf_op jit(solution)/shard_map/ppermute | solution.py:372
  18.6 1.3 %collective-permute-start.8 = (bf16[3,144,128]{2,1,0:T(8,128)(2,1)S(1)}, bf16[3,144,128]{2,1,0:T(8,128)(2,1)S(1)}, u32[]{:S(2)}, u32[]{:S(2)}) collective-permute-start(bf16[3,144,128]{2,1,0:T(8,128)(2,1)S(1)} %collective-permute-done.6), channel_id=1, source_target_pairs={{0,2},{2,0},{4,6},{6,4},{8,10},{10,8},{12,14},{14,12},{16,18},{18,... | collective-permute-start | bytes 331784 | tf_op jit(solution)/shard_map/ppermute | solution.py:372
  18.6 2.4 %copy-start.2 = (bf16[1,128,1,2,32]{1,4,3,2,0:T(8,128)(2,1)S(1)}, bf16[1,128,1,2,32]{1,4,3,2,0:T(8,128)(2,1)}, u32[]{:S(2)}) copy-start(bf16[1,128,1,2,32]{1,4,3,2,0:T(8,128)(2,1)} %param.7) | copy-start | bytes 49156
  29.6 2.4 %collective-permute-start.11 = (bf16[3,144,128]{2,1,0:T(8,128)(2,1)S(1)}, bf16[3,144,128]{2,1,0:T(8,128)(2,1)S(1)}, u32[]{:S(2)}, u32[]{:S(2)}) collective-permute-start(bf16[3,144,128]{2,1,0:T(8,128)(2,1)S(1)} %slice.36), channel_id=1, source_target_pairs={{0,2},{2,0},{4,6},{6,4},{8,10},{10,8},{12,14},{14,12},{16,18},{18,... | collective-permute-start | bytes 331784 | tf_op jit(solution)/shard_map/ppermute | solution.py:372
  29.9 2.8 %collective-permute-start.9 = (bf16[5,144,128]{2,1,0:T(8,128)(2,1)S(1)}, bf16[5,144,128]{2,1,0:T(8,128)(2,1)S(1)}, u32[]{:S(2)}, u32[]{:S(2)}) collective-permute-start(bf16[5,144,128]{2,1,0:T(8,128)(2,1)S(1)} %slice.30), channel_id=1, source_target_pairs={{0,2},{2,0},{4,6},{6,4},{8,10},{10,8},{12,14},{14,12},{16,18},{18,... | collective-permute-start | bytes 552968 | tf_op jit(solution)/shard_map/ppermute | solution.py:372
  32.1 5.6 %collective-permute-start.12 = (bf16[3,144,128]{2,1,0:T(8,128)(2,1)S(1)}, bf16[3,144,128]{2,1,0:T(8,128)(2,1)S(1)}, u32[]{:S(2)}, u32[]{:S(2)}) collective-permute-start(bf16[3,144,128]{2,1,0:T(8,128)(2,1)S(1)} %add_convert_fusion.1), channel_id=1, source_target_pairs={{0,4},{2,6},{4,0},{6,2},{8,12},{10,14},{12,8},{14,10},{16,20},{18,... | collective-permute-start | bytes 331784 | tf_op jit(solution)/shard_map/ppermute | solution.py:372
  32.7 10.3 %collective-permute-start.10 = (bf16[144,128]{1,0:T(8,128)(2,1)S(1)}, bf16[144,128]{1,0:T(8,128)(2,1)S(1)}, u32[]{:S(2)}, u32[]{:S(2)}) collective-permute-start(bf16[144,128]{1,0:T(8,128)(2,1)S(1)} %fusion), channel_id=1, source_target_pairs={{0,4},{2,6},{4,0},{6,2},{8,12},{10,14},{12,8},{14,10},{16,20},{18,... | collective-permute-start | bytes 110600 | tf_op jit(solution)/shard_map/ppermute | solution.py:372
  37.8 5.9 %collective-permute-start.15 = (bf16[144,128]{1,0:T(8,128)(2,1)S(1)}, bf16[144,128]{1,0:T(8,128)(2,1)S(1)}, u32[]{:S(2)}, u32[]{:S(2)}) collective-permute-start(bf16[144,128]{1,0:T(8,128)(2,1)S(1)} %get-tuple-element.16), channel_id=1, source_target_pairs={{0,24},{2,26},{4,28},{6,30},{8,16},{10,18},{12,20},{14,22},{16,8},... | collective-permute-start | bytes 110600 | tf_op jit(solution)/shard_map/ppermute | solution.py:372
  40.2 4.9 %collective-permute-start.14 = (bf16[144,128]{1,0:T(8,128)(2,1)S(1)}, bf16[144,128]{1,0:T(8,128)(2,1)S(1)}, u32[]{:S(2)}, u32[]{:S(2)}) collective-permute-start(bf16[144,128]{1,0:T(8,128)(2,1)S(1)} %get-tuple-element.17), channel_id=1, source_target_pairs={{0,16},{2,18},{4,20},{6,22},{8,24},{10,26},{12,28},{14,30},{16,0},... | collective-permute-start | bytes 110600 | tf_op jit(solution)/shard_map/ppermute | solution.py:372
  40.2 4.9 %collective-permute-start.13 = (bf16[144,128]{1,0:T(8,128)(2,1)S(1)}, bf16[144,128]{1,0:T(8,128)(2,1)S(1)}, u32[]{:S(2)}, u32[]{:S(2)}) collective-permute-start(bf16[144,128]{1,0:T(8,128)(2,1)S(1)} %get-tuple-element.18), channel_id=1, source_target_pairs={{0,8},{2,10},{4,12},{6,14},{8,0},{10,2},{12,4},{14,6},{16,24},{18,... | collective-permute-start | bytes 110600 | tf_op jit(solution)/shard_map/ppermute | solution.py:372

commit v5 on v4

--- a/solution.py
+++ b/solution.py
@@ -66,19 +66,19 @@
         copy.wait()
     wide[0:108, :] = second_here[...].astype(F32)
     narrow[...] = first_here[...].astype(F32)
-    wide[112:140, 0:64] = narrow[0:28, :]
-    wide[112:138, 64:128] = narrow[28:54, :]
+    wide[108:136, 0:64] = narrow[0:28, :]
+    wide[108:134, 64:128] = narrow[28:54, :]
     out[...] = wide[...].astype(BF)
 
 
 def pack_call(first, second):
     return pl.pallas_call(
         pack_kernel,
-        out_shape=jax.ShapeDtypeStruct((144, 128), BF),
+        out_shape=jax.ShapeDtypeStruct((136, 128), BF),
         in_specs=[pl.BlockSpec(memory_space=pltpu.HBM)] * 2,
         out_specs=VMEM,
         scratch_shapes=[
-            pltpu.VMEM((144, 128), F32),
+            pltpu.VMEM((136, 128), F32),
             pltpu.VMEM((54, 64), F32),
             pltpu.VMEM((54, 64), BF),
             pltpu.VMEM((108, 128), BF),
@@ -94,8 +94,8 @@
     total[...] = wire[0].astype(F32) + crossed[0].astype(F32) + beside[...].astype(F32)
     total[...] += one[...].astype(F32) + two[...].astype(F32) + three[...].astype(F32)
     second[...] = total[0:108, :]
-    first[0:28, :] = total[112:140, 0:64]
-    first[28:54, :] = total[112:138, 64:128]
+    first[0:28, :] = total[108:136, 0:64]
+    first[28:54, :] = total[108:134, 64:128]
 
 
 def finish_call(wire, crossed, beside, pieces):
@@ -107,7 +107,7 @@
         ),
         in_specs=[VMEM] * 6,
         out_specs=(VMEM,) * 2,
-        scratch_shapes=[pltpu.VMEM((144, 128), F32)],
+        scratch_shapes=[pltpu.VMEM((136, 128), F32)],
         compiler_params=pltpu.CompilerParams(vmem_limit_bytes=4 << 20),
         cost_estimate=pl.CostEstimate(flops=120_000, bytes_accessed=300_000, transcendentals=0),
         name="finish",
@@ -146,8 +146,8 @@
         place = (k // 2) % 2 * 4 + k // 4
         blk = lax.select(k % 2 == 0, near[place], far[place])
         w2s[108 * d : 108 * d + 108, :] = blk[0:108]
-        w1s[54 * d : 54 * d + 28, :] = blk[112:140, 0:64]
-        w1s[54 * d + 28 : 54 * d + 54, :] = blk[112:138, 64:128]
+        w1s[54 * d : 54 * d + 28, :] = blk[108:136, 0:64]
+        w1s[54 * d + 28 : 54 * d + 54, :] = blk[108:134, 64:128]
 
 
 def fused_kernel(
@@ -289,8 +289,8 @@
     for d in range(16):
         k = jnp.bitwise_xor(me, d)
         place = k % 2 * 8 + (k // 2) % 2 * 4 + k // 4
-        wire_out[place, 0:112, :] = g2s[108 * d : 108 * d + 112, :]
-        wire_out[place, 112:144, :] = g1s[54 * d + 32 : 54 * d + 64, :]
+        wire_out[place, 0:108, :] = g2s[108 * d : 108 * d + 108, :]
+        wire_out[place, 108:136, :] = g1s[54 * d + 32 : 54 * d + 60, :]
 
 
 def volume_kernel(pos, dp, w1, out, wd):
@@ -321,7 +321,7 @@
         functools.partial(fused_kernel, factor_one, factor_two),
         out_shape=(
             jax.ShapeDtypeStruct((64, 128), BF),
-            jax.ShapeDtypeStruct((16, 144, 128), BF),
+            jax.ShapeDtypeStruct((16, 136, 128), BF),
             jax.ShapeDtypeStruct((10, 64, 1280), BF),
             jax.ShapeDtypeStruct((864, 64), BF),
         ),

time: 46.1 us -> 45.8 us (level)
  no operation moved by 1% of the time
where the time goes in v5:
time: 45.8 us; the launch traced here: 45.5 us
  starting transfers between devices  18.3 us (40%)
  Pallas kernels  12 us (26%)
  waiting for transfers between devices  10.5 us (23%)
  local copies, waits for them, and re-layouts  3.61 us (8%)
  between operations  0.83 us (2%)
    ppermute x14, starting transfers between devices, swap(): return lax.ppermute(x, 'dp', [(i, i ^ bit) for i in range(16)])  15.3 us
    ppermute x14, waiting for transfers between devices, swap(): return lax.ppermute(x, 'dp', [(i, i ^ bit) for i in range(16)])  10.5 us
    pallas_call x1, Pallas kernels, fused_call(): pl.pallas_call(functools.partial(fused_kernel, factor_one, factor_two), o...  8.58 us
    pallas_call x1, Pallas kernels, volume_call(): pl.pallas_call(volume_kernel, out_shape=jax.ShapeDtypeStruct((4, 32, 1024...  1.72 us
    unnamed x11, local copies, waits for them, and re-layouts  1.56 us
    ppermute x1, starting transfers between devices, paired(): cot_other = lax.ppermute(cot, 'space', across_space)  1.49 us
    ppermute x1, starting transfers between devices, paired(): volumes_other = lax.ppermute(volumes, 'space', across_space)  1.49 us
    reshape x4, local copies, waits for them, and re-layouts, plane_major(): return jnp.transpose(block[0], (1, 0, 2, 3)).reshape(4, 32, 1024)  1.24 us
  transfers between devices with their start and end apart: 16, of which 7 were waited for; matrix products, arithmetic and copies ran while one was open for 5% of the time, Pallas kernels for 6%

profile of v5, /device:TPU:0, one launch (start us, length us, event | category | flops | bytes accessed | tf_op | source)
XLA Modules:
  0.0 45.5 jit_solution(14541970204958995760)
XLA Ops:
  0.6 0.7 %copy-done = bf16[108,128]{1,0:T(8,128)(2,1)S(1)} copy-done((bf16[108,128]{1,0:T(8,128)(2,1)S(1)}, bf16[108,128]{1,0:T(8,128)(2,1)}, u32[]{:S(2)}) %copy-start) | copy-done | bytes 27672
  1.4 0.7 %copy-done.1 = bf16[54,64]{1,0:T(8,128)(2,1)S(1)} copy-done((bf16[54,64]{1,0:T(8,128)(2,1)S(1)}, bf16[54,64]{1,0:T(8,128)(2,1)}, u32[]{:S(2)}) %copy-start.1) | copy-done | bytes 6936
  2.1 0.1 pack.1
  2.2 3.1 %collective-permute-start.5 = (bf16[136,128]{1,0:T(8,128)(2,1)S(1)}, bf16[136,128]{1,0:T(8,128)(2,1)S(1)}, u32[]{:S(2)}, u32[]{:S(2)}) collective-permute-start(bf16[136,128]{1,0:T(8,128)(2,1)S(1)} %pack.1), channel_id=1, source_target_pairs={{0,4},{2,6},{4,0},{6,2},{8,12},{10,14},{12,8},{14,10},{16,20},{18,... | collective-permute-start | bytes 104456 | tf_op jit(solution)/shard_map/ppermute | solution.py:372
  5.3 3.6 %collective-permute-start.4 = (bf16[136,128]{1,0:T(8,128)(2,1)S(1)}, bf16[136,128]{1,0:T(8,128)(2,1)S(1)}, u32[]{:S(2)}, u32[]{:S(2)}) collective-permute-start(bf16[136,128]{1,0:T(8,128)(2,1)S(1)} %pack.1), channel_id=1, source_target_pairs={{0,24},{2,26},{4,28},{6,30},{8,16},{10,18},{12,20},{14,22},{16,8},... | collective-permute-start | bytes 104456 | tf_op jit(solution)/shard_map/ppermute | solution.py:372
  8.9 0.8 %collective-permute-start.2 = (bf16[136,128]{1,0:T(8,128)(2,1)S(1)}, bf16[136,128]{1,0:T(8,128)(2,1)S(1)}, u32[]{:S(2)}, u32[]{:S(2)}) collective-permute-start(bf16[136,128]{1,0:T(8,128)(2,1)S(1)} %pack.1), channel_id=1, source_target_pairs={{0,8},{2,10},{4,12},{6,14},{8,0},{10,2},{12,4},{14,6},{16,24},{18,... | collective-permute-start | bytes 104456 | tf_op jit(solution)/shard_map/ppermute | solution.py:372
  9.7 1.5 %collective-permute-start.1 = (bf16[64,128]{1,0:T(8,128)(2,1)}, bf16[64,128]{1,0:T(8,128)(2,1)S(1)}, u32[]{:S(2)}, u32[]{:S(2)}) collective-permute-start(bf16[64,128]{1,0:T(8,128)(2,1)} %bitcast.58), channel_id=1, source_target_pairs={{0,1},{1,0},{2,3},{3,2},{4,5},{5,4},{6,7},{7,6},{8,9},{9,8},{10,11... | collective-permute-start | bytes 49160 | tf_op jit(solution)/shard_map/ppermute | solution.py:386
  11.2 0.2 collective-permute-done.4
  11.4 1.5 %collective-permute-start = (bf16[1,32,4,8,128]{4,3,2,1,0:T(8,128)(2,1)}, bf16[1,32,4,8,128]{4,3,2,1,0:T(8,128)(2,1)S(1)}, u32[]{:S(2)}, u32[]{:S(2)}) collective-permute-start(bf16[1,32,4,8,128]{4,3,2,1,0:T(8,128)(2,1)} %param.4), channel_id=1, source_target_pairs={{0,1},{1,0},{2,3},{3,2},{4,5},{5,4},{6,7},{7,6},{8,9},{9,8},{10,11... | collective-permute-start | bytes 786440 | tf_op jit(solution)/shard_map/ppermute | solution.py:384
  12.9 0.8 %collective-permute-done.3 = bf16[136,128]{1,0:T(8,128)(2,1)S(1)} collective-permute-done((bf16[136,128]{1,0:T(8,128)(2,1)S(1)}, bf16[136,128]{1,0:T(8,128)(2,1)S(1)}, u32[]{:S(2)}, u32[]{:S(2)}) %collective-permute-start.3) | collective-permute-done | bytes 34848 | tf_op jit(solution)/shard_map/ppermute | solution.py:372
  13.8 0.6 %collective-permute-start.6 = (bf16[3,136,128]{2,1,0:T(8,128)(2,1)S(1)}, bf16[3,136,128]{2,1,0:T(8,128)(2,1)S(1)}, u32[]{:S(2)}, u32[]{:S(2)}) collective-permute-start(bf16[3,136,128]{2,1,0:T(8,128)(2,1)S(1)} %pad_maximum_fusion.1), channel_id=1, source_target_pairs={{0,4},{2,6},{4,0},{6,2},{8,12},{10,14},{12,8},{14,10},{16,20},{18,... | collective-permute-start | bytes 313352 | tf_op jit(solution)/shard_map/ppermute | solution.py:372
  14.4 0.1 collective-permute-start.7
  14.5 0.1 pad_add_fusion.pos
  14.6 1.0 %reshape.32 = bf16[4,32,1024]{2,0,1:T(4,128)(2,1)S(1)} reshape(bf16[4,32,8,128]{3,2,0,1:T(8,128)(2,1)} %bitcast.61) | data formatting | bytes 524288 | tf_op jit(solution)/shard_map/reshape | solution.py:376
  15.6 0.1 copy.11.own
  15.7 2.8 %collective-permute-done.6 = bf16[3,136,128]{2,1,0:T(8,128)(2,1)S(1)} collective-permute-done((bf16[3,136,128]{2,1,0:T(8,128)(2,1)S(1)}, bf16[3,136,128]{2,1,0:T(8,128)(2,1)S(1)}, u32[]{:S(2)}, u32[]{:S(2)}) %collective-permute-start.6) | collective-permute-done | bytes 104480 | tf_op jit(solution)/shard_map/ppermute | solution.py:372
  18.5 1.3 %collective-permute-done.8 = bf16[3,136,128]{2,1,0:T(8,128)(2,1)S(1)} collective-permute-done((bf16[3,136,128]{2,1,0:T(8,128)(2,1)S(1)}, bf16[3,136,128]{2,1,0:T(8,128)(2,1)S(1)}, u32[]{:S(2)}, u32[]{:S(2)}) %collective-permute-start.8) | collective-permute-done | bytes 104480 | tf_op jit(solution)/shard_map/ppermute | solution.py:372
  19.9 0.1 copy.12.other
  20.0 0.9 %shift.1.v3 = bf16[10,96,1024]{2,1,0:T(8,128)(2,1)S(1)} custom-call(s32[2]{0:T(128)S(1)} %pad_add_fusion.pos, bf16[4,32,1024]{2,1,0:T(8,128)(2,1)S(1)} %copy.11.own, bf16[4,32,1024]{2,1,0:T(8,128)(2,1)S(1)} %copy.12.other), custom_call_target="tpu_custom_call" | custom-call | flops 600000 | bytes 2500000 | tf_op jit(solution)/shard_map/shift/pallas_call | solution.py:132
  20.9 8.6 %fused.1 = (bf16[64,128]{1,0:T(8,128)(2,1)}, bf16[16,136,128]{2,1,0:T(8,128)(2,1)S(1)}, bf16[10,64,1280]{2,1,0:T(8,128)(2,1)S(1)}, bf16[864,64]{1,0:T(8,128)(2,1)S(1)}) custom-call(s32[2]{0:T(128)S(1)} %pad_add_fusion.pos, bf16[10,96,1024]{2,1,0:T(8,128)(2,1)S(1)} %shift.1.v3, bf16[64,128]{1,0:T(8,128)(2,1)S(1)} %bitcast.59, ...), custom_call_target="tpu_custom_call" | custom-call | flops 4000000000 | bytes 6000000 | tf_op jit(solution)/shard_map/fused/pallas_call | solution.py:320
  29.5 0.2 collective-permute-start.11
  29.7 0.4 collective-permute-start.9
  30.2 1.7 %volume.1 = bf16[4,32,1024]{2,1,0:T(8,128)(2,1)S(1)} custom-call(s32[2]{0:T(128)S(1)} %pad_add_fusion.pos, bf16[10,64,1280]{2,1,0:T(8,128)(2,1)S(1)} %get-tuple-element.11.dp, bf16[864,64]{1,0:T(8,128)(2,1)S(1)} %get-tuple-element.12.w1), custom_call_target="tpu_custom_call" | custom-call | flops 1000000000 | bytes 3000000 | tf_op jit(solution)/shard_map/volume/pallas_call | solution.py:348
  32.0 0.6 %collective-permute-start.12 = (bf16[3,136,128]{2,1,0:T(8,128)(2,1)S(1)}, bf16[3,136,128]{2,1,0:T(8,128)(2,1)S(1)}, u32[]{:S(2)}, u32[]{:S(2)}) collective-permute-start(bf16[3,136,128]{2,1,0:T(8,128)(2,1)S(1)} %add_convert_fusion.1), channel_id=1, source_target_pairs={{0,4},{2,6},{4,0},{6,2},{8,12},{10,14},{12,8},{14,10},{16,20},{18,... | collective-permute-start | bytes 313352 | tf_op jit(solution)/shard_map/ppermute | solution.py:372
  32.6 1.6 %collective-permute-start.10 = (bf16[136,128]{1,0:T(8,128)(2,1)S(1)}, bf16[136,128]{1,0:T(8,128)(2,1)S(1)}, u32[]{:S(2)}, u32[]{:S(2)}) collective-permute-start(bf16[136,128]{1,0:T(8,128)(2,1)S(1)} %fusion), channel_id=1, source_target_pairs={{0,4},{2,6},{4,0},{6,2},{8,12},{10,14},{12,8},{14,10},{16,20},{18,... | collective-permute-start | bytes 104456 | tf_op jit(solution)/shard_map/ppermute | solution.py:372
  34.2 3.2 %collective-permute-done.12 = bf16[3,136,128]{2,1,0:T(8,128)(2,1)S(1)} collective-permute-done((bf16[3,136,128]{2,1,0:T(8,128)(2,1)S(1)}, bf16[3,136,128]{2,1,0:T(8,128)(2,1)S(1)}, u32[]{:S(2)}, u32[]{:S(2)}) %collective-permute-start.12) | collective-permute-done | bytes 104480 | tf_op jit(solution)/shard_map/ppermute | solution.py:372
  37.5 2.5 %collective-permute-start.15 = (bf16[136,128]{1,0:T(8,128)(2,1)S(1)}, bf16[136,128]{1,0:T(8,128)(2,1)S(1)}, u32[]{:S(2)}, u32[]{:S(2)}) collective-permute-start(bf16[136,128]{1,0:T(8,128)(2,1)S(1)} %get-tuple-element.16), channel_id=1, source_target_pairs={{0,24},{2,26},{4,28},{6,30},{8,16},{10,18},{12,20},{14,22},{16,8},... | collective-permute-start | bytes 104456 | tf_op jit(solution)/shard_map/ppermute | solution.py:372
  40.0 2.0 %collective-permute-start.13 = (bf16[136,128]{1,0:T(8,128)(2,1)S(1)}, bf16[136,128]{1,0:T(8,128)(2,1)S(1)}, u32[]{:S(2)}, u32[]{:S(2)}) collective-permute-start(bf16[136,128]{1,0:T(8,128)(2,1)S(1)} %get-tuple-element.18), channel_id=1, source_target_pairs={{0,8},{2,10},{4,12},{6,14},{8,0},{10,2},{12,4},{14,6},{16,24},{18,... | collective-permute-start | bytes 104456 | tf_op jit(solution)/shard_map/ppermute | solution.py:372
  41.9 0.7 %copy_bitcast_fusion = bf16[1,32,4,8,128]{4,3,2,1,0:T(8,128)(2,1)} fusion(bf16[4,32,8,128]{3,2,1,0:T(8,128)(2,1)S(1)} %bitcast.60), kind=kLoop, calls=%fused_computation.1 | loop fusion | bytes 524288 | tf_op jit(solution)/shard_map/broadcast_in_dim | solution.py:415
  42.7 0.6 %collective-permute-done.15.three = bf16[136,128]{1,0:T(8,128)(2,1)S(1)} collective-permute-done((bf16[136,128]{1,0:T(8,128)(2,1)S(1)}, bf16[136,128]{1,0:T(8,128)(2,1)S(1)}, u32[]{:S(2)}, u32[]{:S(2)}) %collective-permute-start.15) | collective-permute-done | bytes 34848 | tf_op jit(solution)/shard_map/ppermute | solution.py:372
  43.3 1.5 %collective-permute-done.14.two = bf16[136,128]{1,0:T(8,128)(2,1)S(1)} collective-permute-done((bf16[136,128]{1,0:T(8,128)(2,1)S(1)}, bf16[136,128]{1,0:T(8,128)(2,1)S(1)}, u32[]{:S(2)}, u32[]{:S(2)}) %collective-permute-start.14) | collective-permute-done | bytes 34848 | tf_op jit(solution)/shard_map/ppermute | solution.py:372
  44.8 0.7 %finish.1 = (f32[54,64]{1,0:T(8,128)}, f32[108,128]{1,0:T(8,128)}) custom-call(bf16[16,136,128]{2,1,0:T(8,128)(2,1)S(1)} %get-tuple-element.13.wire, bf16[5,136,128]{2,1,0:T(8,128)(2,1)S(1)} %collective-permute-done.9.crossed, bf16[136,128]{1,0:T(8,128)(2,1)S(1)} %collective-permute-done.10.beside, bf16[136,128]{1,0:T(8,128)(2,1)S(1)} %collective-permute-done.13.one, ...), custom_call_target="tpu_custom_call" | custom-call | flops 120000 | bytes 300000 | tf_op jit(solution)/shard_map/finish/pallas_call | solution.py:102
  (32 shorter events, 0.4 us)
Async XLA Ops:
  0.6 0.7 %copy-start = (bf16[108,128]{1,0:T(8,128)(2,1)S(1)}, bf16[108,128]{1,0:T(8,128)(2,1)}, u32[]{:S(2)}) copy-start(bf16[108,128]{1,0:T(8,128)(2,1)} %second.1) | copy-start | bytes 82948
  1.4 0.7 %copy-start.1 = (bf16[54,64]{1,0:T(8,128)(2,1)S(1)}, bf16[54,64]{1,0:T(8,128)(2,1)}, u32[]{:S(2)}) copy-start(bf16[54,64]{1,0:T(8,128)(2,1)} %first.1) | copy-start | bytes 20740
  2.2 12.1 %collective-permute-start.5 = (bf16[136,128]{1,0:T(8,128)(2,1)S(1)}, bf16[136,128]{1,0:T(8,128)(2,1)S(1)}, u32[]{:S(2)}, u32[]{:S(2)}) collective-permute-start(bf16[136,128]{1,0:T(8,128)(2,1)S(1)} %pack.1), channel_id=1, source_target_pairs={{0,4},{2,6},{4,0},{6,2},{8,12},{10,14},{12,8},{14,10},{16,20},{18,... | collective-permute-start | bytes 104456 | tf_op jit(solution)/shard_map/ppermute | solution.py:372
  5.3 6.1 %collective-permute-start.4 = (bf16[136,128]{1,0:T(8,128)(2,1)S(1)}, bf16[136,128]{1,0:T(8,128)(2,1)S(1)}, u32[]{:S(2)}, u32[]{:S(2)}) collective-permute-start(bf16[136,128]{1,0:T(8,128)(2,1)S(1)} %pack.1), channel_id=1, source_target_pairs={{0,24},{2,26},{4,28},{6,30},{8,16},{10,18},{12,20},{14,22},{16,8},... | collective-permute-start | bytes 104456 | tf_op jit(solution)/shard_map/ppermute | solution.py:372
  8.9 4.8 %collective-permute-start.3 = (bf16[136,128]{1,0:T(8,128)(2,1)S(1)}, bf16[136,128]{1,0:T(8,128)(2,1)S(1)}, u32[]{:S(2)}, u32[]{:S(2)}) collective-permute-start(bf16[136,128]{1,0:T(8,128)(2,1)S(1)} %pack.1), channel_id=1, source_target_pairs={{0,16},{2,18},{4,20},{6,22},{8,24},{10,26},{12,28},{14,30},{16,0},... | collective-permute-start | bytes 104456 | tf_op jit(solution)/shard_map/ppermute | solution.py:372
  8.9 4.8 %collective-permute-start.2 = (bf16[136,128]{1,0:T(8,128)(2,1)S(1)}, bf16[136,128]{1,0:T(8,128)(2,1)S(1)}, u32[]{:S(2)}, u32[]{:S(2)}) collective-permute-start(bf16[136,128]{1,0:T(8,128)(2,1)S(1)} %pack.1), channel_id=1, source_target_pairs={{0,8},{2,10},{4,12},{6,14},{8,0},{10,2},{12,4},{14,6},{16,24},{18,... | collective-permute-start | bytes 104456 | tf_op jit(solution)/shard_map/ppermute | solution.py:372
  9.7 11.2 %collective-permute-start.1 = (bf16[64,128]{1,0:T(8,128)(2,1)}, bf16[64,128]{1,0:T(8,128)(2,1)S(1)}, u32[]{:S(2)}, u32[]{:S(2)}) collective-permute-start(bf16[64,128]{1,0:T(8,128)(2,1)} %bitcast.58), channel_id=1, source_target_pairs={{0,1},{1,0},{2,3},{3,2},{4,5},{5,4},{6,7},{7,6},{8,9},{9,8},{10,11... | collective-permute-start | bytes 49160 | tf_op jit(solution)/shard_map/ppermute | solution.py:386
  11.4 8.4 %collective-permute-start = (bf16[1,32,4,8,128]{4,3,2,1,0:T(8,128)(2,1)}, bf16[1,32,4,8,128]{4,3,2,1,0:T(8,128)(2,1)S(1)}, u32[]{:S(2)}, u32[]{:S(2)}) collective-permute-start(bf16[1,32,4,8,128]{4,3,2,1,0:T(8,128)(2,1)} %param.4), channel_id=1, source_target_pairs={{0,1},{1,0},{2,3},{3,2},{4,5},{5,4},{6,7},{7,6},{8,9},{9,8},{10,11... | collective-permute-start | bytes 786440 | tf_op jit(solution)/shard_map/ppermute | solution.py:384
  13.8 4.7 %collective-permute-start.6 = (bf16[3,136,128]{2,1,0:T(8,128)(2,1)S(1)}, bf16[3,136,128]{2,1,0:T(8,128)(2,1)S(1)}, u32[]{:S(2)}, u32[]{:S(2)}) collective-permute-start(bf16[3,136,128]{2,1,0:T(8,128)(2,1)S(1)} %pad_maximum_fusion.1), channel_id=1, source_target_pairs={{0,4},{2,6},{4,0},{6,2},{8,12},{10,14},{12,8},{14,10},{16,20},{18,... | collective-permute-start | bytes 313352 | tf_op jit(solution)/shard_map/ppermute | solution.py:372
  14.4 4.1 %collective-permute-start.7 = (bf16[5,136,128]{2,1,0:T(8,128)(2,1)S(1)}, bf16[5,136,128]{2,1,0:T(8,128)(2,1)S(1)}, u32[]{:S(2)}, u32[]{:S(2)}) collective-permute-start(bf16[5,136,128]{2,1,0:T(8,128)(2,1)S(1)} %get-tuple-element.19), channel_id=1, source_target_pairs={{0,2},{2,0},{4,6},{6,4},{8,10},{10,8},{12,14},{14,12},{16,18},{18,... | collective-permute-start | bytes 522248 | tf_op jit(solution)/shard_map/ppermute | solution.py:372
  18.5 1.3 %collective-permute-start.8 = (bf16[3,136,128]{2,1,0:T(8,128)(2,1)S(1)}, bf16[3,136,128]{2,1,0:T(8,128)(2,1)S(1)}, u32[]{:S(2)}, u32[]{:S(2)}) collective-permute-start(bf16[3,136,128]{2,1,0:T(8,128)(2,1)S(1)} %collective-permute-done.6), channel_id=1, source_target_pairs={{0,2},{2,0},{4,6},{6,4},{8,10},{10,8},{12,14},{14,12},{16,18},{18,... | collective-permute-start | bytes 313352 | tf_op jit(solution)/shard_map/ppermute | solution.py:372
  18.5 2.4 %copy-start.2 = (bf16[1,128,1,2,32]{1,4,3,2,0:T(8,128)(2,1)S(1)}, bf16[1,128,1,2,32]{1,4,3,2,0:T(8,128)(2,1)}, u32[]{:S(2)}) copy-start(bf16[1,128,1,2,32]{1,4,3,2,0:T(8,128)(2,1)} %param.7) | copy-start | bytes 49156
  29.5 2.4 %collective-permute-start.11 = (bf16[3,136,128]{2,1,0:T(8,128)(2,1)S(1)}, bf16[3,136,128]{2,1,0:T(8,128)(2,1)S(1)}, u32[]{:S(2)}, u32[]{:S(2)}) collective-permute-start(bf16[3,136,128]{2,1,0:T(8,128)(2,1)S(1)} %slice.36), channel_id=1, source_target_pairs={{0,2},{2,0},{4,6},{6,4},{8,10},{10,8},{12,14},{14,12},{16,18},{18,... | collective-permute-start | bytes 313352 | tf_op jit(solution)/shard_map/ppermute | solution.py:372
  29.7 2.8 %collective-permute-start.9 = (bf16[5,136,128]{2,1,0:T(8,128)(2,1)S(1)}, bf16[5,136,128]{2,1,0:T(8,128)(2,1)S(1)}, u32[]{:S(2)}, u32[]{:S(2)}) collective-permute-start(bf16[5,136,128]{2,1,0:T(8,128)(2,1)S(1)} %slice.30), channel_id=1, source_target_pairs={{0,2},{2,0},{4,6},{6,4},{8,10},{10,8},{12,14},{14,12},{16,18},{18,... | collective-permute-start | bytes 522248 | tf_op jit(solution)/shard_map/ppermute | solution.py:372
  32.0 5.4 %collective-permute-start.12 = (bf16[3,136,128]{2,1,0:T(8,128)(2,1)S(1)}, bf16[3,136,128]{2,1,0:T(8,128)(2,1)S(1)}, u32[]{:S(2)}, u32[]{:S(2)}) collective-permute-start(bf16[3,136,128]{2,1,0:T(8,128)(2,1)S(1)} %add_convert_fusion.1), channel_id=1, source_target_pairs={{0,4},{2,6},{4,0},{6,2},{8,12},{10,14},{12,8},{14,10},{16,20},{18,... | collective-permute-start | bytes 313352 | tf_op jit(solution)/shard_map/ppermute | solution.py:372
  32.6 10.1 %collective-permute-start.10 = (bf16[136,128]{1,0:T(8,128)(2,1)S(1)}, bf16[136,128]{1,0:T(8,128)(2,1)S(1)}, u32[]{:S(2)}, u32[]{:S(2)}) collective-permute-start(bf16[136,128]{1,0:T(8,128)(2,1)S(1)} %fusion), channel_id=1, source_target_pairs={{0,4},{2,6},{4,0},{6,2},{8,12},{10,14},{12,8},{14,10},{16,20},{18,... | collective-permute-start | bytes 104456 | tf_op jit(solution)/shard_map/ppermute | solution.py:372
  37.5 5.8 %collective-permute-start.15 = (bf16[136,128]{1,0:T(8,128)(2,1)S(1)}, bf16[136,128]{1,0:T(8,128)(2,1)S(1)}, u32[]{:S(2)}, u32[]{:S(2)}) collective-permute-start(bf16[136,128]{1,0:T(8,128)(2,1)S(1)} %get-tuple-element.16), channel_id=1, source_target_pairs={{0,24},{2,26},{4,28},{6,30},{8,16},{10,18},{12,20},{14,22},{16,8},... | collective-permute-start | bytes 104456 | tf_op jit(solution)/shard_map/ppermute | solution.py:372
  40.0 4.8 %collective-permute-start.14 = (bf16[136,128]{1,0:T(8,128)(2,1)S(1)}, bf16[136,128]{1,0:T(8,128)(2,1)S(1)}, u32[]{:S(2)}, u32[]{:S(2)}) collective-permute-start(bf16[136,128]{1,0:T(8,128)(2,1)S(1)} %get-tuple-element.17), channel_id=1, source_target_pairs={{0,16},{2,18},{4,20},{6,22},{8,24},{10,26},{12,28},{14,30},{16,0},... | collective-permute-start | bytes 104456 | tf_op jit(solution)/shard_map/ppermute | solution.py:372
  40.0 4.8 %collective-permute-start.13 = (bf16[136,128]{1,0:T(8,128)(2,1)S(1)}, bf16[136,128]{1,0:T(8,128)(2,1)S(1)}, u32[]{:S(2)}, u32[]{:S(2)}) collective-permute-start(bf16[136,128]{1,0:T(8,128)(2,1)S(1)} %get-tuple-element.18), channel_id=1, source_target_pairs={{0,8},{2,10},{4,12},{6,14},{8,0},{10,2},{12,4},{14,6},{16,24},{18,... | collective-permute-start | bytes 104456 | tf_op jit(solution)/shard_map/ppermute | solution.py:372
